TPU v7x, 128 devices: a whole 4x4x4 slice. The times are simulated.
128 devices in a mesh: gx: 8 (over y, core), gy: 16 (over x, z).
Axes of the slice: x: 4, y: 4, z: 4, core: 2. Of those that a mesh axis runs over, the one named last changes fastest.
Arguments:
- estimate: bfloat16 [64, 128, 32, 128], P('gx', 'gy'), may hold values from -16 to 16
- dual: bfloat16 [64, 128, 32, 128], P('gx', 'gy'), may hold values from -4 to 4
- corners: int32 [3, 8192], P(None, ('gx', 'gy')), may hold values from 0 to 120, as said below
- members: int32 [2048, 16], replicated, may hold values from -1 to 8191, as said below
- thresholds: float32 [2048], replicated, may hold values from 3000 to 60000
Outputs:
- lowrank: float32 [64, 128, 32, 128], P('gx', 'gy')
- dual_next: float32 [64, 128, 32, 128], P('gx', 'gy')
Inputs may be any that keep to these rules, and one draw needn't show every extreme that they name: `corners`: patch p covers 8 cells from its corner along each dimension and lies inside the volume. Column p belongs to the device at position p // 64 in the mesh's order (gx slowest); such a patch starts at least 4 cells before that device's block and at most 4 cells before the block's end, along each of the first two dimensions. Every patch number appears in exactly one place of members. The root of group g is the device at position g // 16 in the mesh's order (gx slowest); at most 2 of one device's patches lie in groups of one root, and exactly 2 do for some device and root in every draw; some group lists 16 patches in every draw.
All inputs are finite; a program needn't handle non-finite values.
Results may differ from a plain program's by a relative error of at most 0.0093.
Values may be sent and summed in bfloat16 or wider, within the bound.
No kernel may reach another device: no remote copies, remote signals or barrier semaphores. Data moves between devices by JAX's collectives and lax.ppermute only.
A program may use at most 128 MiB of HBM per device.

v0:
```python
import jax
import jax.numpy as jnp
from jax import lax
from jax.sharding import PartitionSpec as P

PATCH = 8
MEMBERS = 16


data_weight = 2.0


def extended(value, sides, width):
    for axis, dim in sides:
        devices, length = (lax.axis_size(axis), value.shape[dim])
        up = [(i, (i + 1) % devices) for i in range(devices - 1)]
        down = [(j, i) for i, j in up]
        last = lax.slice_in_dim(value, length - width, length, axis=dim)
        leading = lax.slice_in_dim(value, 0, width, axis=dim)
        before = lax.ppermute(last, axis, up)
        after = lax.ppermute(leading, axis, down)
        value = jnp.concatenate([before, value, after], axis=dim)
    return value


def shrink(group_grams, tau):
    dimension = group_grams.shape[-1]
    identity = jnp.eye(dimension, dtype=group_grams.dtype)
    system = group_grams + tau[:, None, None] * identity
    cholesky_factor = jnp.linalg.cholesky(system)
    inverse_factor = lax.linalg.triangular_solve(
        cholesky_factor, jnp.broadcast_to(identity, system.shape), left_side=True, lower=True
    )
    inverse = jnp.einsum(
        "gkc,gkd->gcd", inverse_factor, inverse_factor, precision=lax.Precision.HIGHEST
    )
    return (identity - tau[:, None, None] * inverse).astype(jnp.bfloat16)


def shards(estimate, dual, corners, members, thresholds):
    cells_x, cells_y, cells_z, channels = estimate.shape
    margin = PATCH // 2
    along_x = lax.axis_size("gx")
    along_y = lax.axis_size("gy")
    device_list = along_x * along_y
    index_x = lax.axis_index("gx")
    index_y = lax.axis_index("gy")
    myself = index_x * along_y + index_y
    patches = corners.shape[1]
    groups = members.shape[0]
    per_root = groups // device_list
    lane_count = per_root * MEMBERS // device_list
    slot_count = device_list * lane_count
    mixture = (estimate.astype(jnp.float32) + dual.astype(jnp.float32)).astype(jnp.bfloat16)
    padded = extended(mixture, (("gx", 0), ("gy", 1)), margin)
    wide_x = cells_x + 2 * margin
    wide_y = cells_y + 2 * margin
    cell_rows = padded.reshape(wide_x * wide_y * cells_z, channels)
    begin_column = corners[0] - (index_x * cells_x - margin)
    start_y = corners[1] - (index_y * cells_y - margin)
    first_cell = (begin_column * wide_y + start_y) * cells_z + corners[2]
    within = jnp.arange(PATCH**3, dtype=jnp.int32)
    shift_amount = (
        within // (PATCH * PATCH) * wide_y + within // PATCH % PATCH
    ) * cells_z + within % PATCH
    row_index = first_cell[:, None] + shift_amount[None, :]
    block_size = 64
    row_blocks = row_index.reshape(patches // block_size, block_size, PATCH**3)

    def block_gram(picked):
        values = cell_rows[picked]
        return jnp.einsum("kvc,kvd->kcd", values, values, preferred_element_type=jnp.float32)

    patch_grams = lax.map(block_gram, row_blocks).reshape(patches, channels, channels)
    patch_total = patches * device_list
    listed = jnp.where(members >= 0, members, patch_total)
    numbers = jnp.broadcast_to(jnp.arange(groups, dtype=jnp.int32)[:, None], members.shape)
    group_of = jnp.zeros((patch_total,), jnp.int32).at[listed].set(numbers, mode="drop")
    home_group = lax.dynamic_slice_in_dim(group_of, myself * patches, patches)
    target = home_group // per_root
    position = jnp.arange(patches, dtype=jnp.int32)
    earlier = (target[:, None] == target[None, :]) & (position[None, :] < position[:, None])
    lane_index = jnp.sum(earlier.astype(jnp.int32), axis=1)
    slot_index = target * lane_count + lane_index
    outgoing = patch_grams.reshape(patches, channels * channels)
    row_width = outgoing.shape[1]
    outbox = jnp.zeros((slot_count, row_width), jnp.float32).at[slot_index].set(outgoing)
    labels_out = jnp.full((slot_count,), -1, jnp.int32).at[slot_index].set(home_group)
    arrived, labels = (
        lax.all_to_all(
            outbox.reshape(device_list, lane_count, row_width),
            ("gx", "gy"),
            split_axis=0,
            concat_axis=0,
            tiled=True,
        ),
        lax.all_to_all(
            labels_out.reshape(device_list, lane_count),
            ("gx", "gy"),
            split_axis=0,
            concat_axis=0,
            tiled=True,
        ),
    )
    arrived = arrived.reshape(slot_count, row_width)
    labels = labels.reshape(slot_count)
    owned_groups = myself * per_root + jnp.arange(per_root, dtype=jnp.int32)
    matches = labels[:, None] == owned_groups[None, :]
    summed = jnp.dot(matches.astype(jnp.float32).T, arrived, precision=lax.Precision.HIGHEST)
    group_grams = summed.reshape(per_root, channels, channels)
    factors = shrink(group_grams, thresholds[owned_groups])
    factor_rows = factors.reshape(per_root, channels * channels)
    local_index = jnp.sum(
        jnp.where(matches, jnp.arange(per_root, dtype=jnp.int32)[None, :], 0), axis=1
    )
    replies = jnp.where(
        jnp.any(matches, axis=1)[:, None], factor_rows[local_index], jnp.zeros((), jnp.bfloat16)
    )
    reply_width = replies.shape[1]
    returned = lax.all_to_all(
        replies.reshape(device_list, lane_count, reply_width),
        ("gx", "gy"),
        split_axis=0,
        concat_axis=0,
        tiled=True,
    )
    returned = returned.reshape(slot_count, reply_width)[slot_index]
    factors_mine = returned.reshape(patches, channels, channels)
    factor_blocks = factors_mine.reshape(patches // block_size, block_size, channels, channels)

    def add_block(aggregate, block_item):
        picked, factor = block_item
        values = cell_rows[picked]
        result = jnp.einsum("kvc,kcd->kvd", values, factor, preferred_element_type=jnp.float32)
        return (aggregate.at[picked.reshape(-1)].add(result.reshape(-1, channels)), None)

    aggregate, _ = lax.scan(
        add_block,
        jnp.zeros((wide_x * wide_y * cells_z, channels), jnp.float32),
        (row_blocks, factor_blocks),
    )
    covers = jnp.zeros((wide_x * wide_y * cells_z,), jnp.float32).at[row_index.reshape(-1)].add(1.0)
    aggregate = aggregate.reshape(wide_x, wide_y, cells_z, channels)
    covers = covers.reshape(wide_x, wide_y, cells_z)
    edges_x = (
        jnp.concatenate([aggregate[:margin], aggregate[wide_x - margin :]], 0),
        jnp.concatenate([covers[:margin], covers[wide_x - margin :]], 0),
    )
    nearby_x = (
        extended(edges_x[0], (("gx", 0),), margin),
        extended(edges_x[1], (("gx", 0),), margin),
    )
    inner_sums = aggregate[margin : margin + cells_x]
    inner_counts = covers[margin : margin + cells_x]
    inner_sums = (
        inner_sums.at[:margin]
        .add(nearby_x[0][:margin])
        .at[cells_x - margin :]
        .add(nearby_x[0][3 * margin :])
    )
    inner_counts = (
        inner_counts.at[:margin]
        .add(nearby_x[1][:margin])
        .at[cells_x - margin :]
        .add(nearby_x[1][3 * margin :])
    )
    edges_y = (
        jnp.concatenate([inner_sums[:, :margin], inner_sums[:, wide_y - margin :]], 1),
        jnp.concatenate([inner_counts[:, :margin], inner_counts[:, wide_y - margin :]], 1),
    )
    nearby_y = (
        extended(edges_y[0], (("gy", 1),), margin),
        extended(edges_y[1], (("gy", 1),), margin),
    )
    final_sums = inner_sums[:, margin : margin + cells_y]
    final_counts = inner_counts[:, margin : margin + cells_y]
    final_sums = (
        final_sums.at[:, :margin]
        .add(nearby_y[0][:, :margin])
        .at[:, cells_y - margin :]
        .add(nearby_y[0][:, 3 * margin :])
    )
    final_counts = (
        final_counts.at[:, :margin]
        .add(nearby_y[1][:, :margin])
        .at[:, cells_y - margin :]
        .add(nearby_y[1][:, 3 * margin :])
    )
    lowrank = (final_sums + data_weight * mixture.astype(jnp.float32)) / (
        final_counts + data_weight
    )[..., None]
    dual_next = dual.astype(jnp.float32) + estimate.astype(jnp.float32) - lowrank
    return (lowrank, dual_next)


def solution(mesh):
    in_specs = (
        P("gx", "gy", None, None),
        P("gx", "gy", None, None),
        P(None, ("gx", "gy")),
        P(),
        P(),
    )
    out_specs = (P("gx", "gy", None, None), P("gx", "gy", None, None))
    return jax.shard_map(shards, mesh=mesh, in_specs=in_specs, out_specs=out_specs, check_vma=False)
```

profile of v0, /device:TPU:104, one launch (start us, length us, event | category | flops | bytes accessed | tf_op | source)
XLA Modules:
  0.0 1605.5 jit_solution(15965166899518975295)
XLA Ops:
  9.6 120.1 %scatter_custom_fusion = s32[8192]{0:T(1024)S(1)} fusion(s32[32768]{0:T(1024)S(1)} %reshape.595, s32[32768]{0:T(1024)S(1)} %reshape.597, s32[]{:T(128)} %constant.367.clone.1), kind=kCustom, calls=%fused_computation.71 | custom fusion | bytes 32772 | tf_op jit(solution)/shard_map/scatter | solution.py:78
  131.5 9.8 all-to-all-start
  148.6 9.8 collective-permute-done.2
  163.2 114.1 %gather_fusion = bf16[32768,128]{1,0:T(8,128)(2,1)} fusion(bf16[8192,128]{1,0:T(8,128)(2,1)S(1)} %bitcast.58, s32[32768]{0:T(1024)S(1)} %broadcast_clamp_fusion), kind=kCustom, calls=%fused_computation | custom fusion | bytes 16908288 | tf_op jit(solution)/shard_map/while/body/eval_jaxpr/gather | solution.py:133
  277.3 10.1 fusion.55
  287.4 13.6 scatter_custom_fusion.2
  301.1 20.0 %reshape.553 = f32[128,2,16384]{2,1,0:T(2,128)} reshape(f32[256,16384]{1,0:T(8,128)} %scatter_custom_fusion.2) | data formatting | bytes 33554432 | tf_op jit(solution)/shard_map/reshape | solution.py:91
  321.1 10.2 all-to-all-start.1
  334.0 228.4 %all-to-all-done.1 = f32[128,2,16384]{2,1,0:T(2,128)} async-done(((f32[128,2,16384]{2,1,0:T(2,128)}), f32[128,2,16384]{2,1,0:T(2,128)}, u32[]{:S(2)}, u32[]{:S(2)}) %all-to-all-start.1) | async-done | bytes 16777248 | tf_op jit(solution)/shard_map/all_to_all | solution.py:90
  562.4 20.5 %reshape.554 = f32[256,16384]{1,0:T(8,128)} reshape(f32[128,2,16384]{2,1,0:T(2,128)} %all-to-all-done.1) | data formatting | bytes 33554432 | tf_op jit(solution)/shard_map/reshape | solution.py:105
  582.9 17.4 %copy.28 = f32[16384,256]{1,0:T(8,128)} copy(f32[16384,256]{0,1:T(8,128)} %bitcast.62) | data formatting | bytes 33554432 | tf_op jit(solution)/shard_map/dot_general | solution.py:109
  600.4 10.5 fusion.30
  612.7 188.3 %custom-call.7 = f32[16,128,128]{2,1,0:T(8,128)S(1)} custom-call(f32[16,128,128]{2,1,0:T(8,128)} %fusion.12), custom_call_target="Cholesky" | custom-call | tf_op jit(solution)/shard_map/jit(cholesky)/cholesky | solution.py:30
  801.4 157.6 %custom-call.8 = f32[16,1,128,128]{2,3,1,0:T(8,128)S(1)} custom-call(f32[16,1,128,128]{3,2,1,0:T(8,128)S(1)} %select_bitcast_fusion), custom_call_target="InvertDiagBlocksLowerTriangular" | custom-call | tf_op jit(solution)/shard_map/triangular_solve | solution.py:31
  963.1 9.0 gather_fusion.2
  972.2 14.1 gather.20
  986.3 10.3 broadcast_select_fusion
  996.6 19.9 %all-to-all-start.2 = ((bf16[128,2,16384]{2,1,0:T(2,128)(2,1)}), bf16[128,2,16384]{2,1,0:T(2,128)(2,1)}, u32[]{:S(2)}, u32[]{:S(2)}) async-start(bf16[128,2,16384]{2,1,0:T(2,128)(2,1)} %broadcast_select_fusion), calls=%async_computation.2 | async-start | bytes 16777216 | tf_op jit(solution)/shard_map/all_to_all | solution.py:120
  1016.9 97.2 %all-to-all-done.2 = bf16[128,2,16384]{2,1,0:T(2,128)(2,1)} async-done(((bf16[128,2,16384]{2,1,0:T(2,128)(2,1)}), bf16[128,2,16384]{2,1,0:T(2,128)(2,1)}, u32[]{:S(2)}, u32[]{:S(2)}) %all-to-all-start.2) | async-done | bytes 8388640 | tf_op jit(solution)/shard_map/all_to_all | solution.py:120
  1114.1 13.1 reshape.556
  1127.2 8.1 gather_fusion.3
  1135.9 11.5 fusion.56
  1147.4 176.4 %scatter_custom_fusion.3 = f32[8192,128]{1,0:T(8,128)} fusion(s32[32768]{0:T(1024)S(1)} %bitcast.73, f32[32768,128]{1,0:T(8,128)} %bitcast.65, f32[]{:T(128)} %constant.357.clone.1), kind=kCustom, calls=%fused_computation.15 | custom fusion | flops 4194304 | bytes 4194816 | tf_op jit(solution)/shard_map/while/body/eval_jaxpr/scatter-add | solution.py:135
  1329.5 225.5 %scatter_custom_fusion.4 = f32[8192]{0:T(1024)S(1)} fusion(s32[32768]{0:T(1024)S(1)} %bitcast.74, f32[32768]{0:T(1024)S(1)} %broadcast.493, f32[]{:T(128)} %constant.357.clone.1), kind=kCustom, calls=%fused_computation.69 | custom fusion | flops 32768 | bytes 32772 | tf_op jit(solution)/shard_map/scatter-add | solution.py:142
  (104 shorter events, 88.2 us)
Async XLA Ops:
  0.6 330.8 %copy-start = (f32[2048]{0:T(1024)S(1)}, f32[2048]{0:T(1024)}, u32[]{:S(2)}) copy-start(f32[2048]{0:T(1024)} %param.25) | copy-start | bytes 24580
  2.0 140.2 %collective-permute-start = (bf16[4,8,32,128]{3,2,1,0:T(8,128)(2,1)S(1)}, bf16[4,8,32,128]{3,2,1,0:T(8,128)(2,1)S(1)}, u32[]{:S(2)}, u32[]{:S(2)}) collective-permute-start(bf16[4,8,32,128]{3,2,1,0:T(8,128)(2,1)S(1)} %get-tuple-element.136), channel_id=1, source_target_pairs={{0,16},{16,32},{32,48},{48,64},{64,80},{80,96},{96,112},{1,17},{17... | collective-permute-start | bytes 786440 | tf_op jit(solution)/shard_map/ppermute | solution.py:20
  4.0 138.3 %collective-permute-start.1 = (bf16[4,8,32,128]{3,2,1,0:T(8,128)(2,1)S(1)}, bf16[4,8,32,128]{3,2,1,0:T(8,128)(2,1)S(1)}, u32[]{:S(2)}, u32[]{:S(2)}) collective-permute-start(bf16[4,8,32,128]{3,2,1,0:T(8,128)(2,1)S(1)} %get-tuple-element.137), channel_id=1, source_target_pairs={{16,0},{32,16},{48,32},{64,48},{80,64},{96,80},{112,96},{17,1},{33... | collective-permute-start | bytes 786440 | tf_op jit(solution)/shard_map/ppermute | solution.py:21
  131.5 189.6 %all-to-all-start = ((s32[128,1,2]{2,1,0:T(1,128)}), s32[128,1,2]{2,1,0:T(1,128)S(1)}, u32[]{:S(2)}, u32[]{:S(2)}) async-start(s32[128,1,2]{2,1,0:T(1,128)} %bitcast.4), calls=%async_computation | async-start | bytes 131072 | tf_op jit(solution)/shard_map/all_to_all | solution.py:97
  142.5 15.9 collective-permute-start.2
  145.2 17.7 %collective-permute-start.3 = (bf16[16,4,32,128]{3,2,1,0:T(8,128)(2,1)S(1)}, bf16[16,4,32,128]{3,2,1,0:T(8,128)(2,1)S(1)}, u32[]{:S(2)}, u32[]{:S(2)}) collective-permute-start(bf16[16,4,32,128]{3,2,1,0:T(8,128)(2,1)S(1)} %get-tuple-element.135), channel_id=1, source_target_pairs={{1,0},{2,1},{3,2},{4,3},{5,4},{6,5},{7,6},{8,7},{9,8},{10,9},{11,1... | collective-permute-start | bytes 1572872 | tf_op jit(solution)/shard_map/ppermute | solution.py:21
  321.1 241.2 %all-to-all-start.1 = ((f32[128,2,16384]{2,1,0:T(2,128)}), f32[128,2,16384]{2,1,0:T(2,128)}, u32[]{:S(2)}, u32[]{:S(2)}) async-start(f32[128,2,16384]{2,1,0:T(2,128)} %reshape.553), calls=%async_computation.1 | async-start | bytes 33554432 | tf_op jit(solution)/shard_map/all_to_all | solution.py:90
  996.6 117.5 %all-to-all-start.2 = ((bf16[128,2,16384]{2,1,0:T(2,128)(2,1)}), bf16[128,2,16384]{2,1,0:T(2,128)(2,1)}, u32[]{:S(2)}, u32[]{:S(2)}) async-start(bf16[128,2,16384]{2,1,0:T(2,128)(2,1)} %broadcast_select_fusion), calls=%async_computation.2 | async-start | bytes 16777216 | tf_op jit(solution)/shard_map/all_to_all | solution.py:120
  1323.8 254.5 %slice-start = ((f32[8192,128]{1,0:T(8,128)}), f32[4096,128]{1,0:T(8,128)S(1)}, s32[]{:S(2)}) async-start(f32[8192,128]{1,0:T(8,128)} %scatter_custom_fusion.3), calls=%async_computation.3 | async-start | bytes 4194304 | tf_op jit(solution)/shard_map/slice | solution.py:153
  1327.5 250.8 %collective-permute-start.4 = (f32[4,16,32,128]{3,2,1,0:T(8,128)}, f32[4,16,32,128]{3,2,1,0:T(8,128)}, u32[]{:S(2)}, u32[]{:S(2)}) collective-permute-start(f32[4,16,32,128]{3,2,1,0:T(8,128)} %bitcast.17), channel_id=1, source_target_pairs={{0,16},{16,32},{32,48},{48,64},{64,80},{80,96},{96,112},{1,17},{17... | collective-permute-start | bytes 3145736 | tf_op jit(solution)/shard_map/ppermute | solution.py:20
  1555.0 25.1 %collective-permute-start.5 = (f32[4,16,32,128]{3,2,1,0:T(8,128)}, f32[4,16,32,128]{3,2,1,0:T(8,128)}, u32[]{:S(2)}, u32[]{:S(2)}) collective-permute-start(f32[4,16,32,128]{3,2,1,0:T(8,128)} %bitcast.70), channel_id=1, source_target_pairs={{16,0},{32,16},{48,32},{64,48},{80,64},{96,80},{112,96},{17,1},{33... | collective-permute-start | bytes 3145736 | tf_op jit(solution)/shard_map/ppermute | solution.py:21
  1559.5 5.8 collective-permute-start.8
  1561.5 10.8 collective-permute-start.9
  1572.3 15.4 collective-permute-start.10
  1576.1 27.4 %copy-start.2 = (bf16[8,8,32,128]{3,2,1,0:T(8,128)(2,1)S(1)}, bf16[8,8,32,128]{3,2,1,0:T(8,128)(2,1)}, u32[]{:S(2)}) copy-start(bf16[8,8,32,128]{3,2,1,0:T(8,128)(2,1)} %param.22) | copy-start | bytes 1572868
  1576.1 27.4 %copy-start.3 = (bf16[8,8,32,128]{3,2,1,0:T(8,128)(2,1)S(1)}, bf16[8,8,32,128]{3,2,1,0:T(8,128)(2,1)}, u32[]{:S(2)}) copy-start(bf16[8,8,32,128]{3,2,1,0:T(8,128)(2,1)} %param.21) | copy-start | bytes 1572868
  1576.1 13.5 collective-permute-start.11
  1578.3 27.0 %copy-start.1 = (f32[2048]{0:T(1024)S(1)}, f32[2048]{0:T(1024)}, u32[]{:S(2)}) copy-start(f32[2048]{0:T(1024)} %param.25) | copy-start | bytes 24580
  1581.7 15.7 collective-permute-start.6
  1587.7 15.6 collective-permute-start.7
where the time goes:
time: 1610 us
  other arithmetic  770 us (48%)
  local copies, waits for them, and re-layouts  360 us (22%)
  waiting for transfers between devices  360 us (22%)
  starting transfers between devices  77.1 us (5%)
  matrix products  35.9 us (2%)
    all_to_all x1, waiting for transfers between devices, shards(): lax.all_to_all(outbox.reshape(device_list, lane_count, row_width), ('gx',...  228 us
    scatter-add x1, other arithmetic, shards(): jnp.zeros((wide_x * wide_y * cells_z,), jnp.float32)  226 us
    another operation x3, other arithmetic, shrink(): cholesky_factor = jnp.linalg.cholesky(system)  188 us
    scatter-add x1, other arithmetic, add_block(): aggregate.at[picked.reshape(-1)].add(result.reshape(-1, channels))  176 us
    another operation x3, other arithmetic, shrink(): lax.linalg.triangular_solve(cholesky_factor, jnp.broadcast_to(identity, s...  158 us
    scatter x1, local copies, waits for them, and re-layouts, shards(): jnp.zeros((patch_total,), jnp.int32).at[listed].set(numbers, mode='drop')  120 us
    gather x1, local copies, waits for them, and re-layouts, add_block(): values = cell_rows[picked]  114 us
    all_to_all x1, waiting for transfers between devices, shards(): lax.all_to_all(replies.reshape(device_list, lane_count, reply_width), ('g...  97.2 us
  transfers between devices with their start and end apart: 15, of which 7 were waited for; matrix products, arithmetic and copies ran while one was open for 32% of the time, Pallas kernels for 0%

commit v1 on v0

v1 whole, which is shorter than its diff:
```python
import functools

import jax
import jax.numpy as jnp
from jax import lax
from jax.experimental import pallas as pl
from jax.experimental.pallas import tpu as pltpu
from jax.sharding import PartitionSpec as P

PATCH = 8
DATA_WEIGHT = 2.0
F32 = jnp.float32
BF16 = jnp.bfloat16
BOTH = ("gx", "gy")
NB = 16

VMEM = pl.BlockSpec(memory_space=pltpu.VMEM)
SMEM = pl.BlockSpec(memory_space=pltpu.SMEM)
PARAMS = pltpu.CompilerParams(vmem_limit_bytes=48 * 1024 * 1024)


def call(body, out_shape, *args, specs=None, scratch=(), flops=0, nbytes=0):
    outs = jax.tree.map(lambda _: VMEM, out_shape)
    return pl.pallas_call(
        body,
        out_shape=out_shape,
        in_specs=specs or [VMEM] * len(args),
        out_specs=outs,
        scratch_shapes=list(scratch),
        compiler_params=PARAMS,
        cost_estimate=pl.CostEstimate(flops=flops, bytes_accessed=nbytes, transcendentals=0),
    )(*args)


def neighbors(value, axis, first, last):
    size = lax.axis_size(axis)
    up = [(i, i + 1) for i in range(size - 1)]
    down = [(j, i) for i, j in up]
    before = lax.ppermute(last, axis, up)
    after = lax.ppermute(first, axis, down)
    return before, after


def group_table_body(members_ref, out_ref):
    rows = members_ref.shape[0]
    per = 8
    high = lax.broadcasted_iota(jnp.int32, (64, 128), 0)
    low = lax.broadcasted_iota(jnp.int32, (128, 128), 0)
    lane = lax.broadcasted_iota(jnp.int32, (1, 128), 1)

    def step(i, acc):
        block = members_ref[pl.ds(pl.multiple_of(i * per, per), per), :]
        coarse, fine, lows = [], [], []
        for j in range(per):
            entry = block[j : j + 1, :]
            on = high == (entry >> 7)
            group = (i * per + j) * 8 + (lane >> 4)
            zero = jnp.zeros((64, 128), F32)
            coarse.append(
                jnp.where(on, jnp.broadcast_to((group >> 4).astype(F32), (64, 128)), zero)
            )
            fine.append(
                jnp.where(on, jnp.broadcast_to((group & 15).astype(F32), (64, 128)), zero)
            )
            lows.append(jnp.where(low == (entry & 127), 1.0, 0.0))
        left = jnp.concatenate(
            [jnp.concatenate(coarse, 1), jnp.concatenate(fine, 1)], 0
        ).astype(BF16)
        right = jnp.concatenate(lows, 1).astype(BF16)
        return acc + lax.dot_general(
            left, right, (((1,), (1,)), ((), ())), preferred_element_type=F32
        )

    acc = lax.fori_loop(0, rows // per, step, jnp.zeros((128, 128), F32))
    out_ref[...] = (acc[:64] * 16.0 + acc[64:]).astype(jnp.int32)


def counts_body(corner_ref, base_ref, out_ref):
    lanes = corner_ref.shape[1]
    px = corner_ref[0:1, :] - base_ref[0]
    py = corner_ref[1:2, :] - base_ref[1]
    pz = corner_ref[2:3, :]
    z = lax.broadcasted_iota(jnp.int32, (32, lanes), 0)
    in_z = jnp.where((z >= pz) & (z < pz + PATCH), 1.0, 0.0)
    ones = jnp.ones((lanes, 128), BF16)

    def column(x, _):
        in_x = (px <= x) & (px > x - PATCH)
        parts = []
        for y in range(8):
            hit = jnp.where(in_x & (py <= y) & (py > y - PATCH), 1.0, 0.0)
            parts.append((hit * in_z).astype(BF16))
        cover = jnp.dot(jnp.concatenate(parts, 0), ones, preferred_element_type=F32)
        out_ref[pl.ds(pl.multiple_of(x * 256, 256), 256), :] = 1.0 / (cover + DATA_WEIGHT)
        return 0

    lax.fori_loop(0, 8, column, 0)


def load_patch(cells_ref, first):
    rows = []
    for a in range(PATCH):
        for b in range(PATCH):
            rows.append(cells_ref[pl.ds(first + (a * 16 + b) * 32, PATCH), :])
    return jnp.concatenate(rows, 0)


def gram_body(first_ref, own_ref, yb_ref, ya_ref, xb_ref, xa_ref, cells_ref, out_ref):
    cells_ref[pl.ds(0, 2048), :] = xb_ref[...].reshape(2048, 128).astype(F32)
    cells_ref[pl.ds(6144, 2048), :] = xa_ref[...].reshape(2048, 128).astype(F32)

    def fill(x, _):
        row = pl.multiple_of((x + 4) * 512, 512)
        cells_ref[pl.ds(row, 128), :] = yb_ref[x].reshape(128, 128).astype(F32)
        cells_ref[pl.ds(row + 128, 256), :] = own_ref[x].reshape(256, 128).astype(F32)
        cells_ref[pl.ds(row + 384, 128), :] = ya_ref[x].reshape(128, 128).astype(F32)
        return 0

    lax.fori_loop(0, 8, fill, 0)

    def patch(p, _):
        values = load_patch(cells_ref, first_ref[p]).astype(BF16)
        gram = lax.dot_general(values, values, (((0,), (0,)), ((), ())), preferred_element_type=F32)
        out_ref[pl.ds(p, 128, stride=64), :] = gram
        return 0

    lax.fori_loop(0, 64, patch, 0, unroll=2)


def group_sum_body(group_ref, rows_ref, out_ref, limbs_ref, hot_ref):
    def split(i, _):
        row = pl.multiple_of(i * 128, 128)
        value = rows_ref[pl.ds(row, 128), :]
        high = value.astype(BF16)
        limbs_ref[pl.ds(row, 128), 0:128] = high
        limbs_ref[pl.ds(row, 128), 128:256] = (value - high.astype(F32)).astype(BF16)
        return 0

    lax.fori_loop(0, 64, split, 0)
    sub = lax.broadcasted_iota(jnp.int32, (256, 128), 0)

    def chunk(i, _):
        base = i * 256
        for t in range(64):
            entry = group_ref[t : t + 1, :] - base
            hot_ref[:, t * 128 : (t + 1) * 128] = jnp.where(sub == entry, 1.0, 0.0).astype(BF16)
        total = jnp.dot(hot_ref[...], limbs_ref[...], preferred_element_type=F32)
        out_ref[pl.ds(pl.multiple_of(base, 256), 256), :] = total[:, :128] + total[:, 128:]
        return 0

    lax.fori_loop(0, 8, chunk, 0)


def shrink_body(tau_ref, rows_ref, out_ref, sys_ref, stage_ref):
    per = 16
    row_id = lax.broadcasted_iota(jnp.int32, (128, 128), 0)
    lane_id = lax.broadcasted_iota(jnp.int32, (128, 128), 1)
    diagonal = row_id == lane_id
    for g in range(per):
        matrix = rows_ref[pl.ds(g, 128, stride=per), :]
        sys_ref[g] = matrix + jnp.where(diagonal, tau_ref[g], 0.0)
    panel_sub = lax.broadcasted_iota(jnp.int32, (per, NB, 128), 1)
    panel_lane = lax.broadcasted_iota(jnp.int32, (per, NB, 128), 2)

    def block(b, _):
        start = pl.multiple_of(b * NB, NB)
        panel = sys_ref[:, pl.ds(start, NB), :]
        panel = pltpu.roll(panel.reshape(per * NB, 128), 128 - start, axis=1).reshape(per, NB, 128)
        for j in range(NB):
            column = panel[:, :, j : j + 1]
            pivot_row = panel[:, j : j + 1, :]
            pivot = 1.0 / panel[:, j : j + 1, j : j + 1]
            scaled = jnp.where(panel_lane[:, j : j + 1, :] == j, pivot, pivot_row * pivot)
            cleared = jnp.where(panel_lane == j, 0.0, panel)
            panel = jnp.where(panel_sub == j, scaled, cleared - column * scaled)
        panel = pltpu.roll(panel.reshape(per * NB, 128), start, axis=1).reshape(per, NB, 128)
        in_block = (lane_id >= start) & (lane_id < start + NB)
        for g in range(per):
            stage_ref[...] = jnp.zeros((128, 128), F32)
            stage_ref[pl.ds(start, NB), :] = panel[g]
            matrix = sys_ref[g]
            update = jnp.dot(
                matrix, stage_ref[...], precision=lax.Precision.HIGHEST, preferred_element_type=F32
            )
            sys_ref[g] = jnp.where(in_block, 0.0, matrix) - update
            sys_ref[g, pl.ds(start, NB), :] = panel[g]
        return 0

    lax.fori_loop(0, 128 // NB, block, 0)
    for g in range(per):
        factor = jnp.where(diagonal, 1.0, 0.0) - tau_ref[g] * sys_ref[g]
        out_ref[pl.ds(g, 128, stride=per), :] = factor


def expand_body(group_ref, rows_ref, out_ref, turned_ref):
    turned_ref[...] = group_ref[...].astype(F32).T.astype(jnp.int32)
    lane = lax.broadcasted_iota(jnp.int32, (128, 2048), 1)
    table = rows_ref[...]
    for t in range(64):
        hot = jnp.where(lane == turned_ref[:, t : t + 1], 1.0, 0.0).astype(BF16)
        out_ref[t * 128 : (t + 1) * 128, :] = jnp.dot(
            hot, table, preferred_element_type=F32
        ).astype(BF16)


def apply_body(first_ref, cells_ref, rows_ref, out_ref, wide_ref):
    wide_ref[...] = rows_ref[...].astype(F32)
    out_ref[...] = jnp.zeros_like(out_ref)

    def patch(p, _):
        first = first_ref[p]
        values = load_patch(cells_ref, first).astype(BF16)
        factor = wide_ref[pl.ds(p, 128, stride=64), :].astype(BF16)
        result = jnp.dot(values, factor, preferred_element_type=F32)
        for a in range(PATCH):
            for b in range(PATCH):
                at = pl.ds(first + (a * 16 + b) * 32, PATCH)
                i = (a * PATCH + b) * PATCH
                out_ref[at, :] += result[i : i + PATCH]
        return 0

    lax.fori_loop(0, 64, patch, 0)


def exchange(rows, chunk):
    shape = rows.shape
    rows = rows.reshape(128, chunk, 128)
    rows = lax.all_to_all(rows, BOTH, split_axis=0, concat_axis=0, tiled=True)
    return rows.reshape(shape)


def shards(estimate, dual, corners, members, thresholds):
    margin = PATCH // 2
    index_x = lax.axis_index("gx")
    index_y = lax.axis_index("gy")
    myself = index_x * 16 + index_y
    mixture = (estimate.astype(F32) + dual.astype(F32)).astype(BF16)

    yb, ya = neighbors(mixture, "gy", mixture[:, :margin], mixture[:, 8 - margin :])
    marked = corners + 1
    cb, ca = neighbors(marked, "gy", marked, marked)
    wide = jnp.concatenate([yb, mixture, ya], 1)
    xb, xa = neighbors(wide, "gx", wide[:margin], wide[8 - margin :])
    near = jnp.concatenate([cb, marked, ca], 1)
    nb, na = neighbors(near, "gx", near, near)
    near = jnp.concatenate([nb, near, na, jnp.zeros((3, 64), jnp.int32)], 1)
    near = jnp.where(near == 0, -1000, near - 1)

    table = call(
        group_table_body,
        jax.ShapeDtypeStruct((64, 128), jnp.int32),
        members.reshape(256, 128),
        flops=2 * 128 * 32768 * 128,
        nbytes=1 << 17,
    )
    base = jnp.stack([index_x * 8, index_y * 8])
    inverse_counts = call(
        counts_body,
        jax.ShapeDtypeStruct((2048, 128), F32),
        near,
        base,
        specs=[VMEM, SMEM],
        flops=2 * 2048 * 640 * 128,
        nbytes=1 << 20,
    )

    begin_x = corners[0] - (index_x * 8 - margin)
    begin_y = corners[1] - (index_y * 8 - margin)
    first = (begin_x * 16 + begin_y) * 32 + corners[2]
    cells, grams = call(
        gram_body,
        (jax.ShapeDtypeStruct((8192, 128), F32), jax.ShapeDtypeStruct((8192, 128), F32)),
        first,
        mixture,
        yb,
        ya,
        xb,
        xa,
        specs=[SMEM] + [VMEM] * 5,
        flops=2 * 64 * 512 * 128 * 128,
        nbytes=10 << 20,
    )
    rows = exchange(grams, 64)
    sums = call(
        group_sum_body,
        jax.ShapeDtypeStruct((2048, 128), F32),
        table,
        rows,
        scratch=[pltpu.VMEM((8192, 256), BF16), pltpu.VMEM((256, 8192), BF16)],
        flops=2 * 2048 * 8192 * 256,
        nbytes=5 << 20,
    )
    mine = exchange(sums, 16)
    tau = lax.dynamic_slice_in_dim(thresholds, myself * 16, 16)
    factors = call(
        shrink_body,
        jax.ShapeDtypeStruct((2048, 128), F32),
        tau,
        mine,
        specs=[SMEM, VMEM],
        scratch=[pltpu.VMEM((16, 128, 128), F32), pltpu.VMEM((128, 128), F32)],
        flops=2 * 16 * 8 * 6 * 128**3,
        nbytes=2 << 20,
    )
    factor_rows = exchange(factors.astype(BF16), 16)
    patch_rows = call(
        expand_body,
        jax.ShapeDtypeStruct((8192, 128), BF16),
        table,
        factor_rows,
        scratch=[pltpu.VMEM((128, 64), jnp.int32)],
        flops=2 * 2048 * 8192 * 128,
        nbytes=3 << 20,
    )
    patch_factors = exchange(patch_rows, 64)
    aggregate = call(
        apply_body,
        jax.ShapeDtypeStruct((8192, 128), F32),
        first,
        cells,
        patch_factors,
        specs=[SMEM, VMEM, VMEM],
        scratch=[pltpu.VMEM((8192, 128), F32)],
        flops=2 * 64 * 512 * 128 * 128,
        nbytes=10 << 20,
    )
    aggregate = aggregate.reshape(16, 16, 32, 128)

    from_low, from_high = neighbors(
        aggregate, "gx", aggregate[:margin].astype(BF16), aggregate[16 - margin :].astype(BF16)
    )
    inner = aggregate[margin : 16 - margin]
    inner = jnp.concatenate(
        [inner[:margin] + from_low.astype(F32), inner[margin:] + from_high.astype(F32)], 0
    )
    from_low, from_high = neighbors(
        inner, "gy", inner[:, :margin].astype(BF16), inner[:, 16 - margin :].astype(BF16)
    )
    sums = inner[:, margin : 16 - margin]
    sums = jnp.concatenate(
        [sums[:, :margin] + from_low.astype(F32), sums[:, margin:] + from_high.astype(F32)], 1
    )
    lowrank = (sums + DATA_WEIGHT * mixture.astype(F32)) * inverse_counts.reshape(8, 8, 32, 128)
    dual_next = dual.astype(F32) + estimate.astype(F32) - lowrank
    return lowrank, dual_next


def solution(mesh):
    in_specs = (
        P("gx", "gy", None, None),
        P("gx", "gy", None, None),
        P(None, ("gx", "gy")),
        P(),
        P(),
    )
    out_specs = (P("gx", "gy", None, None), P("gx", "gy", None, None))
    return jax.shard_map(shards, mesh=mesh, in_specs=in_specs, out_specs=out_specs, check_vma=False)
```

time: 1610 us -> 329 us (0.20)
  other arithmetic: 770 us -> 6.63 us
  local copies, waits for them, and re-layouts: 360 us -> 3.97 us
  waiting for transfers between devices: 360 us -> 102 us
  Pallas kernels: 0 us -> 135 us
  matrix products: 35.9 us -> 0 us
  blocking collectives: 0 us -> 17.5 us
    scatter-add x10 -> x0, other arithmetic: 405 us -> none  [the longest x1 226 us: shards(): jnp.zeros((wide_x * wide_y * cells_z,), jnp.float32)]
    another operation x6 -> x3, other arithmetic: 346 us -> 2.74 us  [the longest x3 188 us: shrink(): cholesky_factor = jnp.linalg.cholesky(system)]
    all_to_all x3, waiting for transfers between devices: 326 us -> 55 us  [exchange(): rows = lax.all_to_all(rows, BOTH, split_axis=0, concat_axis=0, tiled=True)]
    gather x5 -> x0, local copies, waits for them, and re-layouts: 146 us -> none  [the longest x1 114 us: add_block(): values = cell_rows[picked]]
    pallas_call x0 -> x7, Pallas kernels: none -> 135 us  [call(): pl.pallas_call(body, out_shape=out_shape, in_specs=specs or [VMEM] * len(...]
    scatter x3 -> x0, local copies, waits for them, and re-layouts: 134 us -> none  [the longest x1 120 us: shards(): jnp.zeros((patch_total,), jnp.int32).at[listed].set(numbers, mode='drop')]
    reshape x3 -> x1, local copies, waits for them, and re-layouts: 53.7 us -> 0.31 us  [shards(): members.reshape(256, 128)]
    dot_general x4 -> x0, matrix products: 34.1 us -> none  [the longest x1 11.5 us: add_block(): jnp.einsum('kvc,kcd->kvd', values, factor, preferred_element_type=jnp.flo...]
  transfers between devices with their start and end apart: 15 -> 15, of which waited for: 7 -> 12; matrix products, arithmetic and copies ran while one was open for 32% -> 2% of each run, Pallas kernels for 0% -> 9%
where the time goes in v1:
time: 329 us; the launch traced here: 328 us
  Pallas kernels  135 us (41%)
  waiting for transfers between devices  102 us (31%)
  starting transfers between devices  61.8 us (19%)
  blocking collectives  17.5 us (5%)
  other arithmetic  6.63 us (2%)
  local copies, waits for them, and re-layouts  3.97 us (1%)
    pallas_call x7, Pallas kernels, call(): pl.pallas_call(body, out_shape=out_shape, in_specs=specs or [VMEM] * len(...  135 us
    all_to_all x3, waiting for transfers between devices, exchange(): rows = lax.all_to_all(rows, BOTH, split_axis=0, concat_axis=0, tiled=True)  55 us
    ppermute x6, waiting for transfers between devices, neighbors(): before = lax.ppermute(last, axis, up)  29.6 us
    all_to_all x3, starting transfers between devices, exchange(): rows = lax.all_to_all(rows, BOTH, split_axis=0, concat_axis=0, tiled=True)  27.4 us
    ppermute x6, starting transfers between devices, neighbors(): after = lax.ppermute(first, axis, down)  18.2 us
    all_to_all x1, blocking collectives, exchange(): rows = lax.all_to_all(rows, BOTH, split_axis=0, concat_axis=0, tiled=True)  17.5 us
    ppermute x6, waiting for transfers between devices, neighbors(): after = lax.ppermute(first, axis, down)  17 us
    ppermute x6, starting transfers between devices, neighbors(): before = lax.ppermute(last, axis, up)  16.2 us
  transfers between devices with their start and end apart: 15, of which 12 were waited for; matrix products, arithmetic and copies ran while one was open for 2% of the time, Pallas kernels for 9%

profile of v1, /device:TPU:104, one launch (start us, length us, event | category | flops | bytes accessed | tf_op | source)
XLA Modules:
  0.0 327.8 jit_solution(9364433995044347316)
XLA Ops:
  4.1 3.8 %collective-permute-start.1 = (bf16[8,4,32,128]{3,2,1,0:T(8,128)(2,1)S(1)}, bf16[8,4,32,128]{3,2,1,0:T(8,128)(2,1)S(1)}, u32[]{:S(2)}, u32[]{:S(2)}) collective-permute-start(bf16[8,4,32,128]{3,2,1,0:T(8,128)(2,1)S(1)} %get-tuple-element.18), channel_id=1, source_target_pairs={{1,0},{2,1},{3,2},{4,3},{5,4},{6,5},{7,6},{8,7},{9,8},{10,9},{11,1... | collective-permute-start | bytes 786440 | tf_op jit(solution)/shard_map/ppermute | solution.py:40
  7.9 4.1 %collective-permute-done.yb_ref = bf16[8,4,32,128]{3,2,1,0:T(8,128)(2,1)S(1)} collective-permute-done((bf16[8,4,32,128]{3,2,1,0:T(8,128)(2,1)S(1)}, bf16[8,4,32,128]{3,2,1,0:T(8,128)(2,1)S(1)}, u32[]{:S(2)}, u32[]{:S(2)}) %collective-permute-start) | collective-permute-done | bytes 262176 | tf_op jit(solution)/shard_map/ppermute | solution.py:39
  12.0 4.0 %collective-permute-done.1.ya_ref = bf16[8,4,32,128]{3,2,1,0:T(8,128)(2,1)S(1)} collective-permute-done((bf16[8,4,32,128]{3,2,1,0:T(8,128)(2,1)S(1)}, bf16[8,4,32,128]{3,2,1,0:T(8,128)(2,1)S(1)}, u32[]{:S(2)}, u32[]{:S(2)}) %collective-permute-start.1) | collective-permute-done | bytes 262176 | tf_op jit(solution)/shard_map/ppermute | solution.py:40
  18.2 3.6 %collective-permute-start.3 = (bf16[4,16,32,128]{3,2,1,0:T(8,128)(2,1)S(1)}, bf16[4,16,32,128]{3,2,1,0:T(8,128)(2,1)S(1)}, u32[]{:S(2)}, u32[]{:S(2)}) collective-permute-start(bf16[4,16,32,128]{3,2,1,0:T(8,128)(2,1)S(1)} %get-tuple-element.16), channel_id=1, source_target_pairs={{16,0},{32,16},{48,32},{64,48},{80,64},{96,80},{112,96},{17,1},{33... | collective-permute-start | bytes 1572872 | tf_op jit(solution)/shard_map/ppermute | solution.py:40
  21.9 4.9 %collective-permute-done.2.xb_ref = bf16[4,16,32,128]{3,2,1,0:T(8,128)(2,1)S(1)} collective-permute-done((bf16[4,16,32,128]{3,2,1,0:T(8,128)(2,1)S(1)}, bf16[4,16,32,128]{3,2,1,0:T(8,128)(2,1)S(1)}, u32[]{:S(2)}, u32[]{:S(2)}) %collective-permute-start.2) | collective-permute-done | bytes 524320 | tf_op jit(solution)/shard_map/ppermute | solution.py:39
  28.5 14.9 %shard_map.68 = (f32[8192,128]{1,0:T(8,128)}, f32[8192,128]{1,0:T(8,128)}) custom-call(s32[64]{0:T(128)S(1)} %add_bitcast_fusion.first_ref, bf16[8,8,32,128]{3,2,1,0:T(8,128)(2,1)S(1)} %fusion.3.own_ref, bf16[8,4,32,128]{3,2,1,0:T(8,128)(2,1)S(1)} %collective-permute-done.yb_ref, bf16[8,4,32,128]{3,2,1,0:T(8,128)(2,1)S(1)} %collective-permute-done.1.ya_ref, ...), custom_call_target="tpu_custom_call" | custom-call | flops 1073741824 | bytes 10485760 | tf_op jit(solution)/shard_map/pallas_call | solution.py:24
  43.4 11.4 %all-to-all-start = ((f32[128,64,128]{2,1,0:T(8,128)}), f32[128,64,128]{2,1,0:T(8,128)}, u32[]{:S(2)}, u32[]{:S(2)}) async-start(f32[128,64,128]{2,1,0:T(8,128)} %bitcast.22), calls=%async_computation | async-start | bytes 8388608 | tf_op jit(solution)/shard_map/all_to_all | solution.py:228
  55.5 8.0 %shard_map.69.group_ref = s32[64,128]{1,0:T(8,128)S(1)} custom-call(s32[256,128]{1,0:T(8,128)S(1)} %reshape.51.members_ref), custom_call_target="tpu_custom_call" | custom-call | flops 1073741824 | bytes 131072 | tf_op jit(solution)/shard_map/pallas_call | solution.py:24
  63.4 40.0 %all-to-all-done = f32[128,64,128]{2,1,0:T(8,128)} async-done(((f32[128,64,128]{2,1,0:T(8,128)}), f32[128,64,128]{2,1,0:T(8,128)}, u32[]{:S(2)}, u32[]{:S(2)}) %all-to-all-start) | async-done | bytes 4194336 | tf_op jit(solution)/shard_map/all_to_all | solution.py:228
  103.4 15.0 %shard_map.70 = f32[2048,128]{1,0:T(8,128)} custom-call(s32[64,128]{1,0:T(8,128)S(1)} %shard_map.69.group_ref, f32[8192,128]{1,0:T(8,128)} %bitcast.2.rows_ref), custom_call_target="tpu_custom_call" | custom-call | flops 8589934592 | bytes 5242880 | tf_op jit(solution)/shard_map/pallas_call | solution.py:24
  118.5 8.0 %all-to-all-start.1 = ((f32[128,16,128]{2,1,0:T(8,128)}), f32[128,16,128]{2,1,0:T(8,128)S(1)}, u32[]{:S(2)}, u32[]{:S(2)}) async-start(f32[128,16,128]{2,1,0:T(8,128)} %bitcast.3), calls=%async_computation.1 | async-start | bytes 2097152 | tf_op jit(solution)/shard_map/all_to_all | solution.py:228
  127.3 15.0 %all-to-all-done.1 = f32[128,16,128]{2,1,0:T(8,128)S(1)} async-done(((f32[128,16,128]{2,1,0:T(8,128)}), f32[128,16,128]{2,1,0:T(8,128)S(1)}, u32[]{:S(2)}, u32[]{:S(2)}) %all-to-all-start.1) | async-done | bytes 1048608 | tf_op jit(solution)/shard_map/all_to_all | solution.py:228
  142.3 65.8 %shard_map.71 = f32[2048,128]{1,0:T(8,128)S(1)} custom-call(f32[16]{0:T(128)S(1)} %dynamic_slice.3.tau_ref, f32[2048,128]{1,0:T(8,128)S(1)} %bitcast.19), custom_call_target="tpu_custom_call" | custom-call | flops 3221225472 | bytes 2097152 | tf_op jit(solution)/shard_map/pallas_call | solution.py:24
  208.1 17.5 %all_to_all.20 = bf16[128,16,128]{2,1,0:T(8,128)(2,1)S(1)} all-to-all(bf16[128,16,128]{2,1,0:T(8,128)(2,1)S(1)} %bitcast.25), channel_id=1, replica_groups=mesh['gx'=8,'gy'=16] {'gx','gy'}, dimensions={0} | all-to-all | bytes 1048576 | tf_op jit(solution)/shard_map/all_to_all | solution.py:228
  225.6 9.1 %shard_map.72 = bf16[8192,128]{1,0:T(8,128)(2,1)S(1)} custom-call(s32[64,128]{1,0:T(8,128)S(1)} %shard_map.69.group_ref, bf16[2048,128]{1,0:T(8,128)(2,1)S(1)} %bitcast.21), custom_call_target="tpu_custom_call" | custom-call | flops 4294967296 | bytes 3145728 | tf_op jit(solution)/shard_map/pallas_call | solution.py:24
  236.1 8.0 %all-to-all-start.3 = ((bf16[128,64,128]{2,1,0:T(8,128)(2,1)}), bf16[128,64,128]{2,1,0:T(8,128)(2,1)S(1)}, u32[]{:S(2)}, u32[]{:S(2)}) async-start(bf16[128,64,128]{2,1,0:T(8,128)(2,1)} %bitcast.18), calls=%async_computation.3 | async-start | bytes 4194304 | tf_op jit(solution)/shard_map/all_to_all | solution.py:228
  246.6 3.3 collective-permute-start.9
  249.9 16.5 %collective-permute-done.8 = s32[3,64]{1,0:T(4,128)S(1)} collective-permute-done((s32[3,64]{1,0:T(4,128)S(1)}, s32[3,64]{1,0:T(4,128)S(1)}, u32[]{:S(2)}, u32[]{:S(2)}) %collective-permute-start.8) | collective-permute-done | bytes 800 | tf_op jit(solution)/shard_map/ppermute | solution.py:39
  269.5 3.6 %collective-permute-start.11 = (s32[3,192]{1,0:T(4,128)S(1)}, s32[3,192]{1,0:T(4,128)S(1)}, u32[]{:S(2)}, u32[]{:S(2)}) collective-permute-start(s32[3,192]{1,0:T(4,128)S(1)} %pad_add_fusion), channel_id=1, source_target_pairs={{16,0},{32,16},{48,32},{64,48},{80,64},{96,80},{112,96},{17,1},{33... | collective-permute-start | bytes 6920 | tf_op jit(solution)/shard_map/ppermute | solution.py:40
  273.2 20.0 %shard_map.73 = f32[8192,128]{1,0:T(8,128)} custom-call(s32[64]{0:T(128)S(1)} %add_bitcast_fusion.first_ref, f32[8192,128]{1,0:T(8,128)} %get-tuple-element.4.cells_ref, bf16[8192,128]{1,0:T(8,128)(2,1)S(1)} %bitcast.17), custom_call_target="tpu_custom_call" | custom-call | flops 1073741824 | bytes 10485760 | tf_op jit(solution)/shard_map/pallas_call | solution.py:24
  300.3 4.1 %collective-permute-done.5 = bf16[4,16,32,128]{3,2,1,0:T(8,128)(2,1)S(1)} collective-permute-done((bf16[4,16,32,128]{3,2,1,0:T(8,128)(2,1)S(1)}, bf16[4,16,32,128]{3,2,1,0:T(8,128)(2,1)S(1)}, u32[]{:S(2)}, u32[]{:S(2)}) %collective-permute-start.5) | collective-permute-done | bytes 524320 | tf_op jit(solution)/shard_map/ppermute | solution.py:40
  304.6 3.6 %collective-permute-done.4 = bf16[4,16,32,128]{3,2,1,0:T(8,128)(2,1)S(1)} collective-permute-done((bf16[4,16,32,128]{3,2,1,0:T(8,128)(2,1)S(1)}, bf16[4,16,32,128]{3,2,1,0:T(8,128)(2,1)S(1)}, u32[]{:S(2)}, u32[]{:S(2)}) %collective-permute-start.4) | collective-permute-done | bytes 524320 | tf_op jit(solution)/shard_map/ppermute | solution.py:39
  309.3 5.4 %collective-permute-start.6 = (bf16[8,4,32,128]{3,2,1,0:T(8,128)(2,1)}, bf16[8,4,32,128]{3,2,1,0:T(8,128)(2,1)S(1)}, u32[]{:S(2)}, u32[]{:S(2)}) collective-permute-start(bf16[8,4,32,128]{3,2,1,0:T(8,128)(2,1)} %get-tuple-element.14), channel_id=1, source_target_pairs={{0,1},{1,2},{2,3},{3,4},{4,5},{5,6},{6,7},{7,8},{8,9},{9,10},{10,1... | collective-permute-start | bytes 786440 | tf_op jit(solution)/shard_map/ppermute | solution.py:39
  319.9 5.9 %collective-permute-done.7 = bf16[8,4,32,128]{3,2,1,0:T(8,128)(2,1)S(1)} collective-permute-done((bf16[8,4,32,128]{3,2,1,0:T(8,128)(2,1)S(1)}, bf16[8,4,32,128]{3,2,1,0:T(8,128)(2,1)S(1)}, u32[]{:S(2)}, u32[]{:S(2)}) %collective-permute-start.7) | collective-permute-done | bytes 262176 | tf_op jit(solution)/shard_map/ppermute | solution.py:40
  (50 shorter events, 31.2 us)
Async XLA Ops:
  2.0 9.9 %collective-permute-start = (bf16[8,4,32,128]{3,2,1,0:T(8,128)(2,1)S(1)}, bf16[8,4,32,128]{3,2,1,0:T(8,128)(2,1)S(1)}, u32[]{:S(2)}, u32[]{:S(2)}) collective-permute-start(bf16[8,4,32,128]{3,2,1,0:T(8,128)(2,1)S(1)} %get-tuple-element.19), channel_id=1, source_target_pairs={{0,1},{1,2},{2,3},{3,4},{4,5},{5,6},{6,7},{7,8},{8,9},{9,10},{10,1... | collective-permute-start | bytes 786440 | tf_op jit(solution)/shard_map/ppermute | solution.py:39
  4.1 17.8 %copy-start.5 = (s32[3,64]{1,0:T(4,128)S(1)}, s32[3,64]{1,0:T(4,128)}, u32[]{:S(2)}) copy-start(s32[3,64]{1,0:T(4,128)} %param.7) | copy-start | bytes 2308
  4.1 11.9 %collective-permute-start.1 = (bf16[8,4,32,128]{3,2,1,0:T(8,128)(2,1)S(1)}, bf16[8,4,32,128]{3,2,1,0:T(8,128)(2,1)S(1)}, u32[]{:S(2)}, u32[]{:S(2)}) collective-permute-start(bf16[8,4,32,128]{3,2,1,0:T(8,128)(2,1)S(1)} %get-tuple-element.18), channel_id=1, source_target_pairs={{1,0},{2,1},{3,2},{4,3},{5,4},{6,5},{7,6},{8,7},{9,8},{10,9},{11,1... | collective-permute-start | bytes 786440 | tf_op jit(solution)/shard_map/ppermute | solution.py:40
  16.2 10.5 %collective-permute-start.2 = (bf16[4,16,32,128]{3,2,1,0:T(8,128)(2,1)S(1)}, bf16[4,16,32,128]{3,2,1,0:T(8,128)(2,1)S(1)}, u32[]{:S(2)}, u32[]{:S(2)}) collective-permute-start(bf16[4,16,32,128]{3,2,1,0:T(8,128)(2,1)S(1)} %get-tuple-element.17), channel_id=1, source_target_pairs={{0,16},{16,32},{32,48},{48,64},{64,80},{80,96},{96,112},{1,17},{17... | collective-permute-start | bytes 1572872 | tf_op jit(solution)/shard_map/ppermute | solution.py:39
  18.2 10.3 %collective-permute-start.3 = (bf16[4,16,32,128]{3,2,1,0:T(8,128)(2,1)S(1)}, bf16[4,16,32,128]{3,2,1,0:T(8,128)(2,1)S(1)}, u32[]{:S(2)}, u32[]{:S(2)}) collective-permute-start(bf16[4,16,32,128]{3,2,1,0:T(8,128)(2,1)S(1)} %get-tuple-element.16), channel_id=1, source_target_pairs={{16,0},{32,16},{48,32},{64,48},{80,64},{96,80},{112,96},{17,1},{33... | collective-permute-start | bytes 1572872 | tf_op jit(solution)/shard_map/ppermute | solution.py:40
  43.4 11.4 %copy-start.4 = (s32[2048,16]{0,1:T(8,128)S(1)}, s32[2048,16]{0,1:T(8,128)}, u32[]{:S(2)}) copy-start(s32[2048,16]{0,1:T(8,128)} %param.8) | copy-start | bytes 393220
  43.4 60.1 %all-to-all-start = ((f32[128,64,128]{2,1,0:T(8,128)}), f32[128,64,128]{2,1,0:T(8,128)}, u32[]{:S(2)}, u32[]{:S(2)}) async-start(f32[128,64,128]{2,1,0:T(8,128)} %bitcast.22), calls=%async_computation | async-start | bytes 8388608 | tf_op jit(solution)/shard_map/all_to_all | solution.py:228
  118.5 23.8 %all-to-all-start.1 = ((f32[128,16,128]{2,1,0:T(8,128)}), f32[128,16,128]{2,1,0:T(8,128)S(1)}, u32[]{:S(2)}, u32[]{:S(2)}) async-start(f32[128,16,128]{2,1,0:T(8,128)} %bitcast.3), calls=%async_computation.1 | async-start | bytes 2097152 | tf_op jit(solution)/shard_map/all_to_all | solution.py:228
  234.7 1.4 copy-start
  236.1 37.1 %all-to-all-start.3 = ((bf16[128,64,128]{2,1,0:T(8,128)(2,1)}), bf16[128,64,128]{2,1,0:T(8,128)(2,1)S(1)}, u32[]{:S(2)}, u32[]{:S(2)}) async-start(bf16[128,64,128]{2,1,0:T(8,128)(2,1)} %bitcast.18), calls=%async_computation.3 | async-start | bytes 4194304 | tf_op jit(solution)/shard_map/all_to_all | solution.py:228
  244.0 22.4 %collective-permute-start.8 = (s32[3,64]{1,0:T(4,128)S(1)}, s32[3,64]{1,0:T(4,128)S(1)}, u32[]{:S(2)}, u32[]{:S(2)}) collective-permute-start(s32[3,64]{1,0:T(4,128)S(1)} %broadcast_add_fusion), channel_id=1, source_target_pairs={{0,1},{1,2},{2,3},{3,4},{4,5},{5,6},{6,7},{7,8},{8,9},{9,10},{10,1... | collective-permute-start | bytes 2312 | tf_op jit(solution)/shard_map/ppermute | solution.py:39
  246.6 20.9 %collective-permute-start.9 = (s32[3,64]{1,0:T(4,128)S(1)}, s32[3,64]{1,0:T(4,128)S(1)}, u32[]{:S(2)}, u32[]{:S(2)}) collective-permute-start(s32[3,64]{1,0:T(4,128)S(1)} %broadcast_add_fusion), channel_id=1, source_target_pairs={{1,0},{2,1},{3,2},{4,3},{5,4},{6,5},{7,6},{8,7},{9,8},{10,9},{11,1... | collective-permute-start | bytes 2312 | tf_op jit(solution)/shard_map/ppermute | solution.py:40
  267.6 49.1 %collective-permute-start.10 = (s32[3,192]{1,0:T(4,128)S(1)}, s32[3,192]{1,0:T(4,128)S(1)}, u32[]{:S(2)}, u32[]{:S(2)}) collective-permute-start(s32[3,192]{1,0:T(4,128)S(1)} %pad_add_fusion), channel_id=1, source_target_pairs={{0,16},{16,32},{32,48},{48,64},{64,80},{80,96},{96,112},{1,17},{17... | collective-permute-start | bytes 6920 | tf_op jit(solution)/shard_map/ppermute | solution.py:39
  269.5 47.2 %collective-permute-start.11 = (s32[3,192]{1,0:T(4,128)S(1)}, s32[3,192]{1,0:T(4,128)S(1)}, u32[]{:S(2)}, u32[]{:S(2)}) collective-permute-start(s32[3,192]{1,0:T(4,128)S(1)} %pad_add_fusion), channel_id=1, source_target_pairs={{16,0},{32,16},{48,32},{64,48},{80,64},{96,80},{112,96},{17,1},{33... | collective-permute-start | bytes 6920 | tf_op jit(solution)/shard_map/ppermute | solution.py:40
  293.2 7.0 %copy-start.1 = (f32[8192,128]{1,0:T(8,128)S(1)}, f32[8192,128]{1,0:T(8,128)}, u32[]{:S(2)}) copy-start(f32[8192,128]{1,0:T(8,128)} %shard_map.73) | copy-start | bytes 12582916
  295.8 8.6 %collective-permute-start.5 = (bf16[4,16,32,128]{3,2,1,0:T(8,128)(2,1)S(1)}, bf16[4,16,32,128]{3,2,1,0:T(8,128)(2,1)S(1)}, u32[]{:S(2)}, u32[]{:S(2)}) collective-permute-start(bf16[4,16,32,128]{3,2,1,0:T(8,128)(2,1)S(1)} %bitcast.27), channel_id=1, source_target_pairs={{16,0},{32,16},{48,32},{64,48},{80,64},{96,80},{112,96},{17,1},{33... | collective-permute-start | bytes 1572872 | tf_op jit(solution)/shard_map/ppermute | solution.py:40
  297.8 10.5 %collective-permute-start.4 = (bf16[4,16,32,128]{3,2,1,0:T(8,128)(2,1)S(1)}, bf16[4,16,32,128]{3,2,1,0:T(8,128)(2,1)S(1)}, u32[]{:S(2)}, u32[]{:S(2)}) collective-permute-start(bf16[4,16,32,128]{3,2,1,0:T(8,128)(2,1)S(1)} %bitcast.26), channel_id=1, source_target_pairs={{0,16},{16,32},{32,48},{48,64},{64,80},{80,96},{96,112},{1,17},{17... | collective-permute-start | bytes 1572872 | tf_op jit(solution)/shard_map/ppermute | solution.py:39
  309.3 10.6 %collective-permute-start.6 = (bf16[8,4,32,128]{3,2,1,0:T(8,128)(2,1)}, bf16[8,4,32,128]{3,2,1,0:T(8,128)(2,1)S(1)}, u32[]{:S(2)}, u32[]{:S(2)}) collective-permute-start(bf16[8,4,32,128]{3,2,1,0:T(8,128)(2,1)} %get-tuple-element.14), channel_id=1, source_target_pairs={{0,1},{1,2},{2,3},{3,4},{4,5},{5,6},{6,7},{7,8},{8,9},{9,10},{10,1... | collective-permute-start | bytes 786440 | tf_op jit(solution)/shard_map/ppermute | solution.py:39
  314.7 11.1 %collective-permute-start.7 = (bf16[8,4,32,128]{3,2,1,0:T(8,128)(2,1)S(1)}, bf16[8,4,32,128]{3,2,1,0:T(8,128)(2,1)S(1)}, u32[]{:S(2)}, u32[]{:S(2)}) collective-permute-start(bf16[8,4,32,128]{3,2,1,0:T(8,128)(2,1)S(1)} %get-tuple-element.15), channel_id=1, source_target_pairs={{1,0},{2,1},{3,2},{4,3},{5,4},{6,5},{7,6},{8,7},{9,8},{10,9},{11,1... | collective-permute-start | bytes 786440 | tf_op jit(solution)/shard_map/ppermute | solution.py:40
  319.4 6.6 %copy-start.2 = (bf16[8,8,32,128]{3,2,1,0:T(8,128)(2,1)S(1)}, bf16[8,8,32,128]{3,2,1,0:T(8,128)(2,1)}, u32[]{:S(2)}) copy-start(bf16[8,8,32,128]{3,2,1,0:T(8,128)(2,1)} %param.6) | copy-start | bytes 1572868
  319.4 6.6 %copy-start.3 = (bf16[8,8,32,128]{3,2,1,0:T(8,128)(2,1)S(1)}, bf16[8,8,32,128]{3,2,1,0:T(8,128)(2,1)}, u32[]{:S(2)}) copy-start(bf16[8,8,32,128]{3,2,1,0:T(8,128)(2,1)} %param.5) | copy-start | bytes 1572868

commit v2 on v1

--- a/solution.py
+++ b/solution.py
@@ -41,28 +41,52 @@
     return before, after
 
 
-def group_table_body(members_ref, out_ref):
+def packed_masks():
+    row = lax.broadcasted_iota(jnp.int32, (64, 128), 0)
+    lane = lax.broadcasted_iota(jnp.int32, (64, 128), 1)
+    return (lane < 64) & (row > lane), row == lane, lane == row + 64
+
+
+def pack_symmetric(matrix, masks):
+    moved, _, low_diagonal = masks
+    top, bottom = matrix[:64], matrix[64:]
+    packed = jnp.where(moved, pltpu.roll(bottom, 64, axis=1), top)
+    return packed, jnp.where(low_diagonal, bottom, 0.0)
+
+
+def unpack_symmetric(packed, diagonal, masks):
+    moved, top_diagonal, low_diagonal = masks
+    top = jnp.where(moved, 0.0, jnp.where(top_diagonal, 0.5 * packed, packed))
+    bottom = pltpu.roll(jnp.where(moved, packed, 0.0), 64, axis=1)
+    bottom = bottom + jnp.where(low_diagonal, 0.5 * diagonal, 0.0)
+    half = jnp.concatenate([top, bottom], 0)
+    return half + half.T
+
+
+def group_table_body(side_ref, members_ref, out_ref):
     rows = members_ref.shape[0]
     per = 8
-    high = lax.broadcasted_iota(jnp.int32, (64, 128), 0)
+    high = lax.broadcasted_iota(jnp.int32, (32, 128), 0)
     low = lax.broadcasted_iota(jnp.int32, (128, 128), 0)
     lane = lax.broadcasted_iota(jnp.int32, (1, 128), 1)
+    side = side_ref[0]
 
     def step(i, acc):
         block = members_ref[pl.ds(pl.multiple_of(i * per, per), per), :]
         coarse, fine, lows = [], [], []
         for j in range(per):
             entry = block[j : j + 1, :]
-            on = high == (entry >> 7)
+            at_high = jnp.where(((entry >> 5) & 1) == side, entry >> 8, -1)
+            at_low = ((entry >> 6) & 3) * 32 + (entry & 31)
+            on = high == at_high
             group = (i * per + j) * 8 + (lane >> 4)
-            zero = jnp.zeros((64, 128), F32)
             coarse.append(
-                jnp.where(on, jnp.broadcast_to((group >> 4).astype(F32), (64, 128)), zero)
+                jnp.where(on, jnp.broadcast_to((group >> 4).astype(F32), (32, 128)), 0.0)
             )
             fine.append(
-                jnp.where(on, jnp.broadcast_to((group & 15).astype(F32), (64, 128)), zero)
-            )
-            lows.append(jnp.where(low == (entry & 127), 1.0, 0.0))
+                jnp.where(on, jnp.broadcast_to((group & 15).astype(F32), (32, 128)), 0.0)
+            )
+            lows.append(jnp.where(low == at_low, 1.0, 0.0))
         left = jnp.concatenate(
             [jnp.concatenate(coarse, 1), jnp.concatenate(fine, 1)], 0
         ).astype(BF16)
@@ -71,8 +95,8 @@
             left, right, (((1,), (1,)), ((), ())), preferred_element_type=F32
         )
 
-    acc = lax.fori_loop(0, rows // per, step, jnp.zeros((128, 128), F32))
-    out_ref[...] = (acc[:64] * 16.0 + acc[64:]).astype(jnp.int32)
+    acc = lax.fori_loop(0, rows // per, step, jnp.zeros((64, 128), F32))
+    out_ref[...] = (acc[:32] * 16.0 + acc[32:]).astype(jnp.int32)
 
 
 def counts_body(corner_ref, base_ref, out_ref):
@@ -105,7 +129,7 @@
     return jnp.concatenate(rows, 0)
 
 
-def gram_body(first_ref, own_ref, yb_ref, ya_ref, xb_ref, xa_ref, cells_ref, out_ref):
+def gram_body(first_ref, own_ref, yb_ref, ya_ref, xb_ref, xa_ref, cells_ref, out_ref, diag_ref):
     cells_ref[pl.ds(0, 2048), :] = xb_ref[...].reshape(2048, 128).astype(F32)
     cells_ref[pl.ds(6144, 2048), :] = xa_ref[...].reshape(2048, 128).astype(F32)
 
@@ -117,35 +141,62 @@
         return 0
 
     lax.fori_loop(0, 8, fill, 0)
+    diag_ref[...] = jnp.zeros_like(diag_ref)
+    masks = packed_masks()
 
     def patch(p, _):
         values = load_patch(cells_ref, first_ref[p]).astype(BF16)
         gram = lax.dot_general(values, values, (((0,), (0,)), ((), ())), preferred_element_type=F32)
-        out_ref[pl.ds(p, 128, stride=64), :] = gram
+        packed, rest = pack_symmetric(gram, masks)
+        side = p // 32
+        out_ref[pl.ds(side * (64 * 33) + p - side * 32, 64, stride=33), :] = packed
+        diag_ref[pl.ds(p, 1), :] = jnp.sum(rest, axis=0, keepdims=True)
         return 0
 
     lax.fori_loop(0, 64, patch, 0, unroll=2)
-
-
-def group_sum_body(group_ref, rows_ref, out_ref, limbs_ref, hot_ref):
+    turned = diag_ref[...].T[64:]
+    out_ref[pl.ds(32, 64, stride=33), :] = turned
+    out_ref[pl.ds(64 * 33 + 32, 64, stride=33), :] = pltpu.roll(turned, 96, axis=1)
+
+
+def group_sum_body(group_ref, rows_ref, out_ref, limbs_ref, hot_ref, diag_ref):
     def split(i, _):
-        row = pl.multiple_of(i * 128, 128)
-        value = rows_ref[pl.ds(row, 128), :]
+        value = rows_ref[pl.ds(i * 33, 32), :]
         high = value.astype(BF16)
-        limbs_ref[pl.ds(row, 128), 0:128] = high
-        limbs_ref[pl.ds(row, 128), 128:256] = (value - high.astype(F32)).astype(BF16)
-        return 0
-
-    lax.fori_loop(0, 64, split, 0)
+        row = pl.multiple_of(i * 32, 32)
+        limbs_ref[pl.ds(row, 32), 0:128] = high
+        limbs_ref[pl.ds(row, 32), 128:256] = (value - high.astype(F32)).astype(BF16)
+        return 0
+
+    lax.fori_loop(0, 128, split, 0, unroll=4)
+    used = lax.broadcasted_iota(jnp.int32, (32, 128), 1) < 32
+    diagonal = jnp.zeros((32, 128), F32)
+    for c in range(4):
+        part = jnp.where(used, rows_ref[pl.ds(32 + 33 * c, 32, stride=132), :], 0.0)
+        diagonal = diagonal + (pltpu.roll(part, 32 * c, axis=1) if c else part)
+    diag_ref[...] = diagonal
     sub = lax.broadcasted_iota(jnp.int32, (256, 128), 0)
+    eye = lax.broadcasted_iota(jnp.int32, (16, 128), 0) == lax.broadcasted_iota(
+        jnp.int32, (16, 128), 1
+    )
 
     def chunk(i, _):
         base = i * 256
-        for t in range(64):
-            entry = group_ref[t : t + 1, :] - base
-            hot_ref[:, t * 128 : (t + 1) * 128] = jnp.where(sub == entry, 1.0, 0.0).astype(BF16)
+        picked = jnp.zeros((256, 128), F32)
+        for t in range(32):
+            on = sub == group_ref[t : t + 1, :] - base
+            hot_ref[:, t * 128 : (t + 1) * 128] = jnp.where(on, 1.0, 0.0).astype(BF16)
+            picked = picked + jnp.where(on, diag_ref[t : t + 1, :], 0.0)
         total = jnp.dot(hot_ref[...], limbs_ref[...], preferred_element_type=F32)
-        out_ref[pl.ds(pl.multiple_of(base, 256), 256), :] = total[:, :128] + total[:, 128:]
+        total = total[:, :128] + total[:, 128:]
+        picked = jnp.sum(picked, axis=1, keepdims=True)
+        for d in range(16):
+            row = (i * 16 + d) * 17
+            part = slice(d * 16, d * 16 + 16)
+            out_ref[pl.ds(row, 16), :] = total[part]
+            out_ref[pl.ds(row + 16, 1), :] = jnp.sum(
+                jnp.where(eye, picked[part], 0.0), axis=0, keepdims=True
+            )
         return 0
 
     lax.fori_loop(0, 8, chunk, 0)
@@ -155,10 +206,13 @@
     per = 16
     row_id = lax.broadcasted_iota(jnp.int32, (128, 128), 0)
     lane_id = lax.broadcasted_iota(jnp.int32, (128, 128), 1)
-    diagonal = row_id == lane_id
+    eye = jnp.where(row_id == lane_id, 1.0, 0.0)
+    masks = packed_masks()
+    half = 64 * 17
+    diagonals = rows_ref[pl.ds(16, 64, stride=17), :] + rows_ref[pl.ds(half + 16, 64, stride=17), :]
     for g in range(per):
-        matrix = rows_ref[pl.ds(g, 128, stride=per), :]
-        sys_ref[g] = matrix + jnp.where(diagonal, tau_ref[g], 0.0)
+        packed = rows_ref[pl.ds(g, 64, stride=17), :] + rows_ref[pl.ds(half + g, 64, stride=17), :]
+        sys_ref[g] = unpack_symmetric(packed, diagonals[:, g : g + 1], masks) + tau_ref[g] * eye
     panel_sub = lax.broadcasted_iota(jnp.int32, (per, NB, 128), 1)
     panel_lane = lax.broadcasted_iota(jnp.int32, (per, NB, 128), 2)
 
@@ -174,57 +228,118 @@
             cleared = jnp.where(panel_lane == j, 0.0, panel)
             panel = jnp.where(panel_sub == j, scaled, cleared - column * scaled)
         panel = pltpu.roll(panel.reshape(per * NB, 128), start, axis=1).reshape(per, NB, 128)
-        in_block = (lane_id >= start) & (lane_id < start + NB)
+        in_lanes = (lane_id >= start) & (lane_id < start + NB)
+        in_rows = (row_id >= start) & (row_id < start + NB)
         for g in range(per):
-            stage_ref[...] = jnp.zeros((128, 128), F32)
-            stage_ref[pl.ds(start, NB), :] = panel[g]
             matrix = sys_ref[g]
-            update = jnp.dot(
-                matrix, stage_ref[...], precision=lax.Precision.HIGHEST, preferred_element_type=F32
-            )
-            sys_ref[g] = jnp.where(in_block, 0.0, matrix) - update
-            sys_ref[g, pl.ds(start, NB), :] = panel[g]
+            wide = jnp.where(in_rows, jnp.concatenate([panel[g]] * (128 // NB), 0), 0.0)
+            w0, w1, w2 = limbs(wide)
+            a0, a1, a2 = limbs(matrix)
+            main = jnp.dot(
+                jnp.concatenate([a0, a1], 1),
+                jnp.concatenate([jnp.concatenate([w0, w0], 0), jnp.concatenate([w1, w1], 0)], 1),
+                preferred_element_type=F32,
+            )
+            small = jnp.dot(
+                jnp.concatenate([a0, a2], 1),
+                jnp.concatenate([w2, w0], 0),
+                preferred_element_type=F32,
+            )
+            update = main[:, :128] + (main[:, 128:] + small)
+            sys_ref[g] = jnp.where(in_rows, wide, jnp.where(in_lanes, 0.0, matrix) - update)
         return 0
 
     lax.fori_loop(0, 128 // NB, block, 0)
+    place = lax.broadcasted_iota(jnp.int32, (64, 128), 1)
+    extra = jnp.zeros((64, 128), F32)
     for g in range(per):
-        factor = jnp.where(diagonal, 1.0, 0.0) - tau_ref[g] * sys_ref[g]
-        out_ref[pl.ds(g, 128, stride=per), :] = factor
-
-
-def expand_body(group_ref, rows_ref, out_ref, turned_ref):
+        packed, rest = pack_symmetric(eye - tau_ref[g] * sys_ref[g], masks)
+        stage_ref[pl.ds(g, 64, stride=18), :] = packed
+        extra = jnp.where(place == g, jnp.sum(rest, axis=1, keepdims=True), extra)
+    stage_ref[pl.ds(16, 64, stride=18), :] = extra
+    stage_ref[pl.ds(17, 64, stride=18), :] = jnp.zeros((64, 128), F32)
+    result = stage_ref[...].astype(BF16)
+    out_ref[0:1152, :] = result
+    out_ref[1152:2304, :] = result
+
+
+def limbs(value):
+    first = value.astype(BF16)
+    rest = value - first.astype(F32)
+    second = rest.astype(BF16)
+    return first, second, (rest - second.astype(F32)).astype(BF16)
+
+
+def expand_body(group_ref, rows_ref, out_ref, turned_ref, wide_ref, table_ref, stage_ref):
     turned_ref[...] = group_ref[...].astype(F32).T.astype(jnp.int32)
+    wide_ref[...] = rows_ref[...].astype(F32)
+    eye = lax.broadcasted_iota(jnp.int32, (16, 128), 0) == lax.broadcasted_iota(
+        jnp.int32, (16, 128), 1
+    )
+
+    def gather(d, _):
+        row = pl.multiple_of(d * 16, 16)
+        table_ref[pl.ds(row, 16), 0:128] = wide_ref[pl.ds(d * 18, 16), :].astype(BF16)
+        extra = wide_ref[pl.ds(d * 18 + 16, 1), :]
+        table_ref[pl.ds(row, 16), 128:256] = jnp.where(eye, extra, 0.0).astype(BF16)
+        return 0
+
+    lax.fori_loop(0, 128, gather, 0, unroll=4)
     lane = lax.broadcasted_iota(jnp.int32, (128, 2048), 1)
-    table = rows_ref[...]
-    for t in range(64):
+    eye = lax.broadcasted_iota(jnp.int32, (32, 128), 0) == lax.broadcasted_iota(
+        jnp.int32, (32, 128), 1
+    )
+    for t in range(32):
         hot = jnp.where(lane == turned_ref[:, t : t + 1], 1.0, 0.0).astype(BF16)
-        out_ref[t * 128 : (t + 1) * 128, :] = jnp.dot(
-            hot, table, preferred_element_type=F32
-        ).astype(BF16)
-
-
-def apply_body(first_ref, cells_ref, rows_ref, out_ref, wide_ref):
+        both = jnp.dot(hot, table_ref[...], preferred_element_type=F32)
+        value = jnp.sum(both[:, 128:], axis=1, keepdims=True)
+        for s in range(4):
+            row = (t * 4 + s) * 34
+            part = slice(s * 32, s * 32 + 32)
+            stage_ref[row : row + 32, :] = both[part, :128]
+            stage_ref[row + 32 : row + 33, :] = jnp.sum(
+                jnp.where(eye, value[part], 0.0), axis=0, keepdims=True
+            )
+            stage_ref[row + 33 : row + 34, :] = jnp.zeros((1, 128), F32)
+    out_ref[...] = stage_ref[...].astype(BF16)
+
+
+def apply_body(first_ref, cells_ref, rows_ref, inner_ref, low_ref, high_ref, wide_ref, sum_ref):
     wide_ref[...] = rows_ref[...].astype(F32)
-    out_ref[...] = jnp.zeros_like(out_ref)
-
-    def patch(p, _):
-        first = first_ref[p]
-        values = load_patch(cells_ref, first).astype(BF16)
-        factor = wide_ref[pl.ds(p, 128, stride=64), :].astype(BF16)
-        result = jnp.dot(values, factor, preferred_element_type=F32)
-        for a in range(PATCH):
-            for b in range(PATCH):
-                at = pl.ds(first + (a * 16 + b) * 32, PATCH)
-                i = (a * PATCH + b) * PATCH
-                out_ref[at, :] += result[i : i + PATCH]
-        return 0
-
-    lax.fori_loop(0, 64, patch, 0)
-
-
-def exchange(rows, chunk):
+    sum_ref[...] = jnp.zeros_like(sum_ref)
+    masks = packed_masks()
+    lane = lax.broadcasted_iota(jnp.int32, (64, 128), 1)
+
+    def product(p):
+        side = p // 32
+        slot = p - side * 32
+        base = side * (64 * 34)
+        packed = wide_ref[pl.ds(base + slot, 64, stride=34), :]
+        diagonals = wide_ref[pl.ds(base + 32, 64, stride=34), :]
+        diagonal = jnp.sum(jnp.where(lane == slot, diagonals, 0.0), axis=1, keepdims=True)
+        factor = unpack_symmetric(packed, diagonal, masks).astype(BF16)
+        values = load_patch(cells_ref, first_ref[p]).astype(BF16)
+        return jnp.dot(values, factor, preferred_element_type=F32)
+
+    def pair(i, _):
+        for p, result in [(2 * i + k, product(2 * i + k)) for k in range(2)]:
+            first = first_ref[p]
+            for a in range(PATCH):
+                for b in range(PATCH):
+                    at = pl.ds(first + (a * 16 + b) * 32, PATCH)
+                    row = (a * PATCH + b) * PATCH
+                    sum_ref[at, :] += result[row : row + PATCH]
+        return 0
+
+    lax.fori_loop(0, 32, pair, 0)
+    low_ref[...] = sum_ref[0:2048, :].astype(BF16)
+    inner_ref[...] = sum_ref[2048:6144, :]
+    high_ref[...] = sum_ref[6144:8192, :].astype(BF16)
+
+
+def exchange(rows, sublanes):
     shape = rows.shape
-    rows = rows.reshape(128, chunk, 128)
+    rows = rows.reshape(128, shape[0] // (128 * sublanes), sublanes, 128)
     rows = lax.all_to_all(rows, BOTH, split_axis=0, concat_axis=0, tiled=True)
     return rows.reshape(shape)
 
@@ -246,11 +361,14 @@
     near = jnp.concatenate([nb, near, na, jnp.zeros((3, 64), jnp.int32)], 1)
     near = jnp.where(near == 0, -1000, near - 1)
 
+    side = (myself // 64).reshape(1)
     table = call(
         group_table_body,
-        jax.ShapeDtypeStruct((64, 128), jnp.int32),
+        jax.ShapeDtypeStruct((32, 128), jnp.int32),
+        side,
         members.reshape(256, 128),
-        flops=2 * 128 * 32768 * 128,
+        specs=[SMEM, VMEM],
+        flops=2 * 128 * 32768 * 64,
         nbytes=1 << 17,
     )
     base = jnp.stack([index_x * 8, index_y * 8])
@@ -269,7 +387,7 @@
     first = (begin_x * 16 + begin_y) * 32 + corners[2]
     cells, grams = call(
         gram_body,
-        (jax.ShapeDtypeStruct((8192, 128), F32), jax.ShapeDtypeStruct((8192, 128), F32)),
+        (jax.ShapeDtypeStruct((8192, 128), F32), jax.ShapeDtypeStruct((128 * 33, 128), F32)),
         first,
         mixture,
         yb,
@@ -277,59 +395,68 @@
         xb,
         xa,
         specs=[SMEM] + [VMEM] * 5,
+        scratch=[pltpu.VMEM((128, 128), F32)],
         flops=2 * 64 * 512 * 128 * 128,
         nbytes=10 << 20,
     )
-    rows = exchange(grams, 64)
+    rows = exchange(grams, 1)
     sums = call(
         group_sum_body,
-        jax.ShapeDtypeStruct((2048, 128), F32),
+        jax.ShapeDtypeStruct((128 * 17, 128), F32),
         table,
         rows,
-        scratch=[pltpu.VMEM((8192, 256), BF16), pltpu.VMEM((256, 8192), BF16)],
-        flops=2 * 2048 * 8192 * 256,
+        scratch=[
+            pltpu.VMEM((4096, 256), BF16),
+            pltpu.VMEM((256, 4096), BF16),
+            pltpu.VMEM((32, 128), F32),
+        ],
+        flops=2 * 2048 * 4096 * 256,
         nbytes=5 << 20,
     )
-    mine = exchange(sums, 16)
+    mine = exchange(sums, 1)
     tau = lax.dynamic_slice_in_dim(thresholds, myself * 16, 16)
     factors = call(
         shrink_body,
-        jax.ShapeDtypeStruct((2048, 128), F32),
+        jax.ShapeDtypeStruct((128 * 18, 128), BF16),
         tau,
         mine,
         specs=[SMEM, VMEM],
-        scratch=[pltpu.VMEM((16, 128, 128), F32), pltpu.VMEM((128, 128), F32)],
+        scratch=[pltpu.VMEM((16, 128, 128), F32), pltpu.VMEM((64 * 18, 128), F32)],
         flops=2 * 16 * 8 * 6 * 128**3,
         nbytes=2 << 20,
     )
-    factor_rows = exchange(factors.astype(BF16), 16)
+    factor_rows = exchange(factors, 2)
     patch_rows = call(
         expand_body,
-        jax.ShapeDtypeStruct((8192, 128), BF16),
+        jax.ShapeDtypeStruct((128 * 34, 128), BF16),
         table,
         factor_rows,
-        scratch=[pltpu.VMEM((128, 64), jnp.int32)],
-        flops=2 * 2048 * 8192 * 128,
+        scratch=[
+            pltpu.VMEM((128, 32), jnp.int32),
+            pltpu.VMEM((128 * 18, 128), F32),
+            pltpu.VMEM((2048, 256), BF16),
+            pltpu.VMEM((128 * 34, 128), F32),
+        ],
+        flops=2 * 2048 * 4096 * 256,
         nbytes=3 << 20,
     )
-    patch_factors = exchange(patch_rows, 64)
-    aggregate = call(
+    patch_factors = exchange(patch_rows, 2)
+    edge = jax.ShapeDtypeStruct((2048, 128), BF16)
+    inner, low, high = call(
         apply_body,
-        jax.ShapeDtypeStruct((8192, 128), F32),
+        (jax.ShapeDtypeStruct((4096, 128), F32), edge, edge),
         first,
         cells,
         patch_factors,
         specs=[SMEM, VMEM, VMEM],
-        scratch=[pltpu.VMEM((8192, 128), F32)],
+        scratch=[pltpu.VMEM((128 * 34, 128), F32), pltpu.VMEM((8192, 128), F32)],
         flops=2 * 64 * 512 * 128 * 128,
         nbytes=10 << 20,
     )
-    aggregate = aggregate.reshape(16, 16, 32, 128)
-
+    inner = inner.reshape(8, 16, 32, 128)
     from_low, from_high = neighbors(
-        aggregate, "gx", aggregate[:margin].astype(BF16), aggregate[16 - margin :].astype(BF16)
-    )
-    inner = aggregate[margin : 16 - margin]
+        inner, "gx", low.reshape(4, 16, 32, 128), high.reshape(4, 16, 32, 128)
+    )
     inner = jnp.concatenate(
         [inner[:margin] + from_low.astype(F32), inner[margin:] + from_high.astype(F32)], 0
     )

time: 329 us -> 249 us (0.76)
  Pallas kernels: 135 us -> 89 us
  waiting for transfers between devices: 102 us -> 69.3 us
    pallas_call x7, Pallas kernels: 135 us -> 89 us  [call(): pl.pallas_call(body, out_shape=out_shape, in_specs=specs or [VMEM] * len(...]
    all_to_all x3, waiting for transfers between devices: 55 us -> 33.4 us  [exchange(): rows = lax.all_to_all(rows, BOTH, split_axis=0, concat_axis=0, tiled=True)]
    ppermute x6, waiting for transfers between devices: 29.6 us -> 18.9 us  [neighbors(): before = lax.ppermute(last, axis, up)]
  transfers between devices with their start and end apart: 15 -> 15, of which waited for: 12 -> 12; matrix products, arithmetic and copies ran while one was open for 2% -> 2% of each run, Pallas kernels for 9% -> 11%
where the time goes in v2:
time: 249 us; the launch traced here: 248 us
  Pallas kernels  89 us (36%)
  waiting for transfers between devices  69.3 us (28%)
  starting transfers between devices  61 us (24%)
  blocking collectives  18.2 us (7%)
  local copies, waits for them, and re-layouts  5.79 us (2%)
  other arithmetic  4.07 us (2%)
    pallas_call x7, Pallas kernels, call(): pl.pallas_call(body, out_shape=out_shape, in_specs=specs or [VMEM] * len(...  89 us
    all_to_all x3, waiting for transfers between devices, exchange(): rows = lax.all_to_all(rows, BOTH, split_axis=0, concat_axis=0, tiled=True)  33.4 us
    all_to_all x3, starting transfers between devices, exchange(): rows = lax.all_to_all(rows, BOTH, split_axis=0, concat_axis=0, tiled=True)  26.4 us
    ppermute x6, waiting for transfers between devices, neighbors(): before = lax.ppermute(last, axis, up)  18.9 us
    ppermute x6, starting transfers between devices, neighbors(): after = lax.ppermute(first, axis, down)  18.2 us
    all_to_all x1, blocking collectives, exchange(): rows = lax.all_to_all(rows, BOTH, split_axis=0, concat_axis=0, tiled=True)  18.2 us
    ppermute x6, waiting for transfers between devices, neighbors(): after = lax.ppermute(first, axis, down)  17 us
    ppermute x6, starting transfers between devices, neighbors(): before = lax.ppermute(last, axis, up)  16.4 us
  transfers between devices with their start and end apart: 15, of which 12 were waited for; matrix products, arithmetic and copies ran while one was open for 2% of the time, Pallas kernels for 11%

profile of v2, /device:TPU:104, one launch (start us, length us, event | category | flops | bytes accessed | tf_op | source)
XLA Modules:
  0.0 248.3 jit_solution(8131256855057489114)
XLA Ops:
  4.1 3.8 %collective-permute-start.1 = (bf16[8,4,32,128]{3,2,1,0:T(8,128)(2,1)S(1)}, bf16[8,4,32,128]{3,2,1,0:T(8,128)(2,1)S(1)}, u32[]{:S(2)}, u32[]{:S(2)}) collective-permute-start(bf16[8,4,32,128]{3,2,1,0:T(8,128)(2,1)S(1)} %get-tuple-element.22), channel_id=1, source_target_pairs={{1,0},{2,1},{3,2},{4,3},{5,4},{6,5},{7,6},{8,7},{9,8},{10,9},{11,1... | collective-permute-start | bytes 786440 | tf_op jit(solution)/shard_map/ppermute | solution.py:40
  7.9 4.1 %collective-permute-done.yb_ref = bf16[8,4,32,128]{3,2,1,0:T(8,128)(2,1)S(1)} collective-permute-done((bf16[8,4,32,128]{3,2,1,0:T(8,128)(2,1)S(1)}, bf16[8,4,32,128]{3,2,1,0:T(8,128)(2,1)S(1)}, u32[]{:S(2)}, u32[]{:S(2)}) %collective-permute-start) | collective-permute-done | bytes 262176 | tf_op jit(solution)/shard_map/ppermute | solution.py:39
  12.0 4.0 %collective-permute-done.1.ya_ref = bf16[8,4,32,128]{3,2,1,0:T(8,128)(2,1)S(1)} collective-permute-done((bf16[8,4,32,128]{3,2,1,0:T(8,128)(2,1)S(1)}, bf16[8,4,32,128]{3,2,1,0:T(8,128)(2,1)S(1)}, u32[]{:S(2)}, u32[]{:S(2)}) %collective-permute-start.1) | collective-permute-done | bytes 262176 | tf_op jit(solution)/shard_map/ppermute | solution.py:40
  18.2 3.6 %collective-permute-start.3 = (bf16[4,16,32,128]{3,2,1,0:T(8,128)(2,1)S(1)}, bf16[4,16,32,128]{3,2,1,0:T(8,128)(2,1)S(1)}, u32[]{:S(2)}, u32[]{:S(2)}) collective-permute-start(bf16[4,16,32,128]{3,2,1,0:T(8,128)(2,1)S(1)} %get-tuple-element.20), channel_id=1, source_target_pairs={{16,0},{32,16},{48,32},{64,48},{80,64},{96,80},{112,96},{17,1},{33... | collective-permute-start | bytes 1572872 | tf_op jit(solution)/shard_map/ppermute | solution.py:40
  21.9 4.9 %collective-permute-done.2.xb_ref = bf16[4,16,32,128]{3,2,1,0:T(8,128)(2,1)S(1)} collective-permute-done((bf16[4,16,32,128]{3,2,1,0:T(8,128)(2,1)S(1)}, bf16[4,16,32,128]{3,2,1,0:T(8,128)(2,1)S(1)}, u32[]{:S(2)}, u32[]{:S(2)}) %collective-permute-start.2) | collective-permute-done | bytes 524320 | tf_op jit(solution)/shard_map/ppermute | solution.py:39
  28.5 14.8 %shard_map.68 = (f32[8192,128]{1,0:T(8,128)}, f32[4224,128]{1,0:T(8,128)}) custom-call(s32[64]{0:T(128)S(1)} %add_bitcast_fusion.first_ref, bf16[8,8,32,128]{3,2,1,0:T(8,128)(2,1)S(1)} %fusion.3.own_ref, bf16[8,4,32,128]{3,2,1,0:T(8,128)(2,1)S(1)} %collective-permute-done.yb_ref, bf16[8,4,32,128]{3,2,1,0:T(8,128)(2,1)S(1)} %collective-permute-done.1.ya_ref, ...), custom_call_target="tpu_custom_call" | custom-call | flops 1073741824 | bytes 10485760 | tf_op jit(solution)/shard_map/pallas_call | solution.py:24
  43.3 11.0 %all-to-all-start = ((f32[128,33,1,128]{3,2,1,0:T(1,128)}), f32[128,33,1,128]{3,2,1,0:T(1,128)S(1)}, u32[]{:S(2)}, u32[]{:S(2)}) async-start(f32[128,33,1,128]{3,2,1,0:T(1,128)} %bitcast.2), calls=%async_computation | async-start | bytes 4325376 | tf_op jit(solution)/shard_map/all_to_all | solution.py:343
  57.2 7.0 %shard_map.69.group_ref = s32[32,128]{1,0:T(8,128)S(1)} custom-call(s32[1]{0:T(128)} %bitcast.1.side_ref, s32[256,128]{1,0:T(8,128)S(1)} %reshape.56.members_ref), custom_call_target="tpu_custom_call" | custom-call | flops 536870912 | bytes 131072 | tf_op jit(solution)/shard_map/pallas_call | solution.py:24
  64.2 17.7 %all-to-all-done = f32[128,33,1,128]{3,2,1,0:T(1,128)S(1)} async-done(((f32[128,33,1,128]{3,2,1,0:T(1,128)}), f32[128,33,1,128]{3,2,1,0:T(1,128)S(1)}, u32[]{:S(2)}, u32[]{:S(2)}) %all-to-all-start) | async-done | bytes 2162720 | tf_op jit(solution)/shard_map/all_to_all | solution.py:343
  81.8 12.6 %shard_map.70 = f32[2176,128]{1,0:T(8,128)S(1)} custom-call(s32[32,128]{1,0:T(8,128)S(1)} %shard_map.69.group_ref, f32[4224,128]{1,0:T(8,128)S(1)} %bitcast.19), custom_call_target="tpu_custom_call" | custom-call | flops 4294967296 | bytes 5242880 | tf_op jit(solution)/shard_map/pallas_call | solution.py:24
  95.5 7.5 %all-to-all-start.1 = ((f32[128,17,1,128]{3,2,1,0:T(1,128)}), f32[128,17,1,128]{3,2,1,0:T(1,128)S(1)}, u32[]{:S(2)}, u32[]{:S(2)}) async-start(f32[128,17,1,128]{3,2,1,0:T(1,128)} %bitcast.21), calls=%async_computation.1 | async-start | bytes 2228224 | tf_op jit(solution)/shard_map/all_to_all | solution.py:343
  103.8 15.7 %all-to-all-done.1 = f32[128,17,1,128]{3,2,1,0:T(1,128)S(1)} async-done(((f32[128,17,1,128]{3,2,1,0:T(1,128)}), f32[128,17,1,128]{3,2,1,0:T(1,128)S(1)}, u32[]{:S(2)}, u32[]{:S(2)}) %all-to-all-start.1) | async-done | bytes 1114144 | tf_op jit(solution)/shard_map/all_to_all | solution.py:343
  119.5 27.9 %shard_map.71 = bf16[2304,128]{1,0:T(8,128)(2,1)S(1)} custom-call(f32[16]{0:T(128)S(1)} %dynamic_slice.3.tau_ref, f32[2176,128]{1,0:T(8,128)S(1)} %bitcast.20), custom_call_target="tpu_custom_call" | custom-call | flops 3221225472 | bytes 2097152 | tf_op jit(solution)/shard_map/pallas_call | solution.py:24
  147.4 18.2 %all_to_all.20 = bf16[128,9,2,128]{3,2,1,0:T(2,128)(2,1)S(1)} all-to-all(bf16[128,9,2,128]{3,2,1,0:T(2,128)(2,1)S(1)} %bitcast.23), channel_id=1, replica_groups=mesh['gx'=8,'gy'=16] {'gx','gy'}, dimensions={0} | all-to-all | bytes 1179648 | tf_op jit(solution)/shard_map/all_to_all | solution.py:343
  165.5 6.5 %shard_map.72 = bf16[4352,128]{1,0:T(8,128)(2,1)} custom-call(s32[32,128]{1,0:T(8,128)S(1)} %shard_map.69.group_ref, bf16[2304,128]{1,0:T(8,128)(2,1)S(1)} %bitcast.24), custom_call_target="tpu_custom_call" | custom-call | flops 4294967296 | bytes 3145728 | tf_op jit(solution)/shard_map/pallas_call | solution.py:24
  172.0 7.9 %all-to-all-start.3 = ((bf16[128,17,2,128]{3,2,1,0:T(2,128)(2,1)}), bf16[128,17,2,128]{3,2,1,0:T(2,128)(2,1)S(1)}, u32[]{:S(2)}, u32[]{:S(2)}) async-start(bf16[128,17,2,128]{3,2,1,0:T(2,128)(2,1)} %bitcast.8), calls=%async_computation.3 | async-start | bytes 2228224 | tf_op jit(solution)/shard_map/all_to_all | solution.py:343
  182.5 3.3 %collective-permute-start.9 = (s32[3,64]{1,0:T(4,128)S(1)}, s32[3,64]{1,0:T(4,128)S(1)}, u32[]{:S(2)}, u32[]{:S(2)}) collective-permute-start(s32[3,64]{1,0:T(4,128)S(1)} %broadcast_add_fusion), channel_id=1, source_target_pairs={{1,0},{2,1},{3,2},{4,3},{5,4},{6,5},{7,6},{8,7},{9,8},{10,9},{11,1... | collective-permute-start | bytes 2312 | tf_op jit(solution)/shard_map/ppermute | solution.py:40
  185.8 6.0 %collective-permute-done.8 = s32[3,64]{1,0:T(4,128)S(1)} collective-permute-done((s32[3,64]{1,0:T(4,128)S(1)}, s32[3,64]{1,0:T(4,128)S(1)}, u32[]{:S(2)}, u32[]{:S(2)}) %collective-permute-start.8) | collective-permute-done | bytes 800 | tf_op jit(solution)/shard_map/ppermute | solution.py:39
  194.9 3.6 %collective-permute-start.11 = (s32[3,192]{1,0:T(4,128)S(1)}, s32[3,192]{1,0:T(4,128)S(1)}, u32[]{:S(2)}, u32[]{:S(2)}) collective-permute-start(s32[3,192]{1,0:T(4,128)S(1)} %pad_add_fusion), channel_id=1, source_target_pairs={{16,0},{32,16},{48,32},{64,48},{80,64},{96,80},{112,96},{17,1},{33... | collective-permute-start | bytes 6920 | tf_op jit(solution)/shard_map/ppermute | solution.py:40
  198.5 17.8 %shard_map.73 = (f32[4096,128]{1,0:T(8,128)S(1)}, bf16[2048,128]{1,0:T(8,128)(2,1)S(1)}, bf16[2048,128]{1,0:T(8,128)(2,1)S(1)}) custom-call(s32[64]{0:T(128)S(1)} %add_bitcast_fusion.first_ref, f32[8192,128]{1,0:T(8,128)} %get-tuple-element.7.cells_ref, bf16[4352,128]{1,0:T(8,128)(2,1)S(1)} %bitcast.18), custom_call_target="tpu_custom_call" | custom-call | flops 1073741824 | bytes 10485760 | tf_op jit(solution)/shard_map/pallas_call | solution.py:24
  220.8 4.1 %collective-permute-done.5 = bf16[4,16,32,128]{3,2,1,0:T(8,128)(2,1)S(1)} collective-permute-done((bf16[4,16,32,128]{3,2,1,0:T(8,128)(2,1)S(1)}, bf16[4,16,32,128]{3,2,1,0:T(8,128)(2,1)S(1)}, u32[]{:S(2)}, u32[]{:S(2)}) %collective-permute-start.5) | collective-permute-done | bytes 524320 | tf_op jit(solution)/shard_map/ppermute | solution.py:40
  225.1 3.6 %collective-permute-done.4 = bf16[4,16,32,128]{3,2,1,0:T(8,128)(2,1)S(1)} collective-permute-done((bf16[4,16,32,128]{3,2,1,0:T(8,128)(2,1)S(1)}, bf16[4,16,32,128]{3,2,1,0:T(8,128)(2,1)S(1)}, u32[]{:S(2)}, u32[]{:S(2)}) %collective-permute-start.4) | collective-permute-done | bytes 524320 | tf_op jit(solution)/shard_map/ppermute | solution.py:39
  229.8 5.5 %collective-permute-start.6 = (bf16[8,4,32,128]{3,2,1,0:T(8,128)(2,1)}, bf16[8,4,32,128]{3,2,1,0:T(8,128)(2,1)S(1)}, u32[]{:S(2)}, u32[]{:S(2)}) collective-permute-start(bf16[8,4,32,128]{3,2,1,0:T(8,128)(2,1)} %get-tuple-element.18), channel_id=1, source_target_pairs={{0,1},{1,2},{2,3},{3,4},{4,5},{5,6},{6,7},{7,8},{8,9},{9,10},{10,1... | collective-permute-start | bytes 786440 | tf_op jit(solution)/shard_map/ppermute | solution.py:39
  240.4 5.9 %collective-permute-done.7 = bf16[8,4,32,128]{3,2,1,0:T(8,128)(2,1)S(1)} collective-permute-done((bf16[8,4,32,128]{3,2,1,0:T(8,128)(2,1)S(1)}, bf16[8,4,32,128]{3,2,1,0:T(8,128)(2,1)S(1)}, u32[]{:S(2)}, u32[]{:S(2)}) %collective-permute-start.7) | collective-permute-done | bytes 262176 | tf_op jit(solution)/shard_map/ppermute | solution.py:40
  (45 shorter events, 30.3 us)
Async XLA Ops:
  2.0 9.9 %collective-permute-start = (bf16[8,4,32,128]{3,2,1,0:T(8,128)(2,1)S(1)}, bf16[8,4,32,128]{3,2,1,0:T(8,128)(2,1)S(1)}, u32[]{:S(2)}, u32[]{:S(2)}) collective-permute-start(bf16[8,4,32,128]{3,2,1,0:T(8,128)(2,1)S(1)} %get-tuple-element.23), channel_id=1, source_target_pairs={{0,1},{1,2},{2,3},{3,4},{4,5},{5,6},{6,7},{7,8},{8,9},{9,10},{10,1... | collective-permute-start | bytes 786440 | tf_op jit(solution)/shard_map/ppermute | solution.py:39
  4.1 17.8 %copy-start.4 = (s32[3,64]{1,0:T(4,128)S(1)}, s32[3,64]{1,0:T(4,128)}, u32[]{:S(2)}) copy-start(s32[3,64]{1,0:T(4,128)} %param.7) | copy-start | bytes 2308
  4.1 11.9 %collective-permute-start.1 = (bf16[8,4,32,128]{3,2,1,0:T(8,128)(2,1)S(1)}, bf16[8,4,32,128]{3,2,1,0:T(8,128)(2,1)S(1)}, u32[]{:S(2)}, u32[]{:S(2)}) collective-permute-start(bf16[8,4,32,128]{3,2,1,0:T(8,128)(2,1)S(1)} %get-tuple-element.22), channel_id=1, source_target_pairs={{1,0},{2,1},{3,2},{4,3},{5,4},{6,5},{7,6},{8,7},{9,8},{10,9},{11,1... | collective-permute-start | bytes 786440 | tf_op jit(solution)/shard_map/ppermute | solution.py:40
  16.2 10.5 %collective-permute-start.2 = (bf16[4,16,32,128]{3,2,1,0:T(8,128)(2,1)S(1)}, bf16[4,16,32,128]{3,2,1,0:T(8,128)(2,1)S(1)}, u32[]{:S(2)}, u32[]{:S(2)}) collective-permute-start(bf16[4,16,32,128]{3,2,1,0:T(8,128)(2,1)S(1)} %get-tuple-element.21), channel_id=1, source_target_pairs={{0,16},{16,32},{32,48},{48,64},{64,80},{80,96},{96,112},{1,17},{17... | collective-permute-start | bytes 1572872 | tf_op jit(solution)/shard_map/ppermute | solution.py:39
  18.2 10.3 %collective-permute-start.3 = (bf16[4,16,32,128]{3,2,1,0:T(8,128)(2,1)S(1)}, bf16[4,16,32,128]{3,2,1,0:T(8,128)(2,1)S(1)}, u32[]{:S(2)}, u32[]{:S(2)}) collective-permute-start(bf16[4,16,32,128]{3,2,1,0:T(8,128)(2,1)S(1)} %get-tuple-element.20), channel_id=1, source_target_pairs={{16,0},{32,16},{48,32},{64,48},{80,64},{96,80},{112,96},{17,1},{33... | collective-permute-start | bytes 1572872 | tf_op jit(solution)/shard_map/ppermute | solution.py:40
  43.3 11.0 %copy-start.3 = (s32[2048,16]{0,1:T(8,128)S(1)}, s32[2048,16]{0,1:T(8,128)}, u32[]{:S(2)}) copy-start(s32[2048,16]{0,1:T(8,128)} %param.8) | copy-start | bytes 393220
  43.3 38.5 %all-to-all-start = ((f32[128,33,1,128]{3,2,1,0:T(1,128)}), f32[128,33,1,128]{3,2,1,0:T(1,128)S(1)}, u32[]{:S(2)}, u32[]{:S(2)}) async-start(f32[128,33,1,128]{3,2,1,0:T(1,128)} %bitcast.2), calls=%async_computation | async-start | bytes 4325376 | tf_op jit(solution)/shard_map/all_to_all | solution.py:343
  94.4 1.1 copy-start
  95.5 24.0 %all-to-all-start.1 = ((f32[128,17,1,128]{3,2,1,0:T(1,128)}), f32[128,17,1,128]{3,2,1,0:T(1,128)S(1)}, u32[]{:S(2)}, u32[]{:S(2)}) async-start(f32[128,17,1,128]{3,2,1,0:T(1,128)} %bitcast.21), calls=%async_computation.1 | async-start | bytes 2228224 | tf_op jit(solution)/shard_map/all_to_all | solution.py:343
  172.0 26.5 %all-to-all-start.3 = ((bf16[128,17,2,128]{3,2,1,0:T(2,128)(2,1)}), bf16[128,17,2,128]{3,2,1,0:T(2,128)(2,1)S(1)}, u32[]{:S(2)}, u32[]{:S(2)}) async-start(bf16[128,17,2,128]{3,2,1,0:T(2,128)(2,1)} %bitcast.8), calls=%async_computation.3 | async-start | bytes 2228224 | tf_op jit(solution)/shard_map/all_to_all | solution.py:343
  179.9 11.8 %collective-permute-start.8 = (s32[3,64]{1,0:T(4,128)S(1)}, s32[3,64]{1,0:T(4,128)S(1)}, u32[]{:S(2)}, u32[]{:S(2)}) collective-permute-start(s32[3,64]{1,0:T(4,128)S(1)} %broadcast_add_fusion), channel_id=1, source_target_pairs={{0,1},{1,2},{2,3},{3,4},{4,5},{5,6},{6,7},{7,8},{8,9},{9,10},{10,1... | collective-permute-start | bytes 2312 | tf_op jit(solution)/shard_map/ppermute | solution.py:39
  182.5 10.4 %collective-permute-start.9 = (s32[3,64]{1,0:T(4,128)S(1)}, s32[3,64]{1,0:T(4,128)S(1)}, u32[]{:S(2)}, u32[]{:S(2)}) collective-permute-start(s32[3,64]{1,0:T(4,128)S(1)} %broadcast_add_fusion), channel_id=1, source_target_pairs={{1,0},{2,1},{3,2},{4,3},{5,4},{6,5},{7,6},{8,7},{9,8},{10,9},{11,1... | collective-permute-start | bytes 2312 | tf_op jit(solution)/shard_map/ppermute | solution.py:40
  193.0 44.4 %collective-permute-start.10 = (s32[3,192]{1,0:T(4,128)S(1)}, s32[3,192]{1,0:T(4,128)S(1)}, u32[]{:S(2)}, u32[]{:S(2)}) collective-permute-start(s32[3,192]{1,0:T(4,128)S(1)} %pad_add_fusion), channel_id=1, source_target_pairs={{0,16},{16,32},{32,48},{48,64},{64,80},{80,96},{96,112},{1,17},{17... | collective-permute-start | bytes 6920 | tf_op jit(solution)/shard_map/ppermute | solution.py:39
  194.9 42.5 %collective-permute-start.11 = (s32[3,192]{1,0:T(4,128)S(1)}, s32[3,192]{1,0:T(4,128)S(1)}, u32[]{:S(2)}, u32[]{:S(2)}) collective-permute-start(s32[3,192]{1,0:T(4,128)S(1)} %pad_add_fusion), channel_id=1, source_target_pairs={{16,0},{32,16},{48,32},{64,48},{80,64},{96,80},{112,96},{17,1},{33... | collective-permute-start | bytes 6920 | tf_op jit(solution)/shard_map/ppermute | solution.py:40
  216.3 8.6 %collective-permute-start.5 = (bf16[4,16,32,128]{3,2,1,0:T(8,128)(2,1)S(1)}, bf16[4,16,32,128]{3,2,1,0:T(8,128)(2,1)S(1)}, u32[]{:S(2)}, u32[]{:S(2)}) collective-permute-start(bf16[4,16,32,128]{3,2,1,0:T(8,128)(2,1)S(1)} %bitcast.26), channel_id=1, source_target_pairs={{16,0},{32,16},{48,32},{64,48},{80,64},{96,80},{112,96},{17,1},{33... | collective-permute-start | bytes 1572872 | tf_op jit(solution)/shard_map/ppermute | solution.py:40
  218.3 10.5 %collective-permute-start.4 = (bf16[4,16,32,128]{3,2,1,0:T(8,128)(2,1)S(1)}, bf16[4,16,32,128]{3,2,1,0:T(8,128)(2,1)S(1)}, u32[]{:S(2)}, u32[]{:S(2)}) collective-permute-start(bf16[4,16,32,128]{3,2,1,0:T(8,128)(2,1)S(1)} %bitcast.25), channel_id=1, source_target_pairs={{0,16},{16,32},{32,48},{48,64},{64,80},{80,96},{96,112},{1,17},{17... | collective-permute-start | bytes 1572872 | tf_op jit(solution)/shard_map/ppermute | solution.py:39
  229.8 10.6 %collective-permute-start.6 = (bf16[8,4,32,128]{3,2,1,0:T(8,128)(2,1)}, bf16[8,4,32,128]{3,2,1,0:T(8,128)(2,1)S(1)}, u32[]{:S(2)}, u32[]{:S(2)}) collective-permute-start(bf16[8,4,32,128]{3,2,1,0:T(8,128)(2,1)} %get-tuple-element.18), channel_id=1, source_target_pairs={{0,1},{1,2},{2,3},{3,4},{4,5},{5,6},{6,7},{7,8},{8,9},{9,10},{10,1... | collective-permute-start | bytes 786440 | tf_op jit(solution)/shard_map/ppermute | solution.py:39
  235.4 11.0 %collective-permute-start.7 = (bf16[8,4,32,128]{3,2,1,0:T(8,128)(2,1)S(1)}, bf16[8,4,32,128]{3,2,1,0:T(8,128)(2,1)S(1)}, u32[]{:S(2)}, u32[]{:S(2)}) collective-permute-start(bf16[8,4,32,128]{3,2,1,0:T(8,128)(2,1)S(1)} %get-tuple-element.19), channel_id=1, source_target_pairs={{1,0},{2,1},{3,2},{4,3},{5,4},{6,5},{7,6},{8,7},{9,8},{10,9},{11,1... | collective-permute-start | bytes 786440 | tf_op jit(solution)/shard_map/ppermute | solution.py:40
  240.0 6.5 %copy-start.1 = (bf16[8,8,32,128]{3,2,1,0:T(8,128)(2,1)S(1)}, bf16[8,8,32,128]{3,2,1,0:T(8,128)(2,1)}, u32[]{:S(2)}) copy-start(bf16[8,8,32,128]{3,2,1,0:T(8,128)(2,1)} %param.6) | copy-start | bytes 1572868
  240.0 6.5 %copy-start.2 = (bf16[8,8,32,128]{3,2,1,0:T(8,128)(2,1)S(1)}, bf16[8,8,32,128]{3,2,1,0:T(8,128)(2,1)}, u32[]{:S(2)}) copy-start(bf16[8,8,32,128]{3,2,1,0:T(8,128)(2,1)} %param.5) | copy-start | bytes 1572868

commit v3 on v2

--- a/solution.py
+++ b/solution.py
@@ -54,12 +54,12 @@
     return packed, jnp.where(low_diagonal, bottom, 0.0)
 
 
-def unpack_symmetric(packed, diagonal, masks):
+def unpack_symmetric(packed, diagonal, masks, dtype):
     moved, top_diagonal, low_diagonal = masks
     top = jnp.where(moved, 0.0, jnp.where(top_diagonal, 0.5 * packed, packed))
     bottom = pltpu.roll(jnp.where(moved, packed, 0.0), 64, axis=1)
     bottom = bottom + jnp.where(low_diagonal, 0.5 * diagonal, 0.0)
-    half = jnp.concatenate([top, bottom], 0)
+    half = jnp.concatenate([top, bottom], 0).astype(dtype)
     return half + half.T
 
 
@@ -153,13 +153,13 @@
         diag_ref[pl.ds(p, 1), :] = jnp.sum(rest, axis=0, keepdims=True)
         return 0
 
-    lax.fori_loop(0, 64, patch, 0, unroll=2)
+    lax.fori_loop(0, 64, patch, 0, unroll=8)
     turned = diag_ref[...].T[64:]
     out_ref[pl.ds(32, 64, stride=33), :] = turned
     out_ref[pl.ds(64 * 33 + 32, 64, stride=33), :] = pltpu.roll(turned, 96, axis=1)
 
 
-def group_sum_body(group_ref, rows_ref, out_ref, limbs_ref, hot_ref, diag_ref):
+def group_sum_body(group_ref, rows_ref, out_ref, limbs_ref):
     def split(i, _):
         value = rows_ref[pl.ds(i * 33, 32), :]
         high = value.astype(BF16)
@@ -168,35 +168,53 @@
         limbs_ref[pl.ds(row, 32), 128:256] = (value - high.astype(F32)).astype(BF16)
         return 0
 
-    lax.fori_loop(0, 128, split, 0, unroll=4)
+    lax.fori_loop(0, 128, split, 0, unroll=8)
+    one = jnp.ones((128, 128), BF16)
+    zero = jnp.zeros((128, 128), BF16)
+    sub = lax.broadcasted_iota(jnp.int32, (128, 128), 0)
+    sub16 = sub.astype(F32).astype(BF16)
+
     used = lax.broadcasted_iota(jnp.int32, (32, 128), 1) < 32
     diagonal = jnp.zeros((32, 128), F32)
     for c in range(4):
         part = jnp.where(used, rows_ref[pl.ds(32 + 33 * c, 32, stride=132), :], 0.0)
         diagonal = diagonal + (pltpu.roll(part, 32 * c, axis=1) if c else part)
-    diag_ref[...] = diagonal
-    sub = lax.broadcasted_iota(jnp.int32, (256, 128), 0)
-    eye = lax.broadcasted_iota(jnp.int32, (16, 128), 0) == lax.broadcasted_iota(
-        jnp.int32, (16, 128), 1
-    )
+    group = group_ref[...]
+    owner, place = group >> 4, (group & 15).astype(F32).astype(BF16)
+    left, right = [], []
+    for t in range(32):
+        value = jnp.where(sub == owner[t : t + 1, :], diagonal[t : t + 1, :], 0.0)
+        high = value.astype(BF16)
+        left.append(jnp.concatenate([high, (value - high.astype(F32)).astype(BF16)], 0))
+        spot = jnp.broadcast_to(place[t : t + 1, :], (128, 128))
+        right.append(jnp.where(sub16 == spot, one, zero))
+    extra = lax.dot_general(
+        jnp.concatenate(left, 1),
+        jnp.concatenate(right, 1),
+        (((1,), (1,)), ((), ())),
+        preferred_element_type=F32,
+    )
+    out_ref[pl.ds(16, 128, stride=17), :] = extra[:128] + extra[128:]
 
     def chunk(i, _):
-        base = i * 256
-        picked = jnp.zeros((256, 128), F32)
+        local = group_ref[...] - i * 256
+        local = jnp.where((local >= 0) & (local < 256), local, 512).astype(F32).astype(BF16)
+        hot = []
         for t in range(32):
-            on = sub == group_ref[t : t + 1, :] - base
-            hot_ref[:, t * 128 : (t + 1) * 128] = jnp.where(on, 1.0, 0.0).astype(BF16)
-            picked = picked + jnp.where(on, diag_ref[t : t + 1, :], 0.0)
-        total = jnp.dot(hot_ref[...], limbs_ref[...], preferred_element_type=F32)
+            entry = jnp.broadcast_to(local[t : t + 1, :], (128, 128))
+            hot.append(
+                jnp.concatenate(
+                    [
+                        jnp.where(sub16 == entry, one, zero),
+                        jnp.where(sub16 + jnp.asarray(128, BF16) == entry, one, zero),
+                    ],
+                    0,
+                )
+            )
+        total = jnp.dot(jnp.concatenate(hot, 1), limbs_ref[...], preferred_element_type=F32)
         total = total[:, :128] + total[:, 128:]
-        picked = jnp.sum(picked, axis=1, keepdims=True)
         for d in range(16):
-            row = (i * 16 + d) * 17
-            part = slice(d * 16, d * 16 + 16)
-            out_ref[pl.ds(row, 16), :] = total[part]
-            out_ref[pl.ds(row + 16, 1), :] = jnp.sum(
-                jnp.where(eye, picked[part], 0.0), axis=0, keepdims=True
-            )
+            out_ref[pl.ds((i * 16 + d) * 17, 16), :] = total[d * 16 : d * 16 + 16]
         return 0
 
     lax.fori_loop(0, 8, chunk, 0)
@@ -210,53 +228,52 @@
     masks = packed_masks()
     half = 64 * 17
     diagonals = rows_ref[pl.ds(16, 64, stride=17), :] + rows_ref[pl.ds(half + 16, 64, stride=17), :]
+    diagonals = jnp.concatenate([jnp.zeros((64, 128), F32), diagonals], 0).T
     for g in range(per):
         packed = rows_ref[pl.ds(g, 64, stride=17), :] + rows_ref[pl.ds(half + g, 64, stride=17), :]
-        sys_ref[g] = unpack_symmetric(packed, diagonals[:, g : g + 1], masks) + tau_ref[g] * eye
-    panel_sub = lax.broadcasted_iota(jnp.int32, (per, NB, 128), 1)
-    panel_lane = lax.broadcasted_iota(jnp.int32, (per, NB, 128), 2)
+        sys_ref[g] = unpack_symmetric(packed, diagonals[g : g + 1], masks, F32) + tau_ref[g] * eye
+    lane16 = lax.broadcasted_iota(jnp.int32, (NB, 128), 1)
+    sub16 = lax.broadcasted_iota(jnp.int32, (NB, 128), 0)
+    same = (row_id >> 4) == (lane_id >> 4)
 
     def block(b, _):
         start = pl.multiple_of(b * NB, NB)
-        panel = sys_ref[:, pl.ds(start, NB), :]
-        panel = pltpu.roll(panel.reshape(per * NB, 128), 128 - start, axis=1).reshape(per, NB, 128)
-        for j in range(NB):
-            column = panel[:, :, j : j + 1]
-            pivot_row = panel[:, j : j + 1, :]
-            pivot = 1.0 / panel[:, j : j + 1, j : j + 1]
-            scaled = jnp.where(panel_lane[:, j : j + 1, :] == j, pivot, pivot_row * pivot)
-            cleared = jnp.where(panel_lane == j, 0.0, panel)
-            panel = jnp.where(panel_sub == j, scaled, cleared - column * scaled)
-        panel = pltpu.roll(panel.reshape(per * NB, 128), start, axis=1).reshape(per, NB, 128)
+        panels = [sys_ref[g, pl.ds(start, NB), :] for g in range(per)]
+        pivots = []
+        for h in range(2):
+            joined = jnp.zeros((NB, 128), F32)
+            for k in range(8):
+                moved = pltpu.roll(panels[h * 8 + k], lax.rem(128 + k * NB - start, 128), axis=1)
+                joined = jnp.where((lane16 >> 4) == k, moved, joined)
+            pivots.append(joined)
+        pivots = invert_blocks(jnp.concatenate(pivots, 0))
+        in_block = (lane16 >= start) & (lane16 < start + NB)
+        identity = jnp.where(lane16 - start == sub16, 1.0, 0.0)
         in_lanes = (lane_id >= start) & (lane_id < start + NB)
         in_rows = (row_id >= start) & (row_id < start + NB)
+        scaled = []
+        for h in range(2):
+            left = jnp.where(same, jnp.concatenate([pivots[h * NB : (h + 1) * NB]] * 8, 0), 0.0)
+            right = jnp.concatenate(
+                [jnp.where(in_block, identity, panels[h * 8 + k]) for k in range(8)], 0
+            )
+            product = wide_product(left, right)
+            scaled += [product[k * NB : (k + 1) * NB] for k in range(8)]
         for g in range(per):
             matrix = sys_ref[g]
-            wide = jnp.where(in_rows, jnp.concatenate([panel[g]] * (128 // NB), 0), 0.0)
-            w0, w1, w2 = limbs(wide)
-            a0, a1, a2 = limbs(matrix)
-            main = jnp.dot(
-                jnp.concatenate([a0, a1], 1),
-                jnp.concatenate([jnp.concatenate([w0, w0], 0), jnp.concatenate([w1, w1], 0)], 1),
-                preferred_element_type=F32,
-            )
-            small = jnp.dot(
-                jnp.concatenate([a0, a2], 1),
-                jnp.concatenate([w2, w0], 0),
-                preferred_element_type=F32,
-            )
-            update = main[:, :128] + (main[:, 128:] + small)
+            wide = jnp.where(in_rows, jnp.concatenate([scaled[g]] * (128 // NB), 0), 0.0)
+            update = wide_product(matrix, wide)
             sys_ref[g] = jnp.where(in_rows, wide, jnp.where(in_lanes, 0.0, matrix) - update)
         return 0
 
     lax.fori_loop(0, 128 // NB, block, 0)
-    place = lax.broadcasted_iota(jnp.int32, (64, 128), 1)
-    extra = jnp.zeros((64, 128), F32)
+    extra = []
     for g in range(per):
         packed, rest = pack_symmetric(eye - tau_ref[g] * sys_ref[g], masks)
         stage_ref[pl.ds(g, 64, stride=18), :] = packed
-        extra = jnp.where(place == g, jnp.sum(rest, axis=1, keepdims=True), extra)
-    stage_ref[pl.ds(16, 64, stride=18), :] = extra
+        extra.append(jnp.sum(rest, axis=0, keepdims=True))
+    extra = jnp.concatenate(extra + [jnp.zeros((128 - per, 128), F32)], 0)
+    stage_ref[pl.ds(16, 64, stride=18), :] = extra.T[64:]
     stage_ref[pl.ds(17, 64, stride=18), :] = jnp.zeros((64, 128), F32)
     result = stage_ref[...].astype(BF16)
     out_ref[0:1152, :] = result
@@ -270,68 +287,167 @@
     return first, second, (rest - second.astype(F32)).astype(BF16)
 
 
+def wide_product(left, right):
+    a0, a1, a2 = limbs(left)
+    w0, w1, w2 = limbs(right)
+    main = jnp.dot(
+        jnp.concatenate([a0, a1], 1),
+        jnp.concatenate([jnp.concatenate([w0, w0], 0), jnp.concatenate([w1, w1], 0)], 1),
+        preferred_element_type=F32,
+    )
+    small = jnp.dot(
+        jnp.concatenate([a0, a2], 1), jnp.concatenate([w2, w0], 0), preferred_element_type=F32
+    )
+    return main[:, :128] + (main[:, 128:] + small)
+
+
+def invert_blocks(value):
+    shape = value.shape
+    lane = lax.broadcasted_iota(jnp.int32, shape, 1)
+    sub = lax.broadcasted_iota(jnp.int32, shape, 0) & (NB - 1)
+    within = lane & (NB - 1)
+    segment = lane - within
+
+    def spread(x, row):
+        parts = [jnp.broadcast_to(x[h * NB + row : h * NB + row + 1], (NB, 128)) for h in range(2)]
+        return jnp.concatenate(parts, 0)
+
+    for j in range(0, NB, 2):
+        c0 = jnp.take_along_axis(value, segment + j, axis=1, mode="promise_in_bounds")
+        c1 = jnp.take_along_axis(value, segment + (j + 1), axis=1, mode="promise_in_bounds")
+        at0, at1 = within == j, within == j + 1
+        r0, r1 = spread(value, j), spread(value, j + 1)
+        inverse = 1.0 / spread(c0, j)
+        ratio = spread(c1, j) * inverse
+        below = spread(c0, j + 1)
+        s0 = jnp.where(at0, inverse, r0 * inverse)
+        pivot = 1.0 / (spread(c1, j + 1) - below * ratio)
+        rest = jnp.where(at0, 0.0, r1) - below * s0
+        s1 = jnp.where(at1, pivot, rest * pivot)
+        s0 = jnp.where(at1, 0.0, s0) - ratio * s1
+        kept = jnp.where(at0 | at1, 0.0, value)
+        c1 = c1 - c0 * ratio
+        first = jnp.where(at0, inverse, jnp.where(at1, 0.0, r0 * inverse))
+        value = jnp.where(
+            sub == j, s0, jnp.where(sub == j + 1, s1, (kept - c0 * first) - c1 * s1)
+        )
+    return value
+
+
 def expand_body(group_ref, rows_ref, out_ref, turned_ref, wide_ref, table_ref, stage_ref):
     turned_ref[...] = group_ref[...].astype(F32).T.astype(jnp.int32)
     wide_ref[...] = rows_ref[...].astype(F32)
-    eye = lax.broadcasted_iota(jnp.int32, (16, 128), 0) == lax.broadcasted_iota(
-        jnp.int32, (16, 128), 1
-    )
-
-    def gather(d, _):
-        row = pl.multiple_of(d * 16, 16)
-        table_ref[pl.ds(row, 16), 0:128] = wide_ref[pl.ds(d * 18, 16), :].astype(BF16)
-        extra = wide_ref[pl.ds(d * 18 + 16, 1), :]
-        table_ref[pl.ds(row, 16), 128:256] = jnp.where(eye, extra, 0.0).astype(BF16)
-        return 0
-
-    lax.fori_loop(0, 128, gather, 0, unroll=4)
-    lane = lax.broadcasted_iota(jnp.int32, (128, 2048), 1)
+    for j in range(4):
+
+        def gather(d, _):
+            value = wide_ref[pl.ds((d + 32 * j) * 18, 16), :].astype(BF16)
+            table_ref[pl.ds(pl.multiple_of(d * 16, 16), 16), j * 128 : (j + 1) * 128] = value
+            return 0
+
+        lax.fori_loop(0, 32, gather, 0, unroll=8)
+    extras = wide_ref[pl.ds(16, 128, stride=18), :].astype(BF16)
+    lane = lax.broadcasted_iota(jnp.int32, (128, 128), 1)
+    lane16 = lane.astype(F32).astype(BF16)
+    zero = jnp.zeros((128, 128), BF16)
+    one = jnp.ones((128, 128), BF16)
     eye = lax.broadcasted_iota(jnp.int32, (32, 128), 0) == lax.broadcasted_iota(
         jnp.int32, (32, 128), 1
     )
-    for t in range(32):
-        hot = jnp.where(lane == turned_ref[:, t : t + 1], 1.0, 0.0).astype(BF16)
-        both = jnp.dot(hot, table_ref[...], preferred_element_type=F32)
-        value = jnp.sum(both[:, 128:], axis=1, keepdims=True)
-        for s in range(4):
-            row = (t * 4 + s) * 34
-            part = slice(s * 32, s * 32 + 32)
-            stage_ref[row : row + 32, :] = both[part, :128]
-            stage_ref[row + 32 : row + 33, :] = jnp.sum(
-                jnp.where(eye, value[part], 0.0), axis=0, keepdims=True
+    stage_ref[pl.ds(33, 128, stride=34), :] = jnp.zeros((128, 128), F32)
+    for u in range(8):
+        groups, hot, owners = [], [], []
+        for v in range(4):
+            group = jnp.broadcast_to(turned_ref[:, u * 4 + v : u * 4 + v + 1], (128, 128))
+            groups.append(group)
+            low = jnp.where((group & 127).astype(F32).astype(BF16) == lane16, one, zero)
+            high = ((group >> 7) & 3).astype(F32).astype(BF16)
+            hot.append(
+                jnp.concatenate(
+                    [jnp.where(high == jnp.full((128, 128), c, BF16), low, zero) for c in range(4)],
+                    1,
+                )
             )
-            stage_ref[row + 33 : row + 34, :] = jnp.zeros((1, 128), F32)
+            owners.append(jnp.where((group >> 4).astype(F32).astype(BF16) == lane16, one, zero))
+        wide = jnp.dot(jnp.concatenate(hot, 0), table_ref[...], preferred_element_type=F32)
+        spots = jnp.dot(jnp.concatenate(owners, 0), extras, preferred_element_type=F32)
+        for v in range(4):
+            group = groups[v]
+            rows = slice(v * 128, (v + 1) * 128)
+            quarter = group >> 9
+            piece = wide[rows, 384:512]
+            for j in (2, 1, 0):
+                piece = jnp.where(quarter == j, wide[rows, j * 128 : (j + 1) * 128], piece)
+            spot = jnp.where(lane == (group & 15), spots[rows], 0.0)
+            value = jnp.sum(spot, axis=1, keepdims=True)
+            for k in range(4):
+                row = ((u * 4 + v) * 4 + k) * 34
+                part = slice(k * 32, k * 32 + 32)
+                stage_ref[row : row + 32, :] = piece[part]
+                stage_ref[row + 32 : row + 33, :] = jnp.sum(
+                    jnp.where(eye, value[part], 0.0), axis=0, keepdims=True
+                )
     out_ref[...] = stage_ref[...].astype(BF16)
 
 
-def apply_body(first_ref, cells_ref, rows_ref, inner_ref, low_ref, high_ref, wide_ref, sum_ref):
+def apply_body(
+    first_ref,
+    cells_ref,
+    rows_ref,
+    inner_ref,
+    low_ref,
+    high_ref,
+    wide_ref,
+    sum_ref,
+    factor_ref,
+    even_ref,
+    odd_ref,
+    diag_ref,
+):
     wide_ref[...] = rows_ref[...].astype(F32)
-    sum_ref[...] = jnp.zeros_like(sum_ref)
     masks = packed_masks()
-    lane = lax.broadcasted_iota(jnp.int32, (64, 128), 1)
-
-    def product(p):
+    used = lax.broadcasted_iota(jnp.int32, (64, 128), 1) < 32
+    first_side = jnp.where(used, wide_ref[pl.ds(32, 64, stride=34), :], 0.0)
+    last_side = jnp.where(used, wide_ref[pl.ds(64 * 34 + 32, 64, stride=34), :], 0.0)
+    diagonals = first_side + pltpu.roll(last_side, 32, axis=1)
+    diag_ref[...] = jnp.concatenate([jnp.zeros((64, 128), F32), diagonals], 0).T
+
+    def unpack(p, _):
         side = p // 32
-        slot = p - side * 32
-        base = side * (64 * 34)
-        packed = wide_ref[pl.ds(base + slot, 64, stride=34), :]
-        diagonals = wide_ref[pl.ds(base + 32, 64, stride=34), :]
-        diagonal = jnp.sum(jnp.where(lane == slot, diagonals, 0.0), axis=1, keepdims=True)
-        factor = unpack_symmetric(packed, diagonal, masks).astype(BF16)
-        values = load_patch(cells_ref, first_ref[p]).astype(BF16)
-        return jnp.dot(values, factor, preferred_element_type=F32)
-
-    def pair(i, _):
-        for p, result in [(2 * i + k, product(2 * i + k)) for k in range(2)]:
-            first = first_ref[p]
+        packed = wide_ref[pl.ds(side * (64 * 34 - 32) + p, 64, stride=34), :]
+        sum_ref[pl.ds(pl.multiple_of(p * 128, 128), 128), :] = jnp.zeros((128, 128), F32)
+        factor_ref[p] = unpack_symmetric(packed, diag_ref[pl.ds(p, 1), :], masks, BF16)
+        return 0
+
+    lax.fori_loop(0, 64, unpack, 0, unroll=8)
+    odd_ref[...] = jnp.zeros_like(odd_ref)
+    count = 4
+
+    def multiply(p, ref):
+        for k in range(count):
+            values = load_patch(cells_ref, first_ref[p + k]).astype(BF16)
+            ref[k * 512 : (k + 1) * 512, :] = jnp.dot(
+                values, factor_ref[p + k], preferred_element_type=F32
+            )
+
+    def accumulate(p, ref):
+        for k in range(count):
+            first = first_ref[p + k]
             for a in range(PATCH):
                 for b in range(PATCH):
                     at = pl.ds(first + (a * 16 + b) * 32, PATCH)
-                    row = (a * PATCH + b) * PATCH
-                    sum_ref[at, :] += result[row : row + PATCH]
-        return 0
-
-    lax.fori_loop(0, 32, pair, 0)
+                    row = k * 512 + (a * PATCH + b) * PATCH
+                    sum_ref[at, :] += ref[row : row + PATCH, :]
+
+    def several(i, _):
+        p = i * (2 * count)
+        multiply(p, even_ref)
+        accumulate(jnp.maximum(p - count, 0), odd_ref)
+        multiply(p + count, odd_ref)
+        accumulate(p, even_ref)
+        return 0
+
+    lax.fori_loop(0, 64 // (2 * count), several, 0)
+    accumulate(64 - count, odd_ref)
     low_ref[...] = sum_ref[0:2048, :].astype(BF16)
     inner_ref[...] = sum_ref[2048:6144, :]
     high_ref[...] = sum_ref[6144:8192, :].astype(BF16)
@@ -405,11 +521,7 @@
         jax.ShapeDtypeStruct((128 * 17, 128), F32),
         table,
         rows,
-        scratch=[
-            pltpu.VMEM((4096, 256), BF16),
-            pltpu.VMEM((256, 4096), BF16),
-            pltpu.VMEM((32, 128), F32),
-        ],
+        scratch=[pltpu.VMEM((4096, 256), BF16)],
         flops=2 * 2048 * 4096 * 256,
         nbytes=5 << 20,
     )
@@ -434,7 +546,7 @@
         scratch=[
             pltpu.VMEM((128, 32), jnp.int32),
             pltpu.VMEM((128 * 18, 128), F32),
-            pltpu.VMEM((2048, 256), BF16),
+            pltpu.VMEM((512, 512), BF16),
             pltpu.VMEM((128 * 34, 128), F32),
         ],
         flops=2 * 2048 * 4096 * 256,
@@ -449,7 +561,14 @@
         cells,
         patch_factors,
         specs=[SMEM, VMEM, VMEM],
-        scratch=[pltpu.VMEM((128 * 34, 128), F32), pltpu.VMEM((8192, 128), F32)],
+        scratch=[
+            pltpu.VMEM((128 * 34, 128), F32),
+            pltpu.VMEM((8192, 128), F32),
+            pltpu.VMEM((64, 128, 128), BF16),
+            pltpu.VMEM((2048, 128), F32),
+            pltpu.VMEM((2048, 128), F32),
+            pltpu.VMEM((128, 128), F32),
+        ],
         flops=2 * 64 * 512 * 128 * 128,
         nbytes=10 << 20,
     )

time: 249 us -> 218 us (0.88)
  Pallas kernels: 89 us -> 57.5 us
    pallas_call x7, Pallas kernels: 89 us -> 57.5 us  [call(): pl.pallas_call(body, out_shape=out_shape, in_specs=specs or [VMEM] * len(...]
  transfers between devices with their start and end apart: 15 -> 15, of which waited for: 12 -> 12; matrix products, arithmetic and copies ran while one was open for 2% -> 2% of each run, Pallas kernels for 11% -> 10%
where the time goes in v3:
time: 218 us; the launch traced here: 217 us
  waiting for transfers between devices  69.3 us (32%)
  starting transfers between devices  61.2 us (28%)
  Pallas kernels  57.5 us (26%)
  blocking collectives  18.2 us (8%)
  local copies, waits for them, and re-layouts  5.79 us (3%)
  other arithmetic  4.07 us (2%)
    pallas_call x7, Pallas kernels, call(): pl.pallas_call(body, out_shape=out_shape, in_specs=specs or [VMEM] * len(...  57.5 us
    all_to_all x3, waiting for transfers between devices, exchange(): rows = lax.all_to_all(rows, BOTH, split_axis=0, concat_axis=0, tiled=True)  33.4 us
    all_to_all x3, starting transfers between devices, exchange(): rows = lax.all_to_all(rows, BOTH, split_axis=0, concat_axis=0, tiled=True)  26.4 us
    ppermute x6, waiting for transfers between devices, neighbors(): before = lax.ppermute(last, axis, up)  18.9 us
    ppermute x6, starting transfers between devices, neighbors(): after = lax.ppermute(first, axis, down)  18.4 us
    all_to_all x1, blocking collectives, exchange(): rows = lax.all_to_all(rows, BOTH, split_axis=0, concat_axis=0, tiled=True)  18.2 us
    ppermute x6, waiting for transfers between devices, neighbors(): after = lax.ppermute(first, axis, down)  17 us
    ppermute x6, starting transfers between devices, neighbors(): before = lax.ppermute(last, axis, up)  16.4 us
  transfers between devices with their start and end apart: 15, of which 12 were waited for; matrix products, arithmetic and copies ran while one was open for 2% of the time, Pallas kernels for 10%

profile of v3, /device:TPU:104, one launch (start us, length us, event | category | flops | bytes accessed | tf_op | source)
XLA Modules:
  0.0 217.0 jit_solution(2944680804999289778)
XLA Ops:
  4.1 3.8 %collective-permute-start.1 = (bf16[8,4,32,128]{3,2,1,0:T(8,128)(2,1)S(1)}, bf16[8,4,32,128]{3,2,1,0:T(8,128)(2,1)S(1)}, u32[]{:S(2)}, u32[]{:S(2)}) collective-permute-start(bf16[8,4,32,128]{3,2,1,0:T(8,128)(2,1)S(1)} %get-tuple-element.22), channel_id=1, source_target_pairs={{1,0},{2,1},{3,2},{4,3},{5,4},{6,5},{7,6},{8,7},{9,8},{10,9},{11,1... | collective-permute-start | bytes 786440 | tf_op jit(solution)/shard_map/ppermute | solution.py:40
  7.9 4.1 %collective-permute-done.yb_ref = bf16[8,4,32,128]{3,2,1,0:T(8,128)(2,1)S(1)} collective-permute-done((bf16[8,4,32,128]{3,2,1,0:T(8,128)(2,1)S(1)}, bf16[8,4,32,128]{3,2,1,0:T(8,128)(2,1)S(1)}, u32[]{:S(2)}, u32[]{:S(2)}) %collective-permute-start) | collective-permute-done | bytes 262176 | tf_op jit(solution)/shard_map/ppermute | solution.py:39
  12.0 4.0 %collective-permute-done.1.ya_ref = bf16[8,4,32,128]{3,2,1,0:T(8,128)(2,1)S(1)} collective-permute-done((bf16[8,4,32,128]{3,2,1,0:T(8,128)(2,1)S(1)}, bf16[8,4,32,128]{3,2,1,0:T(8,128)(2,1)S(1)}, u32[]{:S(2)}, u32[]{:S(2)}) %collective-permute-start.1) | collective-permute-done | bytes 262176 | tf_op jit(solution)/shard_map/ppermute | solution.py:40
  18.2 3.6 %collective-permute-start.3 = (bf16[4,16,32,128]{3,2,1,0:T(8,128)(2,1)S(1)}, bf16[4,16,32,128]{3,2,1,0:T(8,128)(2,1)S(1)}, u32[]{:S(2)}, u32[]{:S(2)}) collective-permute-start(bf16[4,16,32,128]{3,2,1,0:T(8,128)(2,1)S(1)} %get-tuple-element.20), channel_id=1, source_target_pairs={{16,0},{32,16},{48,32},{64,48},{80,64},{96,80},{112,96},{17,1},{33... | collective-permute-start | bytes 1572872 | tf_op jit(solution)/shard_map/ppermute | solution.py:40
  21.9 4.9 %collective-permute-done.2.xb_ref = bf16[4,16,32,128]{3,2,1,0:T(8,128)(2,1)S(1)} collective-permute-done((bf16[4,16,32,128]{3,2,1,0:T(8,128)(2,1)S(1)}, bf16[4,16,32,128]{3,2,1,0:T(8,128)(2,1)S(1)}, u32[]{:S(2)}, u32[]{:S(2)}) %collective-permute-start.2) | collective-permute-done | bytes 524320 | tf_op jit(solution)/shard_map/ppermute | solution.py:39
  28.5 8.0 %shard_map.68 = (f32[8192,128]{1,0:T(8,128)}, f32[4224,128]{1,0:T(8,128)}) custom-call(s32[64]{0:T(128)S(1)} %add_bitcast_fusion.first_ref, bf16[8,8,32,128]{3,2,1,0:T(8,128)(2,1)S(1)} %fusion.3.own_ref, bf16[8,4,32,128]{3,2,1,0:T(8,128)(2,1)S(1)} %collective-permute-done.yb_ref, bf16[8,4,32,128]{3,2,1,0:T(8,128)(2,1)S(1)} %collective-permute-done.1.ya_ref, ...), custom_call_target="tpu_custom_call" | custom-call | flops 1073741824 | bytes 10485760 | tf_op jit(solution)/shard_map/pallas_call | solution.py:24
  36.5 11.0 %all-to-all-start = ((f32[128,33,1,128]{3,2,1,0:T(1,128)}), f32[128,33,1,128]{3,2,1,0:T(1,128)S(1)}, u32[]{:S(2)}, u32[]{:S(2)}) async-start(f32[128,33,1,128]{3,2,1,0:T(1,128)} %bitcast.2), calls=%async_computation | async-start | bytes 4325376 | tf_op jit(solution)/shard_map/all_to_all | solution.py:459
  50.4 7.0 %shard_map.69.group_ref = s32[32,128]{1,0:T(8,128)S(1)} custom-call(s32[1]{0:T(128)} %bitcast.1.side_ref, s32[256,128]{1,0:T(8,128)S(1)} %reshape.56.members_ref), custom_call_target="tpu_custom_call" | custom-call | flops 536870912 | bytes 131072 | tf_op jit(solution)/shard_map/pallas_call | solution.py:24
  57.4 17.7 %all-to-all-done = f32[128,33,1,128]{3,2,1,0:T(1,128)S(1)} async-done(((f32[128,33,1,128]{3,2,1,0:T(1,128)}), f32[128,33,1,128]{3,2,1,0:T(1,128)S(1)}, u32[]{:S(2)}, u32[]{:S(2)}) %all-to-all-start) | async-done | bytes 2162720 | tf_op jit(solution)/shard_map/all_to_all | solution.py:459
  75.0 7.1 %shard_map.70 = f32[2176,128]{1,0:T(8,128)S(1)} custom-call(s32[32,128]{1,0:T(8,128)S(1)} %shard_map.69.group_ref, f32[4224,128]{1,0:T(8,128)S(1)} %bitcast.19), custom_call_target="tpu_custom_call" | custom-call | flops 4294967296 | bytes 5242880 | tf_op jit(solution)/shard_map/pallas_call | solution.py:24
  83.2 7.5 %all-to-all-start.1 = ((f32[128,17,1,128]{3,2,1,0:T(1,128)}), f32[128,17,1,128]{3,2,1,0:T(1,128)S(1)}, u32[]{:S(2)}, u32[]{:S(2)}) async-start(f32[128,17,1,128]{3,2,1,0:T(1,128)} %bitcast.21), calls=%async_computation.1 | async-start | bytes 2228224 | tf_op jit(solution)/shard_map/all_to_all | solution.py:459
  91.5 15.7 %all-to-all-done.1 = f32[128,17,1,128]{3,2,1,0:T(1,128)S(1)} async-done(((f32[128,17,1,128]{3,2,1,0:T(1,128)}), f32[128,17,1,128]{3,2,1,0:T(1,128)S(1)}, u32[]{:S(2)}, u32[]{:S(2)}) %all-to-all-start.1) | async-done | bytes 1114144 | tf_op jit(solution)/shard_map/all_to_all | solution.py:459
  107.2 16.5 %shard_map.71 = bf16[2304,128]{1,0:T(8,128)(2,1)S(1)} custom-call(f32[16]{0:T(128)S(1)} %dynamic_slice.3.tau_ref, f32[2176,128]{1,0:T(8,128)S(1)} %bitcast.20), custom_call_target="tpu_custom_call" | custom-call | flops 3221225472 | bytes 2097152 | tf_op jit(solution)/shard_map/pallas_call | solution.py:24
  123.7 18.2 %all_to_all.20 = bf16[128,9,2,128]{3,2,1,0:T(2,128)(2,1)S(1)} all-to-all(bf16[128,9,2,128]{3,2,1,0:T(2,128)(2,1)S(1)} %bitcast.23), channel_id=1, replica_groups=mesh['gx'=8,'gy'=16] {'gx','gy'}, dimensions={0} | all-to-all | bytes 1179648 | tf_op jit(solution)/shard_map/all_to_all | solution.py:459
  141.9 4.6 %shard_map.72 = bf16[4352,128]{1,0:T(8,128)(2,1)} custom-call(s32[32,128]{1,0:T(8,128)S(1)} %shard_map.69.group_ref, bf16[2304,128]{1,0:T(8,128)(2,1)S(1)} %bitcast.24), custom_call_target="tpu_custom_call" | custom-call | flops 4294967296 | bytes 3145728 | tf_op jit(solution)/shard_map/pallas_call | solution.py:24
  146.5 7.9 %all-to-all-start.3 = ((bf16[128,17,2,128]{3,2,1,0:T(2,128)(2,1)}), bf16[128,17,2,128]{3,2,1,0:T(2,128)(2,1)S(1)}, u32[]{:S(2)}, u32[]{:S(2)}) async-start(bf16[128,17,2,128]{3,2,1,0:T(2,128)(2,1)} %bitcast.8), calls=%async_computation.3 | async-start | bytes 2228224 | tf_op jit(solution)/shard_map/all_to_all | solution.py:459
  157.0 3.3 %collective-permute-start.9 = (s32[3,64]{1,0:T(4,128)S(1)}, s32[3,64]{1,0:T(4,128)S(1)}, u32[]{:S(2)}, u32[]{:S(2)}) collective-permute-start(s32[3,64]{1,0:T(4,128)S(1)} %broadcast_add_fusion), channel_id=1, source_target_pairs={{1,0},{2,1},{3,2},{4,3},{5,4},{6,5},{7,6},{8,7},{9,8},{10,9},{11,1... | collective-permute-start | bytes 2312 | tf_op jit(solution)/shard_map/ppermute | solution.py:40
  160.3 6.0 %collective-permute-done.8 = s32[3,64]{1,0:T(4,128)S(1)} collective-permute-done((s32[3,64]{1,0:T(4,128)S(1)}, s32[3,64]{1,0:T(4,128)S(1)}, u32[]{:S(2)}, u32[]{:S(2)}) %collective-permute-start.8) | collective-permute-done | bytes 800 | tf_op jit(solution)/shard_map/ppermute | solution.py:39
  169.4 3.8 %collective-permute-start.11 = (s32[3,192]{1,0:T(4,128)S(1)}, s32[3,192]{1,0:T(4,128)S(1)}, u32[]{:S(2)}, u32[]{:S(2)}) collective-permute-start(s32[3,192]{1,0:T(4,128)S(1)} %pad_add_fusion), channel_id=1, source_target_pairs={{16,0},{32,16},{48,32},{64,48},{80,64},{96,80},{112,96},{17,1},{33... | collective-permute-start | bytes 6920 | tf_op jit(solution)/shard_map/ppermute | solution.py:40
  173.2 11.8 %shard_map.73 = (f32[4096,128]{1,0:T(8,128)S(1)}, bf16[2048,128]{1,0:T(8,128)(2,1)S(1)}, bf16[2048,128]{1,0:T(8,128)(2,1)S(1)}) custom-call(s32[64]{0:T(128)S(1)} %add_bitcast_fusion.first_ref, f32[8192,128]{1,0:T(8,128)} %get-tuple-element.7.cells_ref, bf16[4352,128]{1,0:T(8,128)(2,1)S(1)} %bitcast.18), custom_call_target="tpu_custom_call" | custom-call | flops 1073741824 | bytes 10485760 | tf_op jit(solution)/shard_map/pallas_call | solution.py:24
  189.5 4.1 %collective-permute-done.5 = bf16[4,16,32,128]{3,2,1,0:T(8,128)(2,1)S(1)} collective-permute-done((bf16[4,16,32,128]{3,2,1,0:T(8,128)(2,1)S(1)}, bf16[4,16,32,128]{3,2,1,0:T(8,128)(2,1)S(1)}, u32[]{:S(2)}, u32[]{:S(2)}) %collective-permute-start.5) | collective-permute-done | bytes 524320 | tf_op jit(solution)/shard_map/ppermute | solution.py:40
  193.8 3.6 %collective-permute-done.4 = bf16[4,16,32,128]{3,2,1,0:T(8,128)(2,1)S(1)} collective-permute-done((bf16[4,16,32,128]{3,2,1,0:T(8,128)(2,1)S(1)}, bf16[4,16,32,128]{3,2,1,0:T(8,128)(2,1)S(1)}, u32[]{:S(2)}, u32[]{:S(2)}) %collective-permute-start.4) | collective-permute-done | bytes 524320 | tf_op jit(solution)/shard_map/ppermute | solution.py:39
  198.5 5.6 %collective-permute-start.6 = (bf16[8,4,32,128]{3,2,1,0:T(8,128)(2,1)}, bf16[8,4,32,128]{3,2,1,0:T(8,128)(2,1)S(1)}, u32[]{:S(2)}, u32[]{:S(2)}) collective-permute-start(bf16[8,4,32,128]{3,2,1,0:T(8,128)(2,1)} %get-tuple-element.18), channel_id=1, source_target_pairs={{0,1},{1,2},{2,3},{3,4},{4,5},{5,6},{6,7},{7,8},{8,9},{9,10},{10,1... | collective-permute-start | bytes 786440 | tf_op jit(solution)/shard_map/ppermute | solution.py:39
  209.1 5.9 %collective-permute-done.7 = bf16[8,4,32,128]{3,2,1,0:T(8,128)(2,1)S(1)} collective-permute-done((bf16[8,4,32,128]{3,2,1,0:T(8,128)(2,1)S(1)}, bf16[8,4,32,128]{3,2,1,0:T(8,128)(2,1)S(1)}, u32[]{:S(2)}, u32[]{:S(2)}) %collective-permute-start.7) | collective-permute-done | bytes 262176 | tf_op jit(solution)/shard_map/ppermute | solution.py:40
  (45 shorter events, 30.3 us)
Async XLA Ops:
  2.0 9.9 %collective-permute-start = (bf16[8,4,32,128]{3,2,1,0:T(8,128)(2,1)S(1)}, bf16[8,4,32,128]{3,2,1,0:T(8,128)(2,1)S(1)}, u32[]{:S(2)}, u32[]{:S(2)}) collective-permute-start(bf16[8,4,32,128]{3,2,1,0:T(8,128)(2,1)S(1)} %get-tuple-element.23), channel_id=1, source_target_pairs={{0,1},{1,2},{2,3},{3,4},{4,5},{5,6},{6,7},{7,8},{8,9},{9,10},{10,1... | collective-permute-start | bytes 786440 | tf_op jit(solution)/shard_map/ppermute | solution.py:39
  4.1 17.8 %copy-start.4 = (s32[3,64]{1,0:T(4,128)S(1)}, s32[3,64]{1,0:T(4,128)}, u32[]{:S(2)}) copy-start(s32[3,64]{1,0:T(4,128)} %param.7) | copy-start | bytes 2308
  4.1 11.9 %collective-permute-start.1 = (bf16[8,4,32,128]{3,2,1,0:T(8,128)(2,1)S(1)}, bf16[8,4,32,128]{3,2,1,0:T(8,128)(2,1)S(1)}, u32[]{:S(2)}, u32[]{:S(2)}) collective-permute-start(bf16[8,4,32,128]{3,2,1,0:T(8,128)(2,1)S(1)} %get-tuple-element.22), channel_id=1, source_target_pairs={{1,0},{2,1},{3,2},{4,3},{5,4},{6,5},{7,6},{8,7},{9,8},{10,9},{11,1... | collective-permute-start | bytes 786440 | tf_op jit(solution)/shard_map/ppermute | solution.py:40
  16.2 10.5 %collective-permute-start.2 = (bf16[4,16,32,128]{3,2,1,0:T(8,128)(2,1)S(1)}, bf16[4,16,32,128]{3,2,1,0:T(8,128)(2,1)S(1)}, u32[]{:S(2)}, u32[]{:S(2)}) collective-permute-start(bf16[4,16,32,128]{3,2,1,0:T(8,128)(2,1)S(1)} %get-tuple-element.21), channel_id=1, source_target_pairs={{0,16},{16,32},{32,48},{48,64},{64,80},{80,96},{96,112},{1,17},{17... | collective-permute-start | bytes 1572872 | tf_op jit(solution)/shard_map/ppermute | solution.py:39
  18.2 10.3 %collective-permute-start.3 = (bf16[4,16,32,128]{3,2,1,0:T(8,128)(2,1)S(1)}, bf16[4,16,32,128]{3,2,1,0:T(8,128)(2,1)S(1)}, u32[]{:S(2)}, u32[]{:S(2)}) collective-permute-start(bf16[4,16,32,128]{3,2,1,0:T(8,128)(2,1)S(1)} %get-tuple-element.20), channel_id=1, source_target_pairs={{16,0},{32,16},{48,32},{64,48},{80,64},{96,80},{112,96},{17,1},{33... | collective-permute-start | bytes 1572872 | tf_op jit(solution)/shard_map/ppermute | solution.py:40
  36.5 11.0 %copy-start.3 = (s32[2048,16]{0,1:T(8,128)S(1)}, s32[2048,16]{0,1:T(8,128)}, u32[]{:S(2)}) copy-start(s32[2048,16]{0,1:T(8,128)} %param.8) | copy-start | bytes 393220
  36.5 38.5 %all-to-all-start = ((f32[128,33,1,128]{3,2,1,0:T(1,128)}), f32[128,33,1,128]{3,2,1,0:T(1,128)S(1)}, u32[]{:S(2)}, u32[]{:S(2)}) async-start(f32[128,33,1,128]{3,2,1,0:T(1,128)} %bitcast.2), calls=%async_computation | async-start | bytes 4325376 | tf_op jit(solution)/shard_map/all_to_all | solution.py:459
  82.1 1.1 copy-start
  83.2 24.0 %all-to-all-start.1 = ((f32[128,17,1,128]{3,2,1,0:T(1,128)}), f32[128,17,1,128]{3,2,1,0:T(1,128)S(1)}, u32[]{:S(2)}, u32[]{:S(2)}) async-start(f32[128,17,1,128]{3,2,1,0:T(1,128)} %bitcast.21), calls=%async_computation.1 | async-start | bytes 2228224 | tf_op jit(solution)/shard_map/all_to_all | solution.py:459
  146.5 26.7 %all-to-all-start.3 = ((bf16[128,17,2,128]{3,2,1,0:T(2,128)(2,1)}), bf16[128,17,2,128]{3,2,1,0:T(2,128)(2,1)S(1)}, u32[]{:S(2)}, u32[]{:S(2)}) async-start(bf16[128,17,2,128]{3,2,1,0:T(2,128)(2,1)} %bitcast.8), calls=%async_computation.3 | async-start | bytes 2228224 | tf_op jit(solution)/shard_map/all_to_all | solution.py:459
  154.4 11.8 %collective-permute-start.8 = (s32[3,64]{1,0:T(4,128)S(1)}, s32[3,64]{1,0:T(4,128)S(1)}, u32[]{:S(2)}, u32[]{:S(2)}) collective-permute-start(s32[3,64]{1,0:T(4,128)S(1)} %broadcast_add_fusion), channel_id=1, source_target_pairs={{0,1},{1,2},{2,3},{3,4},{4,5},{5,6},{6,7},{7,8},{8,9},{9,10},{10,1... | collective-permute-start | bytes 2312 | tf_op jit(solution)/shard_map/ppermute | solution.py:39
  157.0 10.4 %collective-permute-start.9 = (s32[3,64]{1,0:T(4,128)S(1)}, s32[3,64]{1,0:T(4,128)S(1)}, u32[]{:S(2)}, u32[]{:S(2)}) collective-permute-start(s32[3,64]{1,0:T(4,128)S(1)} %broadcast_add_fusion), channel_id=1, source_target_pairs={{1,0},{2,1},{3,2},{4,3},{5,4},{6,5},{7,6},{8,7},{9,8},{10,9},{11,1... | collective-permute-start | bytes 2312 | tf_op jit(solution)/shard_map/ppermute | solution.py:40
  167.4 38.7 %collective-permute-start.10 = (s32[3,192]{1,0:T(4,128)S(1)}, s32[3,192]{1,0:T(4,128)S(1)}, u32[]{:S(2)}, u32[]{:S(2)}) collective-permute-start(s32[3,192]{1,0:T(4,128)S(1)} %pad_add_fusion), channel_id=1, source_target_pairs={{0,16},{16,32},{32,48},{48,64},{64,80},{80,96},{96,112},{1,17},{17... | collective-permute-start | bytes 6920 | tf_op jit(solution)/shard_map/ppermute | solution.py:39
  169.4 36.8 %collective-permute-start.11 = (s32[3,192]{1,0:T(4,128)S(1)}, s32[3,192]{1,0:T(4,128)S(1)}, u32[]{:S(2)}, u32[]{:S(2)}) collective-permute-start(s32[3,192]{1,0:T(4,128)S(1)} %pad_add_fusion), channel_id=1, source_target_pairs={{16,0},{32,16},{48,32},{64,48},{80,64},{96,80},{112,96},{17,1},{33... | collective-permute-start | bytes 6920 | tf_op jit(solution)/shard_map/ppermute | solution.py:40
  185.0 8.6 %collective-permute-start.5 = (bf16[4,16,32,128]{3,2,1,0:T(8,128)(2,1)S(1)}, bf16[4,16,32,128]{3,2,1,0:T(8,128)(2,1)S(1)}, u32[]{:S(2)}, u32[]{:S(2)}) collective-permute-start(bf16[4,16,32,128]{3,2,1,0:T(8,128)(2,1)S(1)} %bitcast.26), channel_id=1, source_target_pairs={{16,0},{32,16},{48,32},{64,48},{80,64},{96,80},{112,96},{17,1},{33... | collective-permute-start | bytes 1572872 | tf_op jit(solution)/shard_map/ppermute | solution.py:40
  187.0 10.5 %collective-permute-start.4 = (bf16[4,16,32,128]{3,2,1,0:T(8,128)(2,1)S(1)}, bf16[4,16,32,128]{3,2,1,0:T(8,128)(2,1)S(1)}, u32[]{:S(2)}, u32[]{:S(2)}) collective-permute-start(bf16[4,16,32,128]{3,2,1,0:T(8,128)(2,1)S(1)} %bitcast.25), channel_id=1, source_target_pairs={{0,16},{16,32},{32,48},{48,64},{64,80},{80,96},{96,112},{1,17},{17... | collective-permute-start | bytes 1572872 | tf_op jit(solution)/shard_map/ppermute | solution.py:39
  198.5 10.6 %collective-permute-start.6 = (bf16[8,4,32,128]{3,2,1,0:T(8,128)(2,1)}, bf16[8,4,32,128]{3,2,1,0:T(8,128)(2,1)S(1)}, u32[]{:S(2)}, u32[]{:S(2)}) collective-permute-start(bf16[8,4,32,128]{3,2,1,0:T(8,128)(2,1)} %get-tuple-element.18), channel_id=1, source_target_pairs={{0,1},{1,2},{2,3},{3,4},{4,5},{5,6},{6,7},{7,8},{8,9},{9,10},{10,1... | collective-permute-start | bytes 786440 | tf_op jit(solution)/shard_map/ppermute | solution.py:39
  204.1 10.9 %collective-permute-start.7 = (bf16[8,4,32,128]{3,2,1,0:T(8,128)(2,1)S(1)}, bf16[8,4,32,128]{3,2,1,0:T(8,128)(2,1)S(1)}, u32[]{:S(2)}, u32[]{:S(2)}) collective-permute-start(bf16[8,4,32,128]{3,2,1,0:T(8,128)(2,1)S(1)} %get-tuple-element.19), channel_id=1, source_target_pairs={{1,0},{2,1},{3,2},{4,3},{5,4},{6,5},{7,6},{8,7},{9,8},{10,9},{11,1... | collective-permute-start | bytes 786440 | tf_op jit(solution)/shard_map/ppermute | solution.py:40
  208.8 6.5 %copy-start.1 = (bf16[8,8,32,128]{3,2,1,0:T(8,128)(2,1)S(1)}, bf16[8,8,32,128]{3,2,1,0:T(8,128)(2,1)}, u32[]{:S(2)}) copy-start(bf16[8,8,32,128]{3,2,1,0:T(8,128)(2,1)} %param.6) | copy-start | bytes 1572868
  208.8 6.5 %copy-start.2 = (bf16[8,8,32,128]{3,2,1,0:T(8,128)(2,1)S(1)}, bf16[8,8,32,128]{3,2,1,0:T(8,128)(2,1)}, u32[]{:S(2)}) copy-start(bf16[8,8,32,128]{3,2,1,0:T(8,128)(2,1)} %param.5) | copy-start | bytes 1572868

commit v4 on v3

--- a/solution.py
+++ b/solution.py
@@ -99,11 +99,12 @@
     out_ref[...] = (acc[:32] * 16.0 + acc[32:]).astype(jnp.int32)
 
 
-def counts_body(corner_ref, base_ref, out_ref):
-    lanes = corner_ref.shape[1]
-    px = corner_ref[0:1, :] - base_ref[0]
-    py = corner_ref[1:2, :] - base_ref[1]
-    pz = corner_ref[2:3, :]
+def counts_body(near_ref, base_ref, out_ref):
+    code = jnp.concatenate([near_ref[m : m + 1, :] for m in range(5)], 1).astype(jnp.int32)
+    lanes = code.shape[1]
+    px = jnp.where(code < 0, -1000, code >> 12) - base_ref[0]
+    py = ((code >> 5) & 127) - base_ref[1]
+    pz = code & 31
     z = lax.broadcasted_iota(jnp.int32, (32, lanes), 0)
     in_z = jnp.where((z >= pz) & (z < pz + PATCH), 1.0, 0.0)
     ones = jnp.ones((lanes, 128), BF16)
@@ -121,45 +122,80 @@
     lax.fori_loop(0, 8, column, 0)
 
 
-def load_patch(cells_ref, first):
+def load_half(cells_ref, first):
     rows = []
-    for a in range(PATCH):
+    for a in range(PATCH // 2):
         for b in range(PATCH):
             rows.append(cells_ref[pl.ds(first + (a * 16 + b) * 32, PATCH), :])
-    return jnp.concatenate(rows, 0)
-
-
-def gram_body(first_ref, own_ref, yb_ref, ya_ref, xb_ref, xa_ref, cells_ref, out_ref, diag_ref):
-    cells_ref[pl.ds(0, 2048), :] = xb_ref[...].reshape(2048, 128).astype(F32)
-    cells_ref[pl.ds(6144, 2048), :] = xa_ref[...].reshape(2048, 128).astype(F32)
-
+    return jnp.concatenate(rows, 0).astype(BF16)
+
+
+def half_gram(cells_ref, first):
+    values = load_half(cells_ref, first)
+    return lax.dot_general(values, values, (((0,), (0,)), ((), ())), preferred_element_type=F32)
+
+
+def inner_gram_body(first_ref, own_ref, yb_ref, ya_ref, cells_ref, gram_ref):
     def fill(x, _):
-        row = pl.multiple_of((x + 4) * 512, 512)
+        row = pl.multiple_of(x * 512, 512)
         cells_ref[pl.ds(row, 128), :] = yb_ref[x].reshape(128, 128).astype(F32)
         cells_ref[pl.ds(row + 128, 256), :] = own_ref[x].reshape(256, 128).astype(F32)
         cells_ref[pl.ds(row + 384, 128), :] = ya_ref[x].reshape(128, 128).astype(F32)
         return 0
 
     lax.fori_loop(0, 8, fill, 0)
+
+    def patch(p, _):
+        gram_ref[p] = half_gram(cells_ref, first_ref[p])
+        return 0
+
+    lax.fori_loop(0, 64, patch, 0, unroll=8)
+
+
+def gram_body(
+    first_ref, code_ref, inner_ref, xb_ref, xa_ref, half_ref, cells_ref, out_ref, diag_ref
+):
+    cells_ref[0:2048, :] = xb_ref[...].reshape(2048, 128).astype(F32)
+    cells_ref[2048:6144, :] = inner_ref[...]
+    cells_ref[6144:8192, :] = xa_ref[...].reshape(2048, 128).astype(F32)
     diag_ref[...] = jnp.zeros_like(diag_ref)
     masks = packed_masks()
 
     def patch(p, _):
-        values = load_patch(cells_ref, first_ref[p]).astype(BF16)
-        gram = lax.dot_general(values, values, (((0,), (0,)), ((), ())), preferred_element_type=F32)
+        gram = half_ref[p] + half_gram(cells_ref, first_ref[p])
         packed, rest = pack_symmetric(gram, masks)
-        side = p // 32
-        out_ref[pl.ds(side * (64 * 33) + p - side * 32, 64, stride=33), :] = packed
+        out_ref[pl.ds((p // 32) * (64 * 33 - 32) + p, 64, stride=33), :] = packed
         diag_ref[pl.ds(p, 1), :] = jnp.sum(rest, axis=0, keepdims=True)
         return 0
 
     lax.fori_loop(0, 64, patch, 0, unroll=8)
+    left = lax.broadcasted_iota(jnp.int32, (64, 128), 1) < 64
     turned = diag_ref[...].T[64:]
-    out_ref[pl.ds(32, 64, stride=33), :] = turned
-    out_ref[pl.ds(64 * 33 + 32, 64, stride=33), :] = pltpu.roll(turned, 96, axis=1)
-
-
-def group_sum_body(group_ref, rows_ref, out_ref, limbs_ref):
+    out_ref[pl.ds(32, 64, stride=33), :] = jnp.where(left, turned, code_ref[...])
+    out_ref[pl.ds(64 * 33 + 32, 64, stride=33), :] = jnp.where(
+        left, pltpu.roll(turned, 96, axis=1), code_ref[...]
+    )
+
+
+def group_sum_body(near_id_ref, group_ref, rows_ref, out_ref, near_ref, limbs_ref):
+    right_half = lax.broadcasted_iota(jnp.int32, (1, 128), 1) >= 64
+    codes = []
+    for n in range(10):
+        code = jnp.full((1, 128), -1.0, F32)
+        if n < 9:
+            source = near_id_ref[n]
+            row = rows_ref[pl.ds(jnp.maximum(source, 0) * 33 + 32, 1), :]
+            code = jnp.where(source >= 0, row, code)
+        codes.append(code)
+    near_ref[...] = jnp.concatenate(
+        [
+            jnp.where(right_half, codes[2 * m], pltpu.roll(codes[2 * m + 1], 64, axis=1))
+            for m in range(5)
+        ]
+        + [jnp.full((3, 128), -1.0, F32)],
+        0,
+    )
+
     def split(i, _):
         value = rows_ref[pl.ds(i * 33, 32), :]
         high = value.astype(BF16)
@@ -235,6 +271,9 @@
     lane16 = lax.broadcasted_iota(jnp.int32, (NB, 128), 1)
     sub16 = lax.broadcasted_iota(jnp.int32, (NB, 128), 0)
     same = (row_id >> 4) == (lane_id >> 4)
+    segment = (lane_id >> 4).astype(F32).astype(BF16)
+    first_lanes = segment < jnp.asarray(3, BF16)
+    second_lanes = segment < jnp.asarray(5, BF16)
 
     def block(b, _):
         start = pl.multiple_of(b * NB, NB)
@@ -250,7 +289,6 @@
         in_block = (lane16 >= start) & (lane16 < start + NB)
         identity = jnp.where(lane16 - start == sub16, 1.0, 0.0)
         in_lanes = (lane_id >= start) & (lane_id < start + NB)
-        in_rows = (row_id >= start) & (row_id < start + NB)
         scaled = []
         for h in range(2):
             left = jnp.where(same, jnp.concatenate([pivots[h * NB : (h + 1) * NB]] * 8, 0), 0.0)
@@ -259,11 +297,21 @@
             )
             product = wide_product(left, right)
             scaled += [product[k * NB : (k + 1) * NB] for k in range(8)]
+        pick = start + (lane_id & (NB - 1))
         for g in range(per):
             matrix = sys_ref[g]
-            wide = jnp.where(in_rows, jnp.concatenate([scaled[g]] * (128 // NB), 0), 0.0)
-            update = wide_product(matrix, wide)
-            sys_ref[g] = jnp.where(in_rows, wide, jnp.where(in_lanes, 0.0, matrix) - update)
+            columns = jnp.take_along_axis(matrix, pick, axis=1, mode="promise_in_bounds")
+            c0, c1, c2 = limbs(columns)
+            w0, w1, w2 = limbs(scaled[g])
+            none = jnp.zeros_like(w0)
+            update = jnp.dot(
+                jnp.where(first_lanes, c0, jnp.where(second_lanes, c1, c2)),
+                jnp.concatenate([w2, w1, w0, w1, w0, w0, none, none], 0),
+                preferred_element_type=F32,
+            )
+            sys_ref[g] = jnp.where(in_lanes, 0.0, matrix) - update
+        for g in range(per):
+            sys_ref[g, pl.ds(start, NB), :] = scaled[g]
         return 0
 
     lax.fori_loop(0, 128 // NB, block, 0)
@@ -389,16 +437,48 @@
     out_ref[...] = stage_ref[...].astype(BF16)
 
 
-def apply_body(
+def add_halves(first_ref, cells_ref, factor_ref, sum_ref, even_ref, odd_ref):
+    odd_ref[...] = jnp.zeros_like(odd_ref)
+    count = 4
+
+    def multiply(p, ref):
+        for k in range(count):
+            values = load_half(cells_ref, first_ref[p + k])
+            ref[k * 256 : (k + 1) * 256, :] = jnp.dot(
+                values, factor_ref[p + k], preferred_element_type=F32
+            )
+
+    def accumulate(p, ref):
+        for k in range(count):
+            first = first_ref[p + k]
+            for a in range(PATCH // 2):
+                for b in range(PATCH):
+                    at = pl.ds(first + (a * 16 + b) * 32, PATCH)
+                    row = k * 256 + (a * PATCH + b) * PATCH
+                    sum_ref[at, :] += ref[row : row + PATCH, :]
+
+    def several(i, _):
+        p = i * (2 * count)
+        multiply(p, even_ref)
+        accumulate(jnp.maximum(p - count, 0), odd_ref)
+        multiply(p + count, odd_ref)
+        accumulate(p, even_ref)
+        return 0
+
+    lax.fori_loop(0, 64 // (2 * count), several, 0)
+    accumulate(64 - count, odd_ref)
+
+
+def edge_apply_body(
     first_ref,
     cells_ref,
     rows_ref,
     inner_ref,
     low_ref,
     high_ref,
+    factor_ref,
     wide_ref,
     sum_ref,
-    factor_ref,
     even_ref,
     odd_ref,
     diag_ref,
@@ -419,38 +499,17 @@
         return 0
 
     lax.fori_loop(0, 64, unpack, 0, unroll=8)
-    odd_ref[...] = jnp.zeros_like(odd_ref)
-    count = 4
-
-    def multiply(p, ref):
-        for k in range(count):
-            values = load_patch(cells_ref, first_ref[p + k]).astype(BF16)
-            ref[k * 512 : (k + 1) * 512, :] = jnp.dot(
-                values, factor_ref[p + k], preferred_element_type=F32
-            )
-
-    def accumulate(p, ref):
-        for k in range(count):
-            first = first_ref[p + k]
-            for a in range(PATCH):
-                for b in range(PATCH):
-                    at = pl.ds(first + (a * 16 + b) * 32, PATCH)
-                    row = k * 512 + (a * PATCH + b) * PATCH
-                    sum_ref[at, :] += ref[row : row + PATCH, :]
-
-    def several(i, _):
-        p = i * (2 * count)
-        multiply(p, even_ref)
-        accumulate(jnp.maximum(p - count, 0), odd_ref)
-        multiply(p + count, odd_ref)
-        accumulate(p, even_ref)
-        return 0
-
-    lax.fori_loop(0, 64 // (2 * count), several, 0)
-    accumulate(64 - count, odd_ref)
+    add_halves(first_ref, cells_ref, factor_ref, sum_ref, even_ref, odd_ref)
     low_ref[...] = sum_ref[0:2048, :].astype(BF16)
     inner_ref[...] = sum_ref[2048:6144, :]
     high_ref[...] = sum_ref[6144:8192, :].astype(BF16)
+
+
+def inner_apply_body(
+    first_ref, cells_ref, factor_ref, start_ref, sum_ref, even_ref, odd_ref
+):
+    sum_ref[...] = start_ref[...]
+    add_halves(first_ref, cells_ref, factor_ref, sum_ref, even_ref, odd_ref)
 
 
 def exchange(rows, sublanes):
@@ -467,16 +526,35 @@
     myself = index_x * 16 + index_y
     mixture = (estimate.astype(F32) + dual.astype(F32)).astype(BF16)
 
+    begin_x = corners[0] - (index_x * 8 - margin)
+    begin_y = corners[1] - (index_y * 8 - margin)
+    first = (begin_x * 16 + begin_y) * 32 + corners[2]
+    low_half = begin_x <= margin
+    first_edge = first + jnp.where(low_half, 0, 2048)
+    first_inner = first + jnp.where(low_half, 0, -2048)
+    code = ((corners[0] * 128 + corners[1]) * 32 + corners[2]).astype(F32)
+    code = jnp.concatenate([jnp.zeros((64,), F32), code]).reshape(1, 128)
+
     yb, ya = neighbors(mixture, "gy", mixture[:, :margin], mixture[:, 8 - margin :])
-    marked = corners + 1
-    cb, ca = neighbors(marked, "gy", marked, marked)
-    wide = jnp.concatenate([yb, mixture, ya], 1)
+    inner_cells, half_grams = call(
+        inner_gram_body,
+        (jax.ShapeDtypeStruct((4096, 128), F32), jax.ShapeDtypeStruct((64, 128, 128), F32)),
+        first_inner,
+        mixture,
+        yb,
+        ya,
+        specs=[SMEM] + [VMEM] * 3,
+        flops=2 * 64 * 256 * 128 * 128,
+        nbytes=8 << 20,
+    )
+    wide = jnp.concatenate(
+        [
+            jnp.concatenate([yb[:margin], mixture[:margin], ya[:margin]], 1),
+            jnp.concatenate([yb[margin:], mixture[margin:], ya[margin:]], 1),
+        ],
+        0,
+    )
     xb, xa = neighbors(wide, "gx", wide[:margin], wide[8 - margin :])
-    near = jnp.concatenate([cb, marked, ca], 1)
-    nb, na = neighbors(near, "gx", near, near)
-    near = jnp.concatenate([nb, near, na, jnp.zeros((3, 64), jnp.int32)], 1)
-    near = jnp.where(near == 0, -1000, near - 1)
-
     side = (myself // 64).reshape(1)
     table = call(
         group_table_body,
@@ -488,6 +566,36 @@
         nbytes=1 << 17,
     )
     base = jnp.stack([index_x * 8, index_y * 8])
+    cells, grams = call(
+        gram_body,
+        (jax.ShapeDtypeStruct((8192, 128), F32), jax.ShapeDtypeStruct((128 * 33, 128), F32)),
+        first_edge,
+        code,
+        inner_cells,
+        xb,
+        xa,
+        half_grams,
+        specs=[SMEM] + [VMEM] * 5,
+        scratch=[pltpu.VMEM((128, 128), F32)],
+        flops=2 * 64 * 256 * 128 * 128,
+        nbytes=10 << 20,
+    )
+    rows = exchange(grams, 1)
+    offset = jnp.arange(9, dtype=jnp.int32)
+    near_x = index_x + offset // 3 - 1
+    near_y = index_y + offset % 3 - 1
+    exists = (near_x >= 0) & (near_x < 8) & (near_y >= 0) & (near_y < 16)
+    sums, near = call(
+        group_sum_body,
+        (jax.ShapeDtypeStruct((128 * 17, 128), F32), jax.ShapeDtypeStruct((8, 128), F32)),
+        jnp.where(exists, near_x * 16 + near_y, -1),
+        table,
+        rows,
+        specs=[SMEM, VMEM, VMEM],
+        scratch=[pltpu.VMEM((4096, 256), BF16)],
+        flops=2 * 2048 * 4096 * 256,
+        nbytes=5 << 20,
+    )
     inverse_counts = call(
         counts_body,
         jax.ShapeDtypeStruct((2048, 128), F32),
@@ -496,34 +604,6 @@
         specs=[VMEM, SMEM],
         flops=2 * 2048 * 640 * 128,
         nbytes=1 << 20,
-    )
-
-    begin_x = corners[0] - (index_x * 8 - margin)
-    begin_y = corners[1] - (index_y * 8 - margin)
-    first = (begin_x * 16 + begin_y) * 32 + corners[2]
-    cells, grams = call(
-        gram_body,
-        (jax.ShapeDtypeStruct((8192, 128), F32), jax.ShapeDtypeStruct((128 * 33, 128), F32)),
-        first,
-        mixture,
-        yb,
-        ya,
-        xb,
-        xa,
-        specs=[SMEM] + [VMEM] * 5,
-        scratch=[pltpu.VMEM((128, 128), F32)],
-        flops=2 * 64 * 512 * 128 * 128,
-        nbytes=10 << 20,
-    )
-    rows = exchange(grams, 1)
-    sums = call(
-        group_sum_body,
-        jax.ShapeDtypeStruct((128 * 17, 128), F32),
-        table,
-        rows,
-        scratch=[pltpu.VMEM((4096, 256), BF16)],
-        flops=2 * 2048 * 4096 * 256,
-        nbytes=5 << 20,
     )
     mine = exchange(sums, 1)
     tau = lax.dynamic_slice_in_dim(thresholds, myself * 16, 16)
@@ -554,28 +634,45 @@
     )
     patch_factors = exchange(patch_rows, 2)
     edge = jax.ShapeDtypeStruct((2048, 128), BF16)
-    inner, low, high = call(
-        apply_body,
-        (jax.ShapeDtypeStruct((4096, 128), F32), edge, edge),
-        first,
+    half_result = pltpu.VMEM((1024, 128), F32)
+    partial, low, high, patch_factors = call(
+        edge_apply_body,
+        (
+            jax.ShapeDtypeStruct((4096, 128), F32),
+            edge,
+            edge,
+            jax.ShapeDtypeStruct((64, 128, 128), BF16),
+        ),
+        first_edge,
         cells,
         patch_factors,
         specs=[SMEM, VMEM, VMEM],
         scratch=[
             pltpu.VMEM((128 * 34, 128), F32),
             pltpu.VMEM((8192, 128), F32),
-            pltpu.VMEM((64, 128, 128), BF16),
-            pltpu.VMEM((2048, 128), F32),
-            pltpu.VMEM((2048, 128), F32),
+            half_result,
+            half_result,
             pltpu.VMEM((128, 128), F32),
         ],
-        flops=2 * 64 * 512 * 128 * 128,
+        flops=2 * 64 * 256 * 128 * 128,
         nbytes=10 << 20,
     )
+    from_low, from_high = neighbors(
+        partial, "gx", low.reshape(4, 16, 32, 128), high.reshape(4, 16, 32, 128)
+    )
+    inner = call(
+        inner_apply_body,
+        jax.ShapeDtypeStruct((4096, 128), F32),
+        first_inner,
+        inner_cells,
+        patch_factors,
+        partial,
+        specs=[SMEM, VMEM, VMEM, VMEM],
+        scratch=[half_result, half_result],
+        flops=2 * 64 * 256 * 128 * 128,
+        nbytes=8 << 20,
+    )
     inner = inner.reshape(8, 16, 32, 128)
-    from_low, from_high = neighbors(
-        inner, "gx", low.reshape(4, 16, 32, 128), high.reshape(4, 16, 32, 128)
-    )
     inner = jnp.concatenate(
         [inner[:margin] + from_low.astype(F32), inner[margin:] + from_high.astype(F32)], 0
     )

time: 218 us -> 214 us (0.982)
  blocking collectives: 18.2 us -> 42.1 us
  waiting for transfers between devices: 69.3 us -> 47.1 us
  starting transfers between devices: 61.2 us -> 46.5 us
  Pallas kernels: 57.5 us -> 64.8 us
    all_to_all x1 -> x2, blocking collectives: 18.2 us -> 42.1 us  [exchange(): rows = lax.all_to_all(rows, BOTH, split_axis=0, concat_axis=0, tiled=True)]
    ppermute x6 -> x4, waiting for transfers between devices: 18.9 us -> 2.7 us  [neighbors(): before = lax.ppermute(last, axis, up)]
    pallas_call x7 -> x9, Pallas kernels: 57.5 us -> 64.8 us  [call(): pl.pallas_call(body, out_shape=out_shape, in_specs=specs or [VMEM] * len(...]
    ppermute x6 -> x4, starting transfers between devices: 18.4 us -> 11.5 us  [neighbors(): after = lax.ppermute(first, axis, down)]
    all_to_all x3 -> x2, starting transfers between devices: 26.4 us -> 20.9 us  [exchange(): rows = lax.all_to_all(rows, BOTH, split_axis=0, concat_axis=0, tiled=True)]
    ppermute x6 -> x4, waiting for transfers between devices: 17 us -> 11.6 us  [neighbors(): after = lax.ppermute(first, axis, down)]
    unnamed x11 -> x15, local copies, waits for them, and re-layouts: 2.39 us -> 5.12 us
    ppermute x6 -> x4, starting transfers between devices: 16.4 us -> 14.1 us  [neighbors(): before = lax.ppermute(last, axis, up)]
  transfers between devices with their start and end apart: 15 -> 10, of which waited for: 12 -> 8; matrix products, arithmetic and copies ran while one was open for 2% -> 2% of each run, Pallas kernels for 10% -> 10%
where the time goes in v4:
time: 214 us; the launch traced here: 213 us
  Pallas kernels  64.8 us (30%)
  waiting for transfers between devices  47.1 us (22%)
  starting transfers between devices  46.5 us (22%)
  blocking collectives  42.1 us (20%)
  local copies, waits for them, and re-layouts  7.78 us (4%)
  other arithmetic  3.95 us (2%)
    pallas_call x9, Pallas kernels, call(): pl.pallas_call(body, out_shape=out_shape, in_specs=specs or [VMEM] * len(...  64.8 us
    all_to_all x2, blocking collectives, exchange(): rows = lax.all_to_all(rows, BOTH, split_axis=0, concat_axis=0, tiled=True)  42.1 us
    all_to_all x2, waiting for transfers between devices, exchange(): rows = lax.all_to_all(rows, BOTH, split_axis=0, concat_axis=0, tiled=True)  32.8 us
    all_to_all x2, starting transfers between devices, exchange(): rows = lax.all_to_all(rows, BOTH, split_axis=0, concat_axis=0, tiled=True)  20.9 us
    ppermute x4, starting transfers between devices, neighbors(): before = lax.ppermute(last, axis, up)  14.1 us
    ppermute x4, waiting for transfers between devices, neighbors(): after = lax.ppermute(first, axis, down)  11.6 us
    ppermute x4, starting transfers between devices, neighbors(): after = lax.ppermute(first, axis, down)  11.5 us
    unnamed x15, local copies, waits for them, and re-layouts  5.12 us
  transfers between devices with their start and end apart: 10, of which 8 were waited for; matrix products, arithmetic and copies ran while one was open for 2% of the time, Pallas kernels for 10%

profile of v4, /device:TPU:104, one launch (start us, length us, event | category | flops | bytes accessed | tf_op | source)
XLA Modules:
  0.0 213.2 jit_solution(18041041402082921850)
XLA Ops:
  2.0 2.3 %collective-permute-start.1 = (bf16[8,4,32,128]{3,2,1,0:T(8,128)(2,1)S(1)}, bf16[8,4,32,128]{3,2,1,0:T(8,128)(2,1)S(1)}, u32[]{:S(2)}, u32[]{:S(2)}) collective-permute-start(bf16[8,4,32,128]{3,2,1,0:T(8,128)(2,1)S(1)} %get-tuple-element.34), channel_id=1, source_target_pairs={{1,0},{2,1},{3,2},{4,3},{5,4},{6,5},{7,6},{8,7},{9,8},{10,9},{11,1... | collective-permute-start | bytes 786440 | tf_op jit(solution)/shard_map/ppermute | solution.py:40
  4.4 5.6 %collective-permute-start = (bf16[8,4,32,128]{3,2,1,0:T(8,128)(2,1)S(1)}, bf16[8,4,32,128]{3,2,1,0:T(8,128)(2,1)S(1)}, u32[]{:S(2)}, u32[]{:S(2)}) collective-permute-start(bf16[8,4,32,128]{3,2,1,0:T(8,128)(2,1)S(1)} %get-tuple-element.35), channel_id=1, source_target_pairs={{0,1},{1,2},{2,3},{3,4},{4,5},{5,6},{6,7},{7,8},{8,9},{9,10},{10,1... | collective-permute-start | bytes 786440 | tf_op jit(solution)/shard_map/ppermute | solution.py:39
  10.1 4.0 %collective-permute-done.1.ya_ref = bf16[8,4,32,128]{3,2,1,0:T(8,128)(2,1)S(1)} collective-permute-done((bf16[8,4,32,128]{3,2,1,0:T(8,128)(2,1)S(1)}, bf16[8,4,32,128]{3,2,1,0:T(8,128)(2,1)S(1)}, u32[]{:S(2)}, u32[]{:S(2)}) %collective-permute-start.1) | collective-permute-done | bytes 262176 | tf_op jit(solution)/shard_map/ppermute | solution.py:40
  15.4 1.9 collective-permute-start.2
  17.4 3.6 %collective-permute-start.3 = (bf16[4,16,32,128]{3,2,1,0:T(8,128)(2,1)S(1)}, bf16[4,16,32,128]{3,2,1,0:T(8,128)(2,1)S(1)}, u32[]{:S(2)}, u32[]{:S(2)}) collective-permute-start(bf16[4,16,32,128]{3,2,1,0:T(8,128)(2,1)S(1)} %pad_maximum_fusion.2), channel_id=1, source_target_pairs={{16,0},{32,16},{48,32},{64,48},{80,64},{96,80},{112,96},{17,1},{33... | collective-permute-start | bytes 1572872 | tf_op jit(solution)/shard_map/ppermute | solution.py:40
  21.1 5.6 %shard_map.68 = (f32[4096,128]{1,0:T(8,128)S(1)}, f32[64,128,128]{2,1,0:T(8,128)}) custom-call(s32[64]{0:T(128)S(1)} %get-tuple-element.24.first_ref, bf16[8,8,32,128]{3,2,1,0:T(8,128)(2,1)S(1)} %fusion.3.own_ref, bf16[8,4,32,128]{3,2,1,0:T(8,128)(2,1)S(1)} %collective-permute-done.yb_ref, bf16[8,4,32,128]{3,2,1,0:T(8,128)(2,1)S(1)} %collective-permute-done.1.ya_ref), custom_call_target="tpu_custom_call" | custom-call | flops 536870912 | bytes 8388608 | tf_op jit(solution)/shard_map/pallas_call | solution.py:24
  27.7 7.9 %shard_map.69 = (f32[8192,128]{1,0:T(8,128)}, f32[4224,128]{1,0:T(8,128)S(1)}) custom-call(s32[64]{0:T(128)S(1)} %fusion.14.first_ref, f32[1,128]{1,0:T(1,128)S(1)} %pad_bitcast_fusion.code_ref, f32[4096,128]{1,0:T(8,128)S(1)} %get-tuple-element.12.inner_ref.cells_ref, bf16[4,16,32,128]{3,2,1,0:T(8,128)(2,1)S(1)} %collective-permute-done.2.xb_ref, ...), custom_call_target="tpu_custom_call" | custom-call | flops 536870912 | bytes 10485760 | tf_op jit(solution)/shard_map/pallas_call | solution.py:24
  37.0 12.4 %all-to-all-start = ((f32[128,33,1,128]{3,2,1,0:T(1,128)}), f32[128,33,1,128]{3,2,1,0:T(1,128)}, u32[]{:S(2)}, u32[]{:S(2)}) async-start(f32[128,33,1,128]{3,2,1,0:T(1,128)} %bitcast.25), calls=%async_computation | async-start | bytes 4325376 | tf_op jit(solution)/shard_map/all_to_all | solution.py:518
  52.2 7.0 %shard_map.70.group_ref = s32[32,128]{1,0:T(8,128)S(1)} custom-call(s32[1]{0:T(128)} %bitcast.4.side_ref, s32[256,128]{1,0:T(8,128)S(1)} %reshape.73.members_ref), custom_call_target="tpu_custom_call" | custom-call | flops 536870912 | bytes 131072 | tf_op jit(solution)/shard_map/pallas_call | solution.py:24
  59.3 17.3 %all-to-all-done = f32[128,33,1,128]{3,2,1,0:T(1,128)} async-done(((f32[128,33,1,128]{3,2,1,0:T(1,128)}), f32[128,33,1,128]{3,2,1,0:T(1,128)}, u32[]{:S(2)}, u32[]{:S(2)}) %all-to-all-start) | async-done | bytes 2162720 | tf_op jit(solution)/shard_map/all_to_all | solution.py:518
  76.6 8.8 %shard_map.71 = (f32[2176,128]{1,0:T(8,128)S(1)}, f32[8,128]{1,0:T(8,128)S(1)}) custom-call(s32[9]{0:T(128)S(1)} %and_select_fusion.near_id_ref, s32[32,128]{1,0:T(8,128)S(1)} %shard_map.70.group_ref, f32[4224,128]{1,0:T(8,128)} %bitcast.6.rows_ref), custom_call_target="tpu_custom_call" | custom-call | flops 4294967296 | bytes 5242880 | tf_op jit(solution)/shard_map/pallas_call | solution.py:24
  86.4 8.5 %all-to-all-start.1 = ((f32[128,17,1,128]{3,2,1,0:T(1,128)}), f32[128,17,1,128]{3,2,1,0:T(1,128)}, u32[]{:S(2)}, u32[]{:S(2)}) async-start(f32[128,17,1,128]{3,2,1,0:T(1,128)} %bitcast.26), calls=%async_computation.1 | async-start | bytes 2228224 | tf_op jit(solution)/shard_map/all_to_all | solution.py:518
  95.7 15.4 %all-to-all-done.1 = f32[128,17,1,128]{3,2,1,0:T(1,128)} async-done(((f32[128,17,1,128]{3,2,1,0:T(1,128)}), f32[128,17,1,128]{3,2,1,0:T(1,128)}, u32[]{:S(2)}, u32[]{:S(2)}) %all-to-all-start.1) | async-done | bytes 1114144 | tf_op jit(solution)/shard_map/all_to_all | solution.py:518
  111.1 13.7 %shard_map.72 = bf16[2304,128]{1,0:T(8,128)(2,1)S(1)} custom-call(f32[16]{0:T(128)S(1)} %dynamic_slice.3.tau_ref, f32[2176,128]{1,0:T(8,128)} %bitcast.8.rows_ref), custom_call_target="tpu_custom_call" | custom-call | flops 3221225472 | bytes 2097152 | tf_op jit(solution)/shard_map/pallas_call | solution.py:24
  124.8 18.2 %all_to_all.20 = bf16[128,9,2,128]{3,2,1,0:T(2,128)(2,1)S(1)} all-to-all(bf16[128,9,2,128]{3,2,1,0:T(2,128)(2,1)S(1)} %bitcast.29), channel_id=1, replica_groups=mesh['gx'=8,'gy'=16] {'gx','gy'}, dimensions={0} | all-to-all | bytes 1179648 | tf_op jit(solution)/shard_map/all_to_all | solution.py:518
  143.0 3.6 %shard_map.73 = bf16[4352,128]{1,0:T(8,128)(2,1)S(1)} custom-call(s32[32,128]{1,0:T(8,128)S(1)} %shard_map.70.group_ref, bf16[2304,128]{1,0:T(8,128)(2,1)S(1)} %bitcast.30), custom_call_target="tpu_custom_call" | custom-call | flops 4294967296 | bytes 3145728 | tf_op jit(solution)/shard_map/pallas_call | solution.py:24
  146.6 24.0 %all_to_all.21 = bf16[128,17,2,128]{3,2,1,0:T(2,128)(2,1)S(1)} all-to-all(bf16[128,17,2,128]{3,2,1,0:T(2,128)(2,1)S(1)} %bitcast.27), channel_id=1, replica_groups=mesh['gx'=8,'gy'=16] {'gx','gy'}, dimensions={0} | all-to-all | bytes 2228224 | tf_op jit(solution)/shard_map/all_to_all | solution.py:518
  170.6 9.8 %shard_map.74 = (f32[4096,128]{1,0:T(8,128)S(1)}, bf16[2048,128]{1,0:T(8,128)(2,1)S(1)}, bf16[2048,128]{1,0:T(8,128)(2,1)S(1)}, bf16[64,128,128]{2,1,0:T(8,128)(2,1)}) custom-call(s32[64]{0:T(128)S(1)} %fusion.14.first_ref, f32[8192,128]{1,0:T(8,128)} %get-tuple-element.14.cells_ref, bf16[4352,128]{1,0:T(8,128)(2,1)S(1)} %bitcast.24), custom_call_target="tpu_custom_call" | custom-call | flops 536870912 | bytes 10485760 | tf_op jit(solution)/shard_map/pallas_call | solution.py:24
  183.6 3.6 %collective-permute-start.5 = (bf16[4,16,32,128]{3,2,1,0:T(8,128)(2,1)S(1)}, bf16[4,16,32,128]{3,2,1,0:T(8,128)(2,1)S(1)}, u32[]{:S(2)}, u32[]{:S(2)}) collective-permute-start(bf16[4,16,32,128]{3,2,1,0:T(8,128)(2,1)S(1)} %bitcast.31), channel_id=1, source_target_pairs={{16,0},{32,16},{48,32},{64,48},{80,64},{96,80},{112,96},{17,1},{33... | collective-permute-start | bytes 1572872 | tf_op jit(solution)/shard_map/ppermute | solution.py:40
  187.3 5.9 %shard_map.75 = f32[4096,128]{1,0:T(8,128)S(1)} custom-call(s32[64]{0:T(128)S(1)} %get-tuple-element.24.first_ref, f32[4096,128]{1,0:T(8,128)S(1)} %get-tuple-element.12.inner_ref.cells_ref, bf16[64,128,128]{2,1,0:T(8,128)(2,1)} %get-tuple-element.17.factor_ref, f32[4096,128]{1,0:T(8,128)} %copy-done.1), custom_call_target="tpu_custom_call" | custom-call | flops 536870912 | bytes 8388608 | tf_op jit(solution)/shard_map/pallas_call | solution.py:24
  194.3 4.6 %collective-permute-start.6 = (bf16[8,4,32,128]{3,2,1,0:T(8,128)(2,1)S(1)}, bf16[8,4,32,128]{3,2,1,0:T(8,128)(2,1)S(1)}, u32[]{:S(2)}, u32[]{:S(2)}) collective-permute-start(bf16[8,4,32,128]{3,2,1,0:T(8,128)(2,1)S(1)} %get-tuple-element.30), channel_id=1, source_target_pairs={{0,1},{1,2},{2,3},{3,4},{4,5},{5,6},{6,7},{7,8},{8,9},{9,10},{10,1... | collective-permute-start | bytes 786440 | tf_op jit(solution)/shard_map/ppermute | solution.py:39
  199.0 1.9 collective-permute-start.7
  201.0 2.6 %shard_map.76 = f32[2048,128]{1,0:T(8,128)S(1)} custom-call(f32[8,128]{1,0:T(8,128)S(1)} %get-tuple-element.21.near_ref, s32[2]{0:T(128)S(1)} %pad_add_fusion.base_ref), custom_call_target="tpu_custom_call" | custom-call | flops 335544320 | bytes 1048576 | tf_op jit(solution)/shard_map/pallas_call | solution.py:24
  205.1 6.2 %collective-permute-done.7 = bf16[8,4,32,128]{3,2,1,0:T(8,128)(2,1)S(1)} collective-permute-done((bf16[8,4,32,128]{3,2,1,0:T(8,128)(2,1)S(1)}, bf16[8,4,32,128]{3,2,1,0:T(8,128)(2,1)S(1)}, u32[]{:S(2)}, u32[]{:S(2)}) %collective-permute-start.7) | collective-permute-done | bytes 262176 | tf_op jit(solution)/shard_map/ppermute | solution.py:40
  (43 shorter events, 17.7 us)
Async XLA Ops:
  2.0 12.0 %collective-permute-start.1 = (bf16[8,4,32,128]{3,2,1,0:T(8,128)(2,1)S(1)}, bf16[8,4,32,128]{3,2,1,0:T(8,128)(2,1)S(1)}, u32[]{:S(2)}, u32[]{:S(2)}) collective-permute-start(bf16[8,4,32,128]{3,2,1,0:T(8,128)(2,1)S(1)} %get-tuple-element.34), channel_id=1, source_target_pairs={{1,0},{2,1},{3,2},{4,3},{5,4},{6,5},{7,6},{8,7},{9,8},{10,9},{11,1... | collective-permute-start | bytes 786440 | tf_op jit(solution)/shard_map/ppermute | solution.py:40
  4.3 16.7 %copy-start.6 = (s32[3,64]{1,0:T(4,128)S(1)}, s32[3,64]{1,0:T(4,128)}, u32[]{:S(2)}) copy-start(s32[3,64]{1,0:T(4,128)} %param.7) | copy-start | bytes 2308
  4.4 10.9 %collective-permute-start = (bf16[8,4,32,128]{3,2,1,0:T(8,128)(2,1)S(1)}, bf16[8,4,32,128]{3,2,1,0:T(8,128)(2,1)S(1)}, u32[]{:S(2)}, u32[]{:S(2)}) collective-permute-start(bf16[8,4,32,128]{3,2,1,0:T(8,128)(2,1)S(1)} %get-tuple-element.35), channel_id=1, source_target_pairs={{0,1},{1,2},{2,3},{3,4},{4,5},{5,6},{6,7},{7,8},{8,9},{9,10},{10,1... | collective-permute-start | bytes 786440 | tf_op jit(solution)/shard_map/ppermute | solution.py:39
  15.4 11.4 %collective-permute-start.2 = (bf16[4,16,32,128]{3,2,1,0:T(8,128)(2,1)S(1)}, bf16[4,16,32,128]{3,2,1,0:T(8,128)(2,1)S(1)}, u32[]{:S(2)}, u32[]{:S(2)}) collective-permute-start(bf16[4,16,32,128]{3,2,1,0:T(8,128)(2,1)S(1)} %pad_maximum_fusion.1), channel_id=1, source_target_pairs={{0,16},{16,32},{32,48},{48,64},{64,80},{80,96},{96,112},{1,17},{17... | collective-permute-start | bytes 1572872 | tf_op jit(solution)/shard_map/ppermute | solution.py:39
  17.4 10.3 %collective-permute-start.3 = (bf16[4,16,32,128]{3,2,1,0:T(8,128)(2,1)S(1)}, bf16[4,16,32,128]{3,2,1,0:T(8,128)(2,1)S(1)}, u32[]{:S(2)}, u32[]{:S(2)}) collective-permute-start(bf16[4,16,32,128]{3,2,1,0:T(8,128)(2,1)S(1)} %pad_maximum_fusion.2), channel_id=1, source_target_pairs={{16,0},{32,16},{48,32},{64,48},{80,64},{96,80},{112,96},{17,1},{33... | collective-permute-start | bytes 1572872 | tf_op jit(solution)/shard_map/ppermute | solution.py:40
  35.5 1.4 copy-start
  37.0 12.4 %copy-start.5 = (s32[2048,16]{0,1:T(8,128)S(1)}, s32[2048,16]{0,1:T(8,128)}, u32[]{:S(2)}) copy-start(s32[2048,16]{0,1:T(8,128)} %param.8) | copy-start | bytes 393220
  37.0 39.7 %all-to-all-start = ((f32[128,33,1,128]{3,2,1,0:T(1,128)}), f32[128,33,1,128]{3,2,1,0:T(1,128)}, u32[]{:S(2)}, u32[]{:S(2)}) async-start(f32[128,33,1,128]{3,2,1,0:T(1,128)} %bitcast.25), calls=%async_computation | async-start | bytes 4325376 | tf_op jit(solution)/shard_map/all_to_all | solution.py:518
  85.4 1.0 copy-start.2
  86.4 24.7 %all-to-all-start.1 = ((f32[128,17,1,128]{3,2,1,0:T(1,128)}), f32[128,17,1,128]{3,2,1,0:T(1,128)}, u32[]{:S(2)}, u32[]{:S(2)}) async-start(f32[128,17,1,128]{3,2,1,0:T(1,128)} %bitcast.26), calls=%async_computation.1 | async-start | bytes 2228224 | tf_op jit(solution)/shard_map/all_to_all | solution.py:518
  180.4 1.3 copy-start.1
  181.7 11.6 %collective-permute-start.4 = (bf16[4,16,32,128]{3,2,1,0:T(8,128)(2,1)S(1)}, bf16[4,16,32,128]{3,2,1,0:T(8,128)(2,1)S(1)}, u32[]{:S(2)}, u32[]{:S(2)}) collective-permute-start(bf16[4,16,32,128]{3,2,1,0:T(8,128)(2,1)S(1)} %bitcast.32), channel_id=1, source_target_pairs={{0,16},{16,32},{32,48},{48,64},{64,80},{80,96},{96,112},{1,17},{17... | collective-permute-start | bytes 1572872 | tf_op jit(solution)/shard_map/ppermute | solution.py:39
  183.6 10.3 %collective-permute-start.5 = (bf16[4,16,32,128]{3,2,1,0:T(8,128)(2,1)S(1)}, bf16[4,16,32,128]{3,2,1,0:T(8,128)(2,1)S(1)}, u32[]{:S(2)}, u32[]{:S(2)}) collective-permute-start(bf16[4,16,32,128]{3,2,1,0:T(8,128)(2,1)S(1)} %bitcast.31), channel_id=1, source_target_pairs={{16,0},{32,16},{48,32},{64,48},{80,64},{96,80},{112,96},{17,1},{33... | collective-permute-start | bytes 1572872 | tf_op jit(solution)/shard_map/ppermute | solution.py:40
  194.3 10.8 %collective-permute-start.6 = (bf16[8,4,32,128]{3,2,1,0:T(8,128)(2,1)S(1)}, bf16[8,4,32,128]{3,2,1,0:T(8,128)(2,1)S(1)}, u32[]{:S(2)}, u32[]{:S(2)}) collective-permute-start(bf16[8,4,32,128]{3,2,1,0:T(8,128)(2,1)S(1)} %get-tuple-element.30), channel_id=1, source_target_pairs={{0,1},{1,2},{2,3},{3,4},{4,5},{5,6},{6,7},{7,8},{8,9},{9,10},{10,1... | collective-permute-start | bytes 786440 | tf_op jit(solution)/shard_map/ppermute | solution.py:39
  199.0 12.4 %collective-permute-start.7 = (bf16[8,4,32,128]{3,2,1,0:T(8,128)(2,1)S(1)}, bf16[8,4,32,128]{3,2,1,0:T(8,128)(2,1)S(1)}, u32[]{:S(2)}, u32[]{:S(2)}) collective-permute-start(bf16[8,4,32,128]{3,2,1,0:T(8,128)(2,1)S(1)} %get-tuple-element.31), channel_id=1, source_target_pairs={{1,0},{2,1},{3,2},{4,3},{5,4},{6,5},{7,6},{8,7},{9,8},{10,9},{11,1... | collective-permute-start | bytes 786440 | tf_op jit(solution)/shard_map/ppermute | solution.py:40
  203.5 8.0 %copy-start.3 = (bf16[8,8,32,128]{3,2,1,0:T(8,128)(2,1)S(1)}, bf16[8,8,32,128]{3,2,1,0:T(8,128)(2,1)}, u32[]{:S(2)}) copy-start(bf16[8,8,32,128]{3,2,1,0:T(8,128)(2,1)} %param.6) | copy-start | bytes 1572868
  203.6 8.0 %copy-start.4 = (bf16[8,8,32,128]{3,2,1,0:T(8,128)(2,1)S(1)}, bf16[8,8,32,128]{3,2,1,0:T(8,128)(2,1)}, u32[]{:S(2)}) copy-start(bf16[8,8,32,128]{3,2,1,0:T(8,128)(2,1)} %param.5) | copy-start | bytes 1572868

commit v5 on v4

--- a/solution.py
+++ b/solution.py
@@ -16,7 +16,7 @@
 
 VMEM = pl.BlockSpec(memory_space=pltpu.VMEM)
 SMEM = pl.BlockSpec(memory_space=pltpu.SMEM)
-PARAMS = pltpu.CompilerParams(vmem_limit_bytes=48 * 1024 * 1024)
+PARAMS = pltpu.CompilerParams(vmem_limit_bytes=20 * 1024 * 1024)
 
 
 def call(body, out_shape, *args, specs=None, scratch=(), flops=0, nbytes=0):
@@ -64,28 +64,25 @@
 
 
 def group_table_body(side_ref, members_ref, out_ref):
-    rows = members_ref.shape[0]
-    per = 8
+    groups = members_ref.shape[1]
     high = lax.broadcasted_iota(jnp.int32, (32, 128), 0)
     low = lax.broadcasted_iota(jnp.int32, (128, 128), 0)
     lane = lax.broadcasted_iota(jnp.int32, (1, 128), 1)
     side = side_ref[0]
 
     def step(i, acc):
-        block = members_ref[pl.ds(pl.multiple_of(i * per, per), per), :]
+        block = members_ref[:, pl.ds(pl.multiple_of(i * 128, 128), 128)]
+        group = i * 128 + lane
+        group_high = jnp.broadcast_to((group >> 4).astype(F32), (32, 128))
+        group_low = jnp.broadcast_to((group & 15).astype(F32), (32, 128))
         coarse, fine, lows = [], [], []
-        for j in range(per):
+        for j in range(16):
             entry = block[j : j + 1, :]
             at_high = jnp.where(((entry >> 5) & 1) == side, entry >> 8, -1)
             at_low = ((entry >> 6) & 3) * 32 + (entry & 31)
             on = high == at_high
-            group = (i * per + j) * 8 + (lane >> 4)
-            coarse.append(
-                jnp.where(on, jnp.broadcast_to((group >> 4).astype(F32), (32, 128)), 0.0)
-            )
-            fine.append(
-                jnp.where(on, jnp.broadcast_to((group & 15).astype(F32), (32, 128)), 0.0)
-            )
+            coarse.append(jnp.where(on, group_high, 0.0))
+            fine.append(jnp.where(on, group_low, 0.0))
             lows.append(jnp.where(low == at_low, 1.0, 0.0))
         left = jnp.concatenate(
             [jnp.concatenate(coarse, 1), jnp.concatenate(fine, 1)], 0
@@ -95,7 +92,7 @@
             left, right, (((1,), (1,)), ((), ())), preferred_element_type=F32
         )
 
-    acc = lax.fori_loop(0, rows // per, step, jnp.zeros((64, 128), F32))
+    acc = lax.fori_loop(0, groups // 128, step, jnp.zeros((64, 128), F32))
     out_ref[...] = (acc[:32] * 16.0 + acc[32:]).astype(jnp.int32)
 
 
@@ -535,6 +532,26 @@
     code = ((corners[0] * 128 + corners[1]) * 32 + corners[2]).astype(F32)
     code = jnp.concatenate([jnp.zeros((64,), F32), code]).reshape(1, 128)
 
+    side = (myself // 64).reshape(1)
+    table = call(
+        group_table_body,
+        jax.ShapeDtypeStruct((32, 128), jnp.int32),
+        side,
+        members.T,
+        specs=[SMEM, VMEM],
+        flops=2 * 128 * 32768 * 64,
+        nbytes=1 << 17,
+    )
+    base = jnp.stack([index_x * 8, index_y * 8])
+    offset = jnp.arange(9, dtype=jnp.int32)
+    near_x = index_x + offset // 3 - 1
+    near_y = index_y + offset % 3 - 1
+    exists = (near_x >= 0) & (near_x < 8) & (near_y >= 0) & (near_y < 16)
+    near_id = jnp.where(exists, near_x * 16 + near_y, -1)
+    tau = lax.dynamic_slice_in_dim(thresholds, myself * 16, 16)
+    held, code, table, near_id, tau, base = lax.optimization_barrier(
+        (mixture, code, table, near_id, tau, base)
+    )
     yb, ya = neighbors(mixture, "gy", mixture[:, :margin], mixture[:, 8 - margin :])
     inner_cells, half_grams = call(
         inner_gram_body,
@@ -549,23 +566,12 @@
     )
     wide = jnp.concatenate(
         [
-            jnp.concatenate([yb[:margin], mixture[:margin], ya[:margin]], 1),
-            jnp.concatenate([yb[margin:], mixture[margin:], ya[margin:]], 1),
+            jnp.concatenate([yb[:margin], held[:margin], ya[:margin]], 1),
+            jnp.concatenate([yb[margin:], held[margin:], ya[margin:]], 1),
         ],
         0,
     )
     xb, xa = neighbors(wide, "gx", wide[:margin], wide[8 - margin :])
-    side = (myself // 64).reshape(1)
-    table = call(
-        group_table_body,
-        jax.ShapeDtypeStruct((32, 128), jnp.int32),
-        side,
-        members.reshape(256, 128),
-        specs=[SMEM, VMEM],
-        flops=2 * 128 * 32768 * 64,
-        nbytes=1 << 17,
-    )
-    base = jnp.stack([index_x * 8, index_y * 8])
     cells, grams = call(
         gram_body,
         (jax.ShapeDtypeStruct((8192, 128), F32), jax.ShapeDtypeStruct((128 * 33, 128), F32)),
@@ -581,14 +587,10 @@
         nbytes=10 << 20,
     )
     rows = exchange(grams, 1)
-    offset = jnp.arange(9, dtype=jnp.int32)
-    near_x = index_x + offset // 3 - 1
-    near_y = index_y + offset % 3 - 1
-    exists = (near_x >= 0) & (near_x < 8) & (near_y >= 0) & (near_y < 16)
     sums, near = call(
         group_sum_body,
         (jax.ShapeDtypeStruct((128 * 17, 128), F32), jax.ShapeDtypeStruct((8, 128), F32)),
-        jnp.where(exists, near_x * 16 + near_y, -1),
+        near_id,
         table,
         rows,
         specs=[SMEM, VMEM, VMEM],
@@ -606,7 +608,6 @@
         nbytes=1 << 20,
     )
     mine = exchange(sums, 1)
-    tau = lax.dynamic_slice_in_dim(thresholds, myself * 16, 16)
     factors = call(
         shrink_body,
         jax.ShapeDtypeStruct((128 * 18, 128), BF16),

time: 214 us -> 201 us (0.939)
  blocking collectives: 42.1 us -> 104 us
  waiting for transfers between devices: 47.1 us -> 13.1 us
  starting transfers between devices: 46.5 us -> 25.6 us
  Pallas kernels: 64.8 us -> 50.9 us
  local copies, waits for them, and re-layouts: 7.78 us -> 1.15 us
    all_to_all x2 -> x4, blocking collectives: 42.1 us -> 104 us  [exchange(): rows = lax.all_to_all(rows, BOTH, split_axis=0, concat_axis=0, tiled=True)]
    all_to_all x2 -> x0, waiting for transfers between devices: 32.8 us -> none  [exchange(): rows = lax.all_to_all(rows, BOTH, split_axis=0, concat_axis=0, tiled=True)]
    all_to_all x2 -> x0, starting transfers between devices: 20.9 us -> none  [exchange(): rows = lax.all_to_all(rows, BOTH, split_axis=0, concat_axis=0, tiled=True)]
    pallas_call x9, Pallas kernels: 64.8 us -> 50.9 us  [call(): pl.pallas_call(body, out_shape=out_shape, in_specs=specs or [VMEM] * len(...]
    unnamed x15 -> x8, local copies, waits for them, and re-layouts: 5.12 us -> 0.02 us
  transfers between devices with their start and end apart: 10 -> 8, of which waited for: 8 -> 6; matrix products, arithmetic and copies ran while one was open for 2% -> 1% of each run, Pallas kernels for 10% -> 8%
where the time goes in v5:
time: 201 us; the launch traced here: 200 us
  blocking collectives  104 us (52%)
  Pallas kernels  50.9 us (25%)
  starting transfers between devices  25.6 us (13%)
  waiting for transfers between devices  13.1 us (7%)
  other arithmetic  3.96 us (2%)
    all_to_all x4, blocking collectives, exchange(): rows = lax.all_to_all(rows, BOTH, split_axis=0, concat_axis=0, tiled=True)  104 us
    pallas_call x9, Pallas kernels, call(): pl.pallas_call(body, out_shape=out_shape, in_specs=specs or [VMEM] * len(...  50.9 us
    ppermute x4, starting transfers between devices, neighbors(): before = lax.ppermute(last, axis, up)  14.1 us
    ppermute x4, starting transfers between devices, neighbors(): after = lax.ppermute(first, axis, down)  11.5 us
    ppermute x4, waiting for transfers between devices, neighbors(): after = lax.ppermute(first, axis, down)  9.64 us
  transfers between devices with their start and end apart: 8, of which 6 were waited for; matrix products, arithmetic and copies ran while one was open for 1% of the time, Pallas kernels for 8%

profile of v5, /device:TPU:104, one launch (start us, length us, event | category | flops | bytes accessed | tf_op | source)
XLA Modules:
  0.0 200.1 jit_solution(2017531786023049260)
XLA Ops:
  2.1 2.3 %collective-permute-start.1 = (bf16[8,4,32,128]{3,2,1,0:T(8,128)(2,1)S(1)}, bf16[8,4,32,128]{3,2,1,0:T(8,128)(2,1)S(1)}, u32[]{:S(2)}, u32[]{:S(2)}) collective-permute-start(bf16[8,4,32,128]{3,2,1,0:T(8,128)(2,1)S(1)} %get-tuple-element.46), channel_id=1, source_target_pairs={{1,0},{2,1},{3,2},{4,3},{5,4},{6,5},{7,6},{8,7},{9,8},{10,9},{11,1... | collective-permute-start | bytes 786440 | tf_op jit(solution)/shard_map/ppermute | solution.py:40
  4.4 5.6 %collective-permute-start = (bf16[8,4,32,128]{3,2,1,0:T(8,128)(2,1)S(1)}, bf16[8,4,32,128]{3,2,1,0:T(8,128)(2,1)S(1)}, u32[]{:S(2)}, u32[]{:S(2)}) collective-permute-start(bf16[8,4,32,128]{3,2,1,0:T(8,128)(2,1)S(1)} %get-tuple-element.47), channel_id=1, source_target_pairs={{0,1},{1,2},{2,3},{3,4},{4,5},{5,6},{6,7},{7,8},{8,9},{9,10},{10,1... | collective-permute-start | bytes 786440 | tf_op jit(solution)/shard_map/ppermute | solution.py:39
  10.3 5.0 %shard_map.69.group_ref = s32[32,128]{1,0:T(8,128)S(1)} custom-call(s32[1]{0:T(128)} %bitcast.4.side_ref, s32[16,2048]{1,0:T(8,128)S(1)} %bitcast.36), custom_call_target="tpu_custom_call" | custom-call | flops 536870912 | bytes 131072 | tf_op jit(solution)/shard_map/pallas_call | solution.py:24
  16.2 1.9 collective-permute-start.2
  18.2 3.6 %collective-permute-start.3 = (bf16[4,16,32,128]{3,2,1,0:T(8,128)(2,1)S(1)}, bf16[4,16,32,128]{3,2,1,0:T(8,128)(2,1)S(1)}, u32[]{:S(2)}, u32[]{:S(2)}) collective-permute-start(bf16[4,16,32,128]{3,2,1,0:T(8,128)(2,1)S(1)} %pad_maximum_fusion.2), channel_id=1, source_target_pairs={{16,0},{32,16},{48,32},{64,48},{80,64},{96,80},{112,96},{17,1},{33... | collective-permute-start | bytes 1572872 | tf_op jit(solution)/shard_map/ppermute | solution.py:40
  21.9 3.6 %shard_map.68 = (f32[4096,128]{1,0:T(8,128)S(1)}, f32[64,128,128]{2,1,0:T(8,128)S(1)}) custom-call(s32[64]{0:T(128)S(1)} %get-tuple-element.36.first_ref, bf16[8,8,32,128]{3,2,1,0:T(8,128)(2,1)S(1)} %fusion.3.own_ref, bf16[8,4,32,128]{3,2,1,0:T(8,128)(2,1)S(1)} %collective-permute-done.yb_ref, bf16[8,4,32,128]{3,2,1,0:T(8,128)(2,1)S(1)} %collective-permute-done.1.ya_ref), custom_call_target="tpu_custom_call" | custom-call | flops 536870912 | bytes 8388608 | tf_op jit(solution)/shard_map/pallas_call | solution.py:24
  26.7 1.8 collective-permute-done.3.xa_ref
  28.6 4.4 %shard_map.70 = (f32[8192,128]{1,0:T(8,128)S(1)}, f32[4224,128]{1,0:T(8,128)S(1)}) custom-call(s32[64]{0:T(128)S(1)} %get-tuple-element.52.first_ref, f32[1,128]{1,0:T(1,128)S(1)} %pad_bitcast_fusion.code_ref, f32[4096,128]{1,0:T(8,128)S(1)} %get-tuple-element.18.inner_ref.cells_ref, bf16[4,16,32,128]{3,2,1,0:T(8,128)(2,1)S(1)} %collective-permute-done.2.xb_ref, ...), custom_call_target="tpu_custom_call" | custom-call | flops 536870912 | bytes 10485760 | tf_op jit(solution)/shard_map/pallas_call | solution.py:24
  33.0 38.5 %all_to_all.20 = f32[128,33,1,128]{3,2,1,0:T(1,128)S(1)} all-to-all(f32[128,33,1,128]{3,2,1,0:T(1,128)S(1)} %bitcast.26), channel_id=1, replica_groups=mesh['gx'=8,'gy'=16] {'gx','gy'}, dimensions={0} | all-to-all | bytes 4325376 | tf_op jit(solution)/shard_map/all_to_all | solution.py:515
  71.5 7.7 %shard_map.71 = (f32[2176,128]{1,0:T(8,128)S(1)}, f32[8,128]{1,0:T(8,128)S(1)}) custom-call(s32[9]{0:T(128)S(1)} %and_select_fusion.near_id_ref, s32[32,128]{1,0:T(8,128)S(1)} %shard_map.69.group_ref, f32[4224,128]{1,0:T(8,128)S(1)} %bitcast.27), custom_call_target="tpu_custom_call" | custom-call | flops 4294967296 | bytes 5242880 | tf_op jit(solution)/shard_map/pallas_call | solution.py:24
  79.2 23.7 %all_to_all.21 = f32[128,17,1,128]{3,2,1,0:T(1,128)S(1)} all-to-all(f32[128,17,1,128]{3,2,1,0:T(1,128)S(1)} %bitcast.28), channel_id=1, replica_groups=mesh['gx'=8,'gy'=16] {'gx','gy'}, dimensions={0} | all-to-all | bytes 2228224 | tf_op jit(solution)/shard_map/all_to_all | solution.py:515
  103.0 13.0 %shard_map.72 = bf16[2304,128]{1,0:T(8,128)(2,1)S(1)} custom-call(f32[16]{0:T(128)S(1)} %dynamic_slice.3.tau_ref, f32[2176,128]{1,0:T(8,128)S(1)} %bitcast.29), custom_call_target="tpu_custom_call" | custom-call | flops 3221225472 | bytes 2097152 | tf_op jit(solution)/shard_map/pallas_call | solution.py:24
  115.9 18.2 %all_to_all.22 = bf16[128,9,2,128]{3,2,1,0:T(2,128)(2,1)S(1)} all-to-all(bf16[128,9,2,128]{3,2,1,0:T(2,128)(2,1)S(1)} %bitcast.32), channel_id=1, replica_groups=mesh['gx'=8,'gy'=16] {'gx','gy'}, dimensions={0} | all-to-all | bytes 1179648 | tf_op jit(solution)/shard_map/all_to_all | solution.py:515
  134.1 3.6 %shard_map.73 = bf16[4352,128]{1,0:T(8,128)(2,1)S(1)} custom-call(s32[32,128]{1,0:T(8,128)S(1)} %shard_map.69.group_ref, bf16[2304,128]{1,0:T(8,128)(2,1)S(1)} %bitcast.33), custom_call_target="tpu_custom_call" | custom-call | flops 4294967296 | bytes 3145728 | tf_op jit(solution)/shard_map/pallas_call | solution.py:24
  137.7 24.0 %all_to_all.23 = bf16[128,17,2,128]{3,2,1,0:T(2,128)(2,1)S(1)} all-to-all(bf16[128,17,2,128]{3,2,1,0:T(2,128)(2,1)S(1)} %bitcast.30), channel_id=1, replica_groups=mesh['gx'=8,'gy'=16] {'gx','gy'}, dimensions={0} | all-to-all | bytes 2228224 | tf_op jit(solution)/shard_map/all_to_all | solution.py:515
  161.7 6.8 %shard_map.74 = (f32[4096,128]{1,0:T(8,128)S(1)}, bf16[2048,128]{1,0:T(8,128)(2,1)S(1)}, bf16[2048,128]{1,0:T(8,128)(2,1)S(1)}, bf16[64,128,128]{2,1,0:T(8,128)(2,1)S(1)}) custom-call(s32[64]{0:T(128)S(1)} %get-tuple-element.52.first_ref, f32[8192,128]{1,0:T(8,128)S(1)} %get-tuple-element.22.cells_ref, bf16[4352,128]{1,0:T(8,128)(2,1)S(1)} %bitcast.25), custom_call_target="tpu_custom_call" | custom-call | flops 536870912 | bytes 10485760 | tf_op jit(solution)/shard_map/pallas_call | solution.py:24
  168.5 1.9 collective-permute-start.4
  170.4 3.6 %collective-permute-start.5 = (bf16[4,16,32,128]{3,2,1,0:T(8,128)(2,1)S(1)}, bf16[4,16,32,128]{3,2,1,0:T(8,128)(2,1)S(1)}, u32[]{:S(2)}, u32[]{:S(2)}) collective-permute-start(bf16[4,16,32,128]{3,2,1,0:T(8,128)(2,1)S(1)} %bitcast.34), channel_id=1, source_target_pairs={{16,0},{32,16},{48,32},{64,48},{80,64},{96,80},{112,96},{17,1},{33... | collective-permute-start | bytes 1572872 | tf_op jit(solution)/shard_map/ppermute | solution.py:40
  174.1 4.2 %shard_map.75 = f32[4096,128]{1,0:T(8,128)S(1)} custom-call(s32[64]{0:T(128)S(1)} %get-tuple-element.36.first_ref, f32[4096,128]{1,0:T(8,128)S(1)} %get-tuple-element.18.inner_ref.cells_ref, bf16[64,128,128]{2,1,0:T(8,128)(2,1)S(1)} %get-tuple-element.28.factor_ref, f32[4096,128]{1,0:T(8,128)S(1)} %get-tuple-element.29.start_ref), custom_call_target="tpu_custom_call" | custom-call | flops 536870912 | bytes 8388608 | tf_op jit(solution)/shard_map/pallas_call | solution.py:24
  181.1 4.6 %collective-permute-start.6 = (bf16[8,4,32,128]{3,2,1,0:T(8,128)(2,1)S(1)}, bf16[8,4,32,128]{3,2,1,0:T(8,128)(2,1)S(1)}, u32[]{:S(2)}, u32[]{:S(2)}) collective-permute-start(bf16[8,4,32,128]{3,2,1,0:T(8,128)(2,1)S(1)} %get-tuple-element.42), channel_id=1, source_target_pairs={{0,1},{1,2},{2,3},{3,4},{4,5},{5,6},{6,7},{7,8},{8,9},{9,10},{10,1... | collective-permute-start | bytes 786440 | tf_op jit(solution)/shard_map/ppermute | solution.py:39
  185.8 1.9 collective-permute-start.7
  187.7 2.6 %shard_map.76 = f32[2048,128]{1,0:T(8,128)S(1)} custom-call(f32[8,128]{1,0:T(8,128)S(1)} %get-tuple-element.32.near_ref, s32[2]{0:T(128)S(1)} %pad_add_fusion.base_ref), custom_call_target="tpu_custom_call" | custom-call | flops 335544320 | bytes 1048576 | tf_op jit(solution)/shard_map/pallas_call | solution.py:24
  191.9 6.2 %collective-permute-done.7 = bf16[8,4,32,128]{3,2,1,0:T(8,128)(2,1)S(1)} collective-permute-done((bf16[8,4,32,128]{3,2,1,0:T(8,128)(2,1)S(1)}, bf16[8,4,32,128]{3,2,1,0:T(8,128)(2,1)S(1)}, u32[]{:S(2)}, u32[]{:S(2)}) %collective-permute-start.7) | collective-permute-done | bytes 262176 | tf_op jit(solution)/shard_map/ppermute | solution.py:40
  198.3 1.7 fusion.2
  (33 shorter events, 8.4 us)
Async XLA Ops:
  0.6 9.5 %copy-start.3 = (s32[3,64]{1,0:T(4,128)S(1)}, s32[3,64]{1,0:T(4,128)}, u32[]{:S(2)}) copy-start(s32[3,64]{1,0:T(4,128)} %param.7) | copy-start | bytes 2308
  0.6 9.6 %copy-start = (s32[2048,16]{0,1:T(8,128)S(1)}, s32[2048,16]{0,1:T(8,128)}, u32[]{:S(2)}) copy-start(s32[2048,16]{0,1:T(8,128)} %param.8) | copy-start | bytes 393220
  2.1 14.0 %collective-permute-start.1 = (bf16[8,4,32,128]{3,2,1,0:T(8,128)(2,1)S(1)}, bf16[8,4,32,128]{3,2,1,0:T(8,128)(2,1)S(1)}, u32[]{:S(2)}, u32[]{:S(2)}) collective-permute-start(bf16[8,4,32,128]{3,2,1,0:T(8,128)(2,1)S(1)} %get-tuple-element.46), channel_id=1, source_target_pairs={{1,0},{2,1},{3,2},{4,3},{5,4},{6,5},{7,6},{8,7},{9,8},{10,9},{11,1... | collective-permute-start | bytes 786440 | tf_op jit(solution)/shard_map/ppermute | solution.py:40
  4.4 11.7 %collective-permute-start = (bf16[8,4,32,128]{3,2,1,0:T(8,128)(2,1)S(1)}, bf16[8,4,32,128]{3,2,1,0:T(8,128)(2,1)S(1)}, u32[]{:S(2)}, u32[]{:S(2)}) collective-permute-start(bf16[8,4,32,128]{3,2,1,0:T(8,128)(2,1)S(1)} %get-tuple-element.47), channel_id=1, source_target_pairs={{0,1},{1,2},{2,3},{3,4},{4,5},{5,6},{6,7},{7,8},{8,9},{9,10},{10,1... | collective-permute-start | bytes 786440 | tf_op jit(solution)/shard_map/ppermute | solution.py:39
  16.2 10.5 %collective-permute-start.2 = (bf16[4,16,32,128]{3,2,1,0:T(8,128)(2,1)S(1)}, bf16[4,16,32,128]{3,2,1,0:T(8,128)(2,1)S(1)}, u32[]{:S(2)}, u32[]{:S(2)}) collective-permute-start(bf16[4,16,32,128]{3,2,1,0:T(8,128)(2,1)S(1)} %pad_maximum_fusion.1), channel_id=1, source_target_pairs={{0,16},{16,32},{32,48},{48,64},{64,80},{80,96},{96,112},{1,17},{17... | collective-permute-start | bytes 1572872 | tf_op jit(solution)/shard_map/ppermute | solution.py:39
  18.2 10.3 %collective-permute-start.3 = (bf16[4,16,32,128]{3,2,1,0:T(8,128)(2,1)S(1)}, bf16[4,16,32,128]{3,2,1,0:T(8,128)(2,1)S(1)}, u32[]{:S(2)}, u32[]{:S(2)}) collective-permute-start(bf16[4,16,32,128]{3,2,1,0:T(8,128)(2,1)S(1)} %pad_maximum_fusion.2), channel_id=1, source_target_pairs={{16,0},{32,16},{48,32},{64,48},{80,64},{96,80},{112,96},{17,1},{33... | collective-permute-start | bytes 1572872 | tf_op jit(solution)/shard_map/ppermute | solution.py:40
  168.5 10.5 %collective-permute-start.4 = (bf16[4,16,32,128]{3,2,1,0:T(8,128)(2,1)S(1)}, bf16[4,16,32,128]{3,2,1,0:T(8,128)(2,1)S(1)}, u32[]{:S(2)}, u32[]{:S(2)}) collective-permute-start(bf16[4,16,32,128]{3,2,1,0:T(8,128)(2,1)S(1)} %bitcast.35), channel_id=1, source_target_pairs={{0,16},{16,32},{32,48},{48,64},{64,80},{80,96},{96,112},{1,17},{17... | collective-permute-start | bytes 1572872 | tf_op jit(solution)/shard_map/ppermute | solution.py:39
  170.4 10.3 %collective-permute-start.5 = (bf16[4,16,32,128]{3,2,1,0:T(8,128)(2,1)S(1)}, bf16[4,16,32,128]{3,2,1,0:T(8,128)(2,1)S(1)}, u32[]{:S(2)}, u32[]{:S(2)}) collective-permute-start(bf16[4,16,32,128]{3,2,1,0:T(8,128)(2,1)S(1)} %bitcast.34), channel_id=1, source_target_pairs={{16,0},{32,16},{48,32},{64,48},{80,64},{96,80},{112,96},{17,1},{33... | collective-permute-start | bytes 1572872 | tf_op jit(solution)/shard_map/ppermute | solution.py:40
  181.1 10.8 %collective-permute-start.6 = (bf16[8,4,32,128]{3,2,1,0:T(8,128)(2,1)S(1)}, bf16[8,4,32,128]{3,2,1,0:T(8,128)(2,1)S(1)}, u32[]{:S(2)}, u32[]{:S(2)}) collective-permute-start(bf16[8,4,32,128]{3,2,1,0:T(8,128)(2,1)S(1)} %get-tuple-element.42), channel_id=1, source_target_pairs={{0,1},{1,2},{2,3},{3,4},{4,5},{5,6},{6,7},{7,8},{8,9},{9,10},{10,1... | collective-permute-start | bytes 786440 | tf_op jit(solution)/shard_map/ppermute | solution.py:39
  185.8 12.4 %collective-permute-start.7 = (bf16[8,4,32,128]{3,2,1,0:T(8,128)(2,1)S(1)}, bf16[8,4,32,128]{3,2,1,0:T(8,128)(2,1)S(1)}, u32[]{:S(2)}, u32[]{:S(2)}) collective-permute-start(bf16[8,4,32,128]{3,2,1,0:T(8,128)(2,1)S(1)} %get-tuple-element.43), channel_id=1, source_target_pairs={{1,0},{2,1},{3,2},{4,3},{5,4},{6,5},{7,6},{8,7},{9,8},{10,9},{11,1... | collective-permute-start | bytes 786440 | tf_op jit(solution)/shard_map/ppermute | solution.py:40
  190.3 8.1 %copy-start.1 = (bf16[8,8,32,128]{3,2,1,0:T(8,128)(2,1)S(1)}, bf16[8,8,32,128]{3,2,1,0:T(8,128)(2,1)}, u32[]{:S(2)}) copy-start(bf16[8,8,32,128]{3,2,1,0:T(8,128)(2,1)} %param.6) | copy-start | bytes 1572868
  190.3 8.1 %copy-start.2 = (bf16[8,8,32,128]{3,2,1,0:T(8,128)(2,1)S(1)}, bf16[8,8,32,128]{3,2,1,0:T(8,128)(2,1)}, u32[]{:S(2)}) copy-start(bf16[8,8,32,128]{3,2,1,0:T(8,128)(2,1)} %param.5) | copy-start | bytes 1572868

commit v6 on v5

--- a/solution.py
+++ b/solution.py
@@ -146,7 +146,7 @@
         gram_ref[p] = half_gram(cells_ref, first_ref[p])
         return 0
 
-    lax.fori_loop(0, 64, patch, 0, unroll=8)
+    lax.fori_loop(0, 64, patch, 0, unroll=16)
 
 
 def gram_body(
@@ -165,7 +165,7 @@
         diag_ref[pl.ds(p, 1), :] = jnp.sum(rest, axis=0, keepdims=True)
         return 0
 
-    lax.fori_loop(0, 64, patch, 0, unroll=8)
+    lax.fori_loop(0, 64, patch, 0, unroll=16)
     left = lax.broadcasted_iota(jnp.int32, (64, 128), 1) < 64
     turned = diag_ref[...].T[64:]
     out_ref[pl.ds(32, 64, stride=33), :] = jnp.where(left, turned, code_ref[...])
@@ -204,23 +204,34 @@
     lax.fori_loop(0, 128, split, 0, unroll=8)
     one = jnp.ones((128, 128), BF16)
     zero = jnp.zeros((128, 128), BF16)
-    sub = lax.broadcasted_iota(jnp.int32, (128, 128), 0)
-    sub16 = sub.astype(F32).astype(BF16)
+    sub16 = lax.broadcasted_iota(jnp.int32, (128, 128), 0).astype(F32).astype(BF16)
 
     used = lax.broadcasted_iota(jnp.int32, (32, 128), 1) < 32
     diagonal = jnp.zeros((32, 128), F32)
     for c in range(4):
         part = jnp.where(used, rows_ref[pl.ds(32 + 33 * c, 32, stride=132), :], 0.0)
         diagonal = diagonal + (pltpu.roll(part, 32 * c, axis=1) if c else part)
+    diagonal_high = diagonal.astype(BF16)
+    diagonal_low = (diagonal - diagonal_high.astype(F32)).astype(BF16)
     group = group_ref[...]
-    owner, place = group >> 4, (group & 15).astype(F32).astype(BF16)
+    owner, place = (group >> 4).astype(F32).astype(BF16), (group & 15).astype(F32).astype(BF16)
     left, right = [], []
+
+    def rows_of(x, t):
+        return jnp.broadcast_to(x[t : t + 1, :], (128, 128))
+
     for t in range(32):
-        value = jnp.where(sub == owner[t : t + 1, :], diagonal[t : t + 1, :], 0.0)
-        high = value.astype(BF16)
-        left.append(jnp.concatenate([high, (value - high.astype(F32)).astype(BF16)], 0))
-        spot = jnp.broadcast_to(place[t : t + 1, :], (128, 128))
-        right.append(jnp.where(sub16 == spot, one, zero))
+        on = sub16 == rows_of(owner, t)
+        left.append(
+            jnp.concatenate(
+                [
+                    jnp.where(on, rows_of(diagonal_high, t), zero),
+                    jnp.where(on, rows_of(diagonal_low, t), zero),
+                ],
+                0,
+            )
+        )
+        right.append(jnp.where(sub16 == rows_of(place, t), one, zero))
     extra = lax.dot_general(
         jnp.concatenate(left, 1),
         jnp.concatenate(right, 1),
@@ -448,11 +459,15 @@
     def accumulate(p, ref):
         for k in range(count):
             first = first_ref[p + k]
+            spots, sums = [], []
             for a in range(PATCH // 2):
                 for b in range(PATCH):
                     at = pl.ds(first + (a * 16 + b) * 32, PATCH)
                     row = k * 256 + (a * PATCH + b) * PATCH
-                    sum_ref[at, :] += ref[row : row + PATCH, :]
+                    spots.append(at)
+                    sums.append(sum_ref[at, :] + ref[row : row + PATCH, :])
+            for at, value in zip(spots, sums):
+                sum_ref[at, :] = value
 
     def several(i, _):
         p = i * (2 * count)

time: 201 us -> 199 us (0.990)
  Pallas kernels: 50.9 us -> 48.6 us
    pallas_call x9, Pallas kernels: 50.9 us -> 48.6 us  [call(): pl.pallas_call(body, out_shape=out_shape, in_specs=specs or [VMEM] * len(...]
  transfers between devices with their start and end apart: 8 -> 8, of which waited for: 6 -> 6; matrix products, arithmetic and copies ran while one was open for 1% -> 1% of each run, Pallas kernels for 8% -> 7%
where the time goes in v6:
time: 199 us
  blocking collectives  104 us (52%)
  Pallas kernels  48.6 us (24%)
  starting transfers between devices  25.6 us (13%)
  waiting for transfers between devices  14 us (7%)
  other arithmetic  3.96 us (2%)
    all_to_all x4, blocking collectives, exchange(): rows = lax.all_to_all(rows, BOTH, split_axis=0, concat_axis=0, tiled=True)  104 us
    pallas_call x9, Pallas kernels, call(): pl.pallas_call(body, out_shape=out_shape, in_specs=specs or [VMEM] * len(...  48.6 us
    ppermute x4, starting transfers between devices, neighbors(): before = lax.ppermute(last, axis, up)  14.1 us
    ppermute x4, starting transfers between devices, neighbors(): after = lax.ppermute(first, axis, down)  11.5 us
    ppermute x4, waiting for transfers between devices, neighbors(): after = lax.ppermute(first, axis, down)  9.64 us
    ppermute x4, waiting for transfers between devices, neighbors(): before = lax.ppermute(last, axis, up)  4.34 us
  transfers between devices with their start and end apart: 8, of which 6 were waited for; matrix products, arithmetic and copies ran while one was open for 1% of the time, Pallas kernels for 7%

profile of v6, /device:TPU:104, one launch (start us, length us, event | category | flops | bytes accessed | tf_op | source)
XLA Modules:
  0.0 198.7 jit_solution(3631321365727197376)
XLA Ops:
  2.1 2.3 %collective-permute-start.1 = (bf16[8,4,32,128]{3,2,1,0:T(8,128)(2,1)S(1)}, bf16[8,4,32,128]{3,2,1,0:T(8,128)(2,1)S(1)}, u32[]{:S(2)}, u32[]{:S(2)}) collective-permute-start(bf16[8,4,32,128]{3,2,1,0:T(8,128)(2,1)S(1)} %get-tuple-element.46), channel_id=1, source_target_pairs={{1,0},{2,1},{3,2},{4,3},{5,4},{6,5},{7,6},{8,7},{9,8},{10,9},{11,1... | collective-permute-start | bytes 786440 | tf_op jit(solution)/shard_map/ppermute | solution.py:40
  4.4 5.6 %collective-permute-start = (bf16[8,4,32,128]{3,2,1,0:T(8,128)(2,1)S(1)}, bf16[8,4,32,128]{3,2,1,0:T(8,128)(2,1)S(1)}, u32[]{:S(2)}, u32[]{:S(2)}) collective-permute-start(bf16[8,4,32,128]{3,2,1,0:T(8,128)(2,1)S(1)} %get-tuple-element.47), channel_id=1, source_target_pairs={{0,1},{1,2},{2,3},{3,4},{4,5},{5,6},{6,7},{7,8},{8,9},{9,10},{10,1... | collective-permute-start | bytes 786440 | tf_op jit(solution)/shard_map/ppermute | solution.py:39
  10.3 5.0 %shard_map.69.group_ref = s32[32,128]{1,0:T(8,128)S(1)} custom-call(s32[1]{0:T(128)} %bitcast.4.side_ref, s32[16,2048]{1,0:T(8,128)S(1)} %bitcast.36), custom_call_target="tpu_custom_call" | custom-call | flops 536870912 | bytes 131072 | tf_op jit(solution)/shard_map/pallas_call | solution.py:24
  16.2 1.9 collective-permute-start.2
  18.2 3.6 %collective-permute-start.3 = (bf16[4,16,32,128]{3,2,1,0:T(8,128)(2,1)S(1)}, bf16[4,16,32,128]{3,2,1,0:T(8,128)(2,1)S(1)}, u32[]{:S(2)}, u32[]{:S(2)}) collective-permute-start(bf16[4,16,32,128]{3,2,1,0:T(8,128)(2,1)S(1)} %pad_maximum_fusion.2), channel_id=1, source_target_pairs={{16,0},{32,16},{48,32},{64,48},{80,64},{96,80},{112,96},{17,1},{33... | collective-permute-start | bytes 1572872 | tf_op jit(solution)/shard_map/ppermute | solution.py:40
  21.9 2.7 %shard_map.68 = (f32[4096,128]{1,0:T(8,128)S(1)}, f32[64,128,128]{2,1,0:T(8,128)S(1)}) custom-call(s32[64]{0:T(128)S(1)} %get-tuple-element.36.first_ref, bf16[8,8,32,128]{3,2,1,0:T(8,128)(2,1)S(1)} %fusion.3.own_ref, bf16[8,4,32,128]{3,2,1,0:T(8,128)(2,1)S(1)} %collective-permute-done.yb_ref, bf16[8,4,32,128]{3,2,1,0:T(8,128)(2,1)S(1)} %collective-permute-done.1.ya_ref), custom_call_target="tpu_custom_call" | custom-call | flops 536870912 | bytes 8388608 | tf_op jit(solution)/shard_map/pallas_call | solution.py:24
  24.6 2.2 %collective-permute-done.2.xb_ref = bf16[4,16,32,128]{3,2,1,0:T(8,128)(2,1)S(1)} collective-permute-done((bf16[4,16,32,128]{3,2,1,0:T(8,128)(2,1)S(1)}, bf16[4,16,32,128]{3,2,1,0:T(8,128)(2,1)S(1)}, u32[]{:S(2)}, u32[]{:S(2)}) %collective-permute-start.2) | collective-permute-done | bytes 524320 | tf_op jit(solution)/shard_map/ppermute | solution.py:39
  26.7 1.8 collective-permute-done.3.xa_ref
  28.6 3.3 %shard_map.70 = (f32[8192,128]{1,0:T(8,128)S(1)}, f32[4224,128]{1,0:T(8,128)S(1)}) custom-call(s32[64]{0:T(128)S(1)} %get-tuple-element.52.first_ref, f32[1,128]{1,0:T(1,128)S(1)} %pad_bitcast_fusion.code_ref, f32[4096,128]{1,0:T(8,128)S(1)} %get-tuple-element.18.inner_ref.cells_ref, bf16[4,16,32,128]{3,2,1,0:T(8,128)(2,1)S(1)} %collective-permute-done.2.xb_ref, ...), custom_call_target="tpu_custom_call" | custom-call | flops 536870912 | bytes 10485760 | tf_op jit(solution)/shard_map/pallas_call | solution.py:24
  31.8 38.5 %all_to_all.20 = f32[128,33,1,128]{3,2,1,0:T(1,128)S(1)} all-to-all(f32[128,33,1,128]{3,2,1,0:T(1,128)S(1)} %bitcast.26), channel_id=1, replica_groups=mesh['gx'=8,'gy'=16] {'gx','gy'}, dimensions={0} | all-to-all | bytes 4325376 | tf_op jit(solution)/shard_map/all_to_all | solution.py:530
  70.4 7.5 %shard_map.71 = (f32[2176,128]{1,0:T(8,128)S(1)}, f32[8,128]{1,0:T(8,128)S(1)}) custom-call(s32[9]{0:T(128)S(1)} %and_select_fusion.near_id_ref, s32[32,128]{1,0:T(8,128)S(1)} %shard_map.69.group_ref, f32[4224,128]{1,0:T(8,128)S(1)} %bitcast.27), custom_call_target="tpu_custom_call" | custom-call | flops 4294967296 | bytes 5242880 | tf_op jit(solution)/shard_map/pallas_call | solution.py:24
  77.8 23.7 %all_to_all.21 = f32[128,17,1,128]{3,2,1,0:T(1,128)S(1)} all-to-all(f32[128,17,1,128]{3,2,1,0:T(1,128)S(1)} %bitcast.28), channel_id=1, replica_groups=mesh['gx'=8,'gy'=16] {'gx','gy'}, dimensions={0} | all-to-all | bytes 2228224 | tf_op jit(solution)/shard_map/all_to_all | solution.py:530
  101.6 13.0 %shard_map.72 = bf16[2304,128]{1,0:T(8,128)(2,1)S(1)} custom-call(f32[16]{0:T(128)S(1)} %dynamic_slice.3.tau_ref, f32[2176,128]{1,0:T(8,128)S(1)} %bitcast.29), custom_call_target="tpu_custom_call" | custom-call | flops 3221225472 | bytes 2097152 | tf_op jit(solution)/shard_map/pallas_call | solution.py:24
  114.5 18.2 %all_to_all.22 = bf16[128,9,2,128]{3,2,1,0:T(2,128)(2,1)S(1)} all-to-all(bf16[128,9,2,128]{3,2,1,0:T(2,128)(2,1)S(1)} %bitcast.32), channel_id=1, replica_groups=mesh['gx'=8,'gy'=16] {'gx','gy'}, dimensions={0} | all-to-all | bytes 1179648 | tf_op jit(solution)/shard_map/all_to_all | solution.py:530
  132.7 3.6 %shard_map.73 = bf16[4352,128]{1,0:T(8,128)(2,1)S(1)} custom-call(s32[32,128]{1,0:T(8,128)S(1)} %shard_map.69.group_ref, bf16[2304,128]{1,0:T(8,128)(2,1)S(1)} %bitcast.33), custom_call_target="tpu_custom_call" | custom-call | flops 4294967296 | bytes 3145728 | tf_op jit(solution)/shard_map/pallas_call | solution.py:24
  136.3 24.0 %all_to_all.23 = bf16[128,17,2,128]{3,2,1,0:T(2,128)(2,1)S(1)} all-to-all(bf16[128,17,2,128]{3,2,1,0:T(2,128)(2,1)S(1)} %bitcast.30), channel_id=1, replica_groups=mesh['gx'=8,'gy'=16] {'gx','gy'}, dimensions={0} | all-to-all | bytes 2228224 | tf_op jit(solution)/shard_map/all_to_all | solution.py:530
  160.3 6.9 %shard_map.74 = (f32[4096,128]{1,0:T(8,128)S(1)}, bf16[2048,128]{1,0:T(8,128)(2,1)S(1)}, bf16[2048,128]{1,0:T(8,128)(2,1)S(1)}, bf16[64,128,128]{2,1,0:T(8,128)(2,1)S(1)}) custom-call(s32[64]{0:T(128)S(1)} %get-tuple-element.52.first_ref, f32[8192,128]{1,0:T(8,128)S(1)} %get-tuple-element.22.cells_ref, bf16[4352,128]{1,0:T(8,128)(2,1)S(1)} %bitcast.25), custom_call_target="tpu_custom_call" | custom-call | flops 536870912 | bytes 10485760 | tf_op jit(solution)/shard_map/pallas_call | solution.py:24
  167.2 1.9 collective-permute-start.4
  169.1 3.6 %collective-permute-start.5 = (bf16[4,16,32,128]{3,2,1,0:T(8,128)(2,1)S(1)}, bf16[4,16,32,128]{3,2,1,0:T(8,128)(2,1)S(1)}, u32[]{:S(2)}, u32[]{:S(2)}) collective-permute-start(bf16[4,16,32,128]{3,2,1,0:T(8,128)(2,1)S(1)} %bitcast.34), channel_id=1, source_target_pairs={{16,0},{32,16},{48,32},{64,48},{80,64},{96,80},{112,96},{17,1},{33... | collective-permute-start | bytes 1572872 | tf_op jit(solution)/shard_map/ppermute | solution.py:40
  172.7 4.2 %shard_map.75 = f32[4096,128]{1,0:T(8,128)S(1)} custom-call(s32[64]{0:T(128)S(1)} %get-tuple-element.36.first_ref, f32[4096,128]{1,0:T(8,128)S(1)} %get-tuple-element.18.inner_ref.cells_ref, bf16[64,128,128]{2,1,0:T(8,128)(2,1)S(1)} %get-tuple-element.28.factor_ref, f32[4096,128]{1,0:T(8,128)S(1)} %get-tuple-element.29.start_ref), custom_call_target="tpu_custom_call" | custom-call | flops 536870912 | bytes 8388608 | tf_op jit(solution)/shard_map/pallas_call | solution.py:24
  179.8 4.6 %collective-permute-start.6 = (bf16[8,4,32,128]{3,2,1,0:T(8,128)(2,1)S(1)}, bf16[8,4,32,128]{3,2,1,0:T(8,128)(2,1)S(1)}, u32[]{:S(2)}, u32[]{:S(2)}) collective-permute-start(bf16[8,4,32,128]{3,2,1,0:T(8,128)(2,1)S(1)} %get-tuple-element.42), channel_id=1, source_target_pairs={{0,1},{1,2},{2,3},{3,4},{4,5},{5,6},{6,7},{7,8},{8,9},{9,10},{10,1... | collective-permute-start | bytes 786440 | tf_op jit(solution)/shard_map/ppermute | solution.py:39
  184.4 1.9 collective-permute-start.7
  186.3 2.6 %shard_map.76 = f32[2048,128]{1,0:T(8,128)S(1)} custom-call(f32[8,128]{1,0:T(8,128)S(1)} %get-tuple-element.32.near_ref, s32[2]{0:T(128)S(1)} %pad_add_fusion.base_ref), custom_call_target="tpu_custom_call" | custom-call | flops 335544320 | bytes 1048576 | tf_op jit(solution)/shard_map/pallas_call | solution.py:24
  190.5 6.2 %collective-permute-done.7 = bf16[8,4,32,128]{3,2,1,0:T(8,128)(2,1)S(1)} collective-permute-done((bf16[8,4,32,128]{3,2,1,0:T(8,128)(2,1)S(1)}, bf16[8,4,32,128]{3,2,1,0:T(8,128)(2,1)S(1)}, u32[]{:S(2)}, u32[]{:S(2)}) %collective-permute-start.7) | collective-permute-done | bytes 262176 | tf_op jit(solution)/shard_map/ppermute | solution.py:40
  (33 shorter events, 8.9 us)
Async XLA Ops:
  0.6 9.5 %copy-start.3 = (s32[3,64]{1,0:T(4,128)S(1)}, s32[3,64]{1,0:T(4,128)}, u32[]{:S(2)}) copy-start(s32[3,64]{1,0:T(4,128)} %param.7) | copy-start | bytes 2308
  0.6 9.6 %copy-start = (s32[2048,16]{0,1:T(8,128)S(1)}, s32[2048,16]{0,1:T(8,128)}, u32[]{:S(2)}) copy-start(s32[2048,16]{0,1:T(8,128)} %param.8) | copy-start | bytes 393220
  2.1 14.0 %collective-permute-start.1 = (bf16[8,4,32,128]{3,2,1,0:T(8,128)(2,1)S(1)}, bf16[8,4,32,128]{3,2,1,0:T(8,128)(2,1)S(1)}, u32[]{:S(2)}, u32[]{:S(2)}) collective-permute-start(bf16[8,4,32,128]{3,2,1,0:T(8,128)(2,1)S(1)} %get-tuple-element.46), channel_id=1, source_target_pairs={{1,0},{2,1},{3,2},{4,3},{5,4},{6,5},{7,6},{8,7},{9,8},{10,9},{11,1... | collective-permute-start | bytes 786440 | tf_op jit(solution)/shard_map/ppermute | solution.py:40
  4.4 11.7 %collective-permute-start = (bf16[8,4,32,128]{3,2,1,0:T(8,128)(2,1)S(1)}, bf16[8,4,32,128]{3,2,1,0:T(8,128)(2,1)S(1)}, u32[]{:S(2)}, u32[]{:S(2)}) collective-permute-start(bf16[8,4,32,128]{3,2,1,0:T(8,128)(2,1)S(1)} %get-tuple-element.47), channel_id=1, source_target_pairs={{0,1},{1,2},{2,3},{3,4},{4,5},{5,6},{6,7},{7,8},{8,9},{9,10},{10,1... | collective-permute-start | bytes 786440 | tf_op jit(solution)/shard_map/ppermute | solution.py:39
  16.2 10.5 %collective-permute-start.2 = (bf16[4,16,32,128]{3,2,1,0:T(8,128)(2,1)S(1)}, bf16[4,16,32,128]{3,2,1,0:T(8,128)(2,1)S(1)}, u32[]{:S(2)}, u32[]{:S(2)}) collective-permute-start(bf16[4,16,32,128]{3,2,1,0:T(8,128)(2,1)S(1)} %pad_maximum_fusion.1), channel_id=1, source_target_pairs={{0,16},{16,32},{32,48},{48,64},{64,80},{80,96},{96,112},{1,17},{17... | collective-permute-start | bytes 1572872 | tf_op jit(solution)/shard_map/ppermute | solution.py:39
  18.2 10.3 %collective-permute-start.3 = (bf16[4,16,32,128]{3,2,1,0:T(8,128)(2,1)S(1)}, bf16[4,16,32,128]{3,2,1,0:T(8,128)(2,1)S(1)}, u32[]{:S(2)}, u32[]{:S(2)}) collective-permute-start(bf16[4,16,32,128]{3,2,1,0:T(8,128)(2,1)S(1)} %pad_maximum_fusion.2), channel_id=1, source_target_pairs={{16,0},{32,16},{48,32},{64,48},{80,64},{96,80},{112,96},{17,1},{33... | collective-permute-start | bytes 1572872 | tf_op jit(solution)/shard_map/ppermute | solution.py:40
  167.2 10.5 %collective-permute-start.4 = (bf16[4,16,32,128]{3,2,1,0:T(8,128)(2,1)S(1)}, bf16[4,16,32,128]{3,2,1,0:T(8,128)(2,1)S(1)}, u32[]{:S(2)}, u32[]{:S(2)}) collective-permute-start(bf16[4,16,32,128]{3,2,1,0:T(8,128)(2,1)S(1)} %bitcast.35), channel_id=1, source_target_pairs={{0,16},{16,32},{32,48},{48,64},{64,80},{80,96},{96,112},{1,17},{17... | collective-permute-start | bytes 1572872 | tf_op jit(solution)/shard_map/ppermute | solution.py:39
  169.1 10.3 %collective-permute-start.5 = (bf16[4,16,32,128]{3,2,1,0:T(8,128)(2,1)S(1)}, bf16[4,16,32,128]{3,2,1,0:T(8,128)(2,1)S(1)}, u32[]{:S(2)}, u32[]{:S(2)}) collective-permute-start(bf16[4,16,32,128]{3,2,1,0:T(8,128)(2,1)S(1)} %bitcast.34), channel_id=1, source_target_pairs={{16,0},{32,16},{48,32},{64,48},{80,64},{96,80},{112,96},{17,1},{33... | collective-permute-start | bytes 1572872 | tf_op jit(solution)/shard_map/ppermute | solution.py:40
  179.8 10.8 %collective-permute-start.6 = (bf16[8,4,32,128]{3,2,1,0:T(8,128)(2,1)S(1)}, bf16[8,4,32,128]{3,2,1,0:T(8,128)(2,1)S(1)}, u32[]{:S(2)}, u32[]{:S(2)}) collective-permute-start(bf16[8,4,32,128]{3,2,1,0:T(8,128)(2,1)S(1)} %get-tuple-element.42), channel_id=1, source_target_pairs={{0,1},{1,2},{2,3},{3,4},{4,5},{5,6},{6,7},{7,8},{8,9},{9,10},{10,1... | collective-permute-start | bytes 786440 | tf_op jit(solution)/shard_map/ppermute | solution.py:39
  184.4 12.4 %collective-permute-start.7 = (bf16[8,4,32,128]{3,2,1,0:T(8,128)(2,1)S(1)}, bf16[8,4,32,128]{3,2,1,0:T(8,128)(2,1)S(1)}, u32[]{:S(2)}, u32[]{:S(2)}) collective-permute-start(bf16[8,4,32,128]{3,2,1,0:T(8,128)(2,1)S(1)} %get-tuple-element.43), channel_id=1, source_target_pairs={{1,0},{2,1},{3,2},{4,3},{5,4},{6,5},{7,6},{8,7},{9,8},{10,9},{11,1... | collective-permute-start | bytes 786440 | tf_op jit(solution)/shard_map/ppermute | solution.py:40
  188.9 8.0 %copy-start.1 = (bf16[8,8,32,128]{3,2,1,0:T(8,128)(2,1)S(1)}, bf16[8,8,32,128]{3,2,1,0:T(8,128)(2,1)}, u32[]{:S(2)}) copy-start(bf16[8,8,32,128]{3,2,1,0:T(8,128)(2,1)} %param.6) | copy-start | bytes 1572868
  188.9 8.0 %copy-start.2 = (bf16[8,8,32,128]{3,2,1,0:T(8,128)(2,1)S(1)}, bf16[8,8,32,128]{3,2,1,0:T(8,128)(2,1)}, u32[]{:S(2)}) copy-start(bf16[8,8,32,128]{3,2,1,0:T(8,128)(2,1)} %param.5) | copy-start | bytes 1572868

commit v7 on v6

--- a/solution.py
+++ b/solution.py
@@ -103,20 +103,20 @@
     py = ((code >> 5) & 127) - base_ref[1]
     pz = code & 31
     z = lax.broadcasted_iota(jnp.int32, (32, lanes), 0)
-    in_z = jnp.where((z >= pz) & (z < pz + PATCH), 1.0, 0.0)
+    in_z = jnp.where((z >= pz) & (z < pz + PATCH), 1.0, 0.0).astype(BF16)
     ones = jnp.ones((lanes, 128), BF16)
 
     def column(x, _):
         in_x = (px <= x) & (px > x - PATCH)
         parts = []
         for y in range(8):
-            hit = jnp.where(in_x & (py <= y) & (py > y - PATCH), 1.0, 0.0)
-            parts.append((hit * in_z).astype(BF16))
+            hit = jnp.where(in_x & (py <= y) & (py > y - PATCH), 1.0, 0.0).astype(BF16)
+            parts.append(jnp.broadcast_to(hit, in_z.shape) * in_z)
         cover = jnp.dot(jnp.concatenate(parts, 0), ones, preferred_element_type=F32)
         out_ref[pl.ds(pl.multiple_of(x * 256, 256), 256), :] = 1.0 / (cover + DATA_WEIGHT)
         return 0
 
-    lax.fori_loop(0, 8, column, 0)
+    lax.fori_loop(0, 8, column, 0, unroll=4)
 
 
 def load_half(cells_ref, first):
@@ -241,27 +241,25 @@
     out_ref[pl.ds(16, 128, stride=17), :] = extra[:128] + extra[128:]
 
     def chunk(i, _):
-        local = group_ref[...] - i * 256
-        local = jnp.where((local >= 0) & (local < 256), local, 512).astype(F32).astype(BF16)
+        locals_ = []
+        for k in range(8):
+            local = group_ref[...] - (i * 8 + k) * 128
+            inside = (local >= 0) & (local < 128)
+            locals_.append(jnp.where(inside, local, 128).astype(F32).astype(BF16))
         hot = []
         for t in range(32):
-            entry = jnp.broadcast_to(local[t : t + 1, :], (128, 128))
             hot.append(
                 jnp.concatenate(
-                    [
-                        jnp.where(sub16 == entry, one, zero),
-                        jnp.where(sub16 + jnp.asarray(128, BF16) == entry, one, zero),
-                    ],
-                    0,
+                    [jnp.where(sub16 == rows_of(local, t), one, zero) for local in locals_], 0
                 )
             )
         total = jnp.dot(jnp.concatenate(hot, 1), limbs_ref[...], preferred_element_type=F32)
         total = total[:, :128] + total[:, 128:]
-        for d in range(16):
-            out_ref[pl.ds((i * 16 + d) * 17, 16), :] = total[d * 16 : d * 16 + 16]
-        return 0
-
-    lax.fori_loop(0, 8, chunk, 0)
+        for d in range(8 * 8):
+            out_ref[pl.ds((i * 8 * 8 + d) * 17, 16), :] = total[d * 16 : d * 16 + 16]
+        return 0
+
+    lax.fori_loop(0, 16 // 8, chunk, 0)
 
 
 def shrink_body(tau_ref, rows_ref, out_ref, sys_ref, stage_ref):
@@ -410,10 +408,10 @@
         jnp.int32, (32, 128), 1
     )
     stage_ref[pl.ds(33, 128, stride=34), :] = jnp.zeros((128, 128), F32)
-    for u in range(8):
+    for u in range(4):
         groups, hot, owners = [], [], []
-        for v in range(4):
-            group = jnp.broadcast_to(turned_ref[:, u * 4 + v : u * 4 + v + 1], (128, 128))
+        for v in range(8):
+            group = jnp.broadcast_to(turned_ref[:, u * 8 + v : u * 8 + v + 1], (128, 128))
             groups.append(group)
             low = jnp.where((group & 127).astype(F32).astype(BF16) == lane16, one, zero)
             high = ((group >> 7) & 3).astype(F32).astype(BF16)
@@ -426,7 +424,7 @@
             owners.append(jnp.where((group >> 4).astype(F32).astype(BF16) == lane16, one, zero))
         wide = jnp.dot(jnp.concatenate(hot, 0), table_ref[...], preferred_element_type=F32)
         spots = jnp.dot(jnp.concatenate(owners, 0), extras, preferred_element_type=F32)
-        for v in range(4):
+        for v in range(8):
             group = groups[v]
             rows = slice(v * 128, (v + 1) * 128)
             quarter = group >> 9
@@ -436,7 +434,7 @@
             spot = jnp.where(lane == (group & 15), spots[rows], 0.0)
             value = jnp.sum(spot, axis=1, keepdims=True)
             for k in range(4):
-                row = ((u * 4 + v) * 4 + k) * 34
+                row = ((u * 8 + v) * 4 + k) * 34
                 part = slice(k * 32, k * 32 + 32)
                 stage_ref[row : row + 32, :] = piece[part]
                 stage_ref[row + 32 : row + 33, :] = jnp.sum(

time: 199 us -> 198 us (level)
  Pallas kernels: 48.6 us -> 46.5 us
    pallas_call x9, Pallas kernels: 48.6 us -> 46.5 us  [call(): pl.pallas_call(body, out_shape=out_shape, in_specs=specs or [VMEM] * len(...]
where the time goes in v7:
time: 198 us
  blocking collectives  104 us (53%)
  Pallas kernels  46.5 us (23%)
  starting transfers between devices  25.7 us (13%)
  waiting for transfers between devices  15 us (8%)
  other arithmetic  3.96 us (2%)
    all_to_all x4, blocking collectives, exchange(): rows = lax.all_to_all(rows, BOTH, split_axis=0, concat_axis=0, tiled=True)  104 us
    pallas_call x9, Pallas kernels, call(): pl.pallas_call(body, out_shape=out_shape, in_specs=specs or [VMEM] * len(...  46.5 us
    ppermute x4, starting transfers between devices, neighbors(): before = lax.ppermute(last, axis, up)  14.1 us
    ppermute x4, starting transfers between devices, neighbors(): after = lax.ppermute(first, axis, down)  11.5 us
    ppermute x4, waiting for transfers between devices, neighbors(): after = lax.ppermute(first, axis, down)  9.64 us
    ppermute x4, waiting for transfers between devices, neighbors(): before = lax.ppermute(last, axis, up)  5.39 us
  transfers between devices with their start and end apart: 8, of which 6 were waited for; matrix products, arithmetic and copies ran while one was open for 1% of the time, Pallas kernels for 7%

profile of v7, /device:TPU:104, one launch (start us, length us, event | category | flops | bytes accessed | tf_op | source)
XLA Modules:
  0.0 197.6 jit_solution(5140307660041616819)
XLA Ops:
  2.1 2.3 %collective-permute-start.1 = (bf16[8,4,32,128]{3,2,1,0:T(8,128)(2,1)S(1)}, bf16[8,4,32,128]{3,2,1,0:T(8,128)(2,1)S(1)}, u32[]{:S(2)}, u32[]{:S(2)}) collective-permute-start(bf16[8,4,32,128]{3,2,1,0:T(8,128)(2,1)S(1)} %get-tuple-element.46), channel_id=1, source_target_pairs={{1,0},{2,1},{3,2},{4,3},{5,4},{6,5},{7,6},{8,7},{9,8},{10,9},{11,1... | collective-permute-start | bytes 786440 | tf_op jit(solution)/shard_map/ppermute | solution.py:40
  4.4 5.6 %collective-permute-start = (bf16[8,4,32,128]{3,2,1,0:T(8,128)(2,1)S(1)}, bf16[8,4,32,128]{3,2,1,0:T(8,128)(2,1)S(1)}, u32[]{:S(2)}, u32[]{:S(2)}) collective-permute-start(bf16[8,4,32,128]{3,2,1,0:T(8,128)(2,1)S(1)} %get-tuple-element.47), channel_id=1, source_target_pairs={{0,1},{1,2},{2,3},{3,4},{4,5},{5,6},{6,7},{7,8},{8,9},{9,10},{10,1... | collective-permute-start | bytes 786440 | tf_op jit(solution)/shard_map/ppermute | solution.py:39
  10.3 5.0 %shard_map.69.group_ref = s32[32,128]{1,0:T(8,128)S(1)} custom-call(s32[1]{0:T(128)} %bitcast.4.side_ref, s32[16,2048]{1,0:T(8,128)S(1)} %bitcast.36), custom_call_target="tpu_custom_call" | custom-call | flops 536870912 | bytes 131072 | tf_op jit(solution)/shard_map/pallas_call | solution.py:24
  16.2 1.9 collective-permute-start.2
  18.2 3.6 %collective-permute-start.3 = (bf16[4,16,32,128]{3,2,1,0:T(8,128)(2,1)S(1)}, bf16[4,16,32,128]{3,2,1,0:T(8,128)(2,1)S(1)}, u32[]{:S(2)}, u32[]{:S(2)}) collective-permute-start(bf16[4,16,32,128]{3,2,1,0:T(8,128)(2,1)S(1)} %pad_maximum_fusion.2), channel_id=1, source_target_pairs={{16,0},{32,16},{48,32},{64,48},{80,64},{96,80},{112,96},{17,1},{33... | collective-permute-start | bytes 1572872 | tf_op jit(solution)/shard_map/ppermute | solution.py:40
  21.9 2.7 %shard_map.68 = (f32[4096,128]{1,0:T(8,128)S(1)}, f32[64,128,128]{2,1,0:T(8,128)S(1)}) custom-call(s32[64]{0:T(128)S(1)} %get-tuple-element.36.first_ref, bf16[8,8,32,128]{3,2,1,0:T(8,128)(2,1)S(1)} %fusion.3.own_ref, bf16[8,4,32,128]{3,2,1,0:T(8,128)(2,1)S(1)} %collective-permute-done.yb_ref, bf16[8,4,32,128]{3,2,1,0:T(8,128)(2,1)S(1)} %collective-permute-done.1.ya_ref), custom_call_target="tpu_custom_call" | custom-call | flops 536870912 | bytes 8388608 | tf_op jit(solution)/shard_map/pallas_call | solution.py:24
  24.6 2.2 %collective-permute-done.2.xb_ref = bf16[4,16,32,128]{3,2,1,0:T(8,128)(2,1)S(1)} collective-permute-done((bf16[4,16,32,128]{3,2,1,0:T(8,128)(2,1)S(1)}, bf16[4,16,32,128]{3,2,1,0:T(8,128)(2,1)S(1)}, u32[]{:S(2)}, u32[]{:S(2)}) %collective-permute-start.2) | collective-permute-done | bytes 524320 | tf_op jit(solution)/shard_map/ppermute | solution.py:39
  26.7 1.8 collective-permute-done.3.xa_ref
  28.6 3.3 %shard_map.70 = (f32[8192,128]{1,0:T(8,128)S(1)}, f32[4224,128]{1,0:T(8,128)S(1)}) custom-call(s32[64]{0:T(128)S(1)} %get-tuple-element.52.first_ref, f32[1,128]{1,0:T(1,128)S(1)} %pad_bitcast_fusion.code_ref, f32[4096,128]{1,0:T(8,128)S(1)} %get-tuple-element.18.inner_ref.cells_ref, bf16[4,16,32,128]{3,2,1,0:T(8,128)(2,1)S(1)} %collective-permute-done.2.xb_ref, ...), custom_call_target="tpu_custom_call" | custom-call | flops 536870912 | bytes 10485760 | tf_op jit(solution)/shard_map/pallas_call | solution.py:24
  31.9 38.5 %all_to_all.20 = f32[128,33,1,128]{3,2,1,0:T(1,128)S(1)} all-to-all(f32[128,33,1,128]{3,2,1,0:T(1,128)S(1)} %bitcast.26), channel_id=1, replica_groups=mesh['gx'=8,'gy'=16] {'gx','gy'}, dimensions={0} | all-to-all | bytes 4325376 | tf_op jit(solution)/shard_map/all_to_all | solution.py:528
  70.4 6.4 %shard_map.71 = (f32[2176,128]{1,0:T(8,128)S(1)}, f32[8,128]{1,0:T(8,128)S(1)}) custom-call(s32[9]{0:T(128)S(1)} %and_select_fusion.near_id_ref, s32[32,128]{1,0:T(8,128)S(1)} %shard_map.69.group_ref, f32[4224,128]{1,0:T(8,128)S(1)} %bitcast.27), custom_call_target="tpu_custom_call" | custom-call | flops 4294967296 | bytes 5242880 | tf_op jit(solution)/shard_map/pallas_call | solution.py:24
  76.8 23.7 %all_to_all.21 = f32[128,17,1,128]{3,2,1,0:T(1,128)S(1)} all-to-all(f32[128,17,1,128]{3,2,1,0:T(1,128)S(1)} %bitcast.28), channel_id=1, replica_groups=mesh['gx'=8,'gy'=16] {'gx','gy'}, dimensions={0} | all-to-all | bytes 2228224 | tf_op jit(solution)/shard_map/all_to_all | solution.py:528
  100.5 13.0 %shard_map.72 = bf16[2304,128]{1,0:T(8,128)(2,1)S(1)} custom-call(f32[16]{0:T(128)S(1)} %dynamic_slice.3.tau_ref, f32[2176,128]{1,0:T(8,128)S(1)} %bitcast.29), custom_call_target="tpu_custom_call" | custom-call | flops 3221225472 | bytes 2097152 | tf_op jit(solution)/shard_map/pallas_call | solution.py:24
  113.5 18.2 %all_to_all.22 = bf16[128,9,2,128]{3,2,1,0:T(2,128)(2,1)S(1)} all-to-all(bf16[128,9,2,128]{3,2,1,0:T(2,128)(2,1)S(1)} %bitcast.32), channel_id=1, replica_groups=mesh['gx'=8,'gy'=16] {'gx','gy'}, dimensions={0} | all-to-all | bytes 1179648 | tf_op jit(solution)/shard_map/all_to_all | solution.py:528
  131.7 3.6 %shard_map.73 = bf16[4352,128]{1,0:T(8,128)(2,1)S(1)} custom-call(s32[32,128]{1,0:T(8,128)S(1)} %shard_map.69.group_ref, bf16[2304,128]{1,0:T(8,128)(2,1)S(1)} %bitcast.33), custom_call_target="tpu_custom_call" | custom-call | flops 4294967296 | bytes 3145728 | tf_op jit(solution)/shard_map/pallas_call | solution.py:24
  135.2 24.0 %all_to_all.23 = bf16[128,17,2,128]{3,2,1,0:T(2,128)(2,1)S(1)} all-to-all(bf16[128,17,2,128]{3,2,1,0:T(2,128)(2,1)S(1)} %bitcast.30), channel_id=1, replica_groups=mesh['gx'=8,'gy'=16] {'gx','gy'}, dimensions={0} | all-to-all | bytes 2228224 | tf_op jit(solution)/shard_map/all_to_all | solution.py:528
  159.2 6.8 %shard_map.74 = (f32[4096,128]{1,0:T(8,128)S(1)}, bf16[2048,128]{1,0:T(8,128)(2,1)S(1)}, bf16[2048,128]{1,0:T(8,128)(2,1)S(1)}, bf16[64,128,128]{2,1,0:T(8,128)(2,1)S(1)}) custom-call(s32[64]{0:T(128)S(1)} %get-tuple-element.52.first_ref, f32[8192,128]{1,0:T(8,128)S(1)} %get-tuple-element.22.cells_ref, bf16[4352,128]{1,0:T(8,128)(2,1)S(1)} %bitcast.25), custom_call_target="tpu_custom_call" | custom-call | flops 536870912 | bytes 10485760 | tf_op jit(solution)/shard_map/pallas_call | solution.py:24
  166.0 1.9 collective-permute-start.4
  168.0 3.6 %collective-permute-start.5 = (bf16[4,16,32,128]{3,2,1,0:T(8,128)(2,1)S(1)}, bf16[4,16,32,128]{3,2,1,0:T(8,128)(2,1)S(1)}, u32[]{:S(2)}, u32[]{:S(2)}) collective-permute-start(bf16[4,16,32,128]{3,2,1,0:T(8,128)(2,1)S(1)} %bitcast.34), channel_id=1, source_target_pairs={{16,0},{32,16},{48,32},{64,48},{80,64},{96,80},{112,96},{17,1},{33... | collective-permute-start | bytes 1572872 | tf_op jit(solution)/shard_map/ppermute | solution.py:40
  171.6 4.2 %shard_map.75 = f32[4096,128]{1,0:T(8,128)S(1)} custom-call(s32[64]{0:T(128)S(1)} %get-tuple-element.36.first_ref, f32[4096,128]{1,0:T(8,128)S(1)} %get-tuple-element.18.inner_ref.cells_ref, bf16[64,128,128]{2,1,0:T(8,128)(2,1)S(1)} %get-tuple-element.28.factor_ref, f32[4096,128]{1,0:T(8,128)S(1)} %get-tuple-element.29.start_ref), custom_call_target="tpu_custom_call" | custom-call | flops 536870912 | bytes 8388608 | tf_op jit(solution)/shard_map/pallas_call | solution.py:24
  178.7 4.7 %collective-permute-start.6 = (bf16[8,4,32,128]{3,2,1,0:T(8,128)(2,1)S(1)}, bf16[8,4,32,128]{3,2,1,0:T(8,128)(2,1)S(1)}, u32[]{:S(2)}, u32[]{:S(2)}) collective-permute-start(bf16[8,4,32,128]{3,2,1,0:T(8,128)(2,1)S(1)} %get-tuple-element.42), channel_id=1, source_target_pairs={{0,1},{1,2},{2,3},{3,4},{4,5},{5,6},{6,7},{7,8},{8,9},{9,10},{10,1... | collective-permute-start | bytes 786440 | tf_op jit(solution)/shard_map/ppermute | solution.py:39
  183.3 1.9 collective-permute-start.7
  186.9 2.6 %collective-permute-done.6 = bf16[8,4,32,128]{3,2,1,0:T(8,128)(2,1)S(1)} collective-permute-done((bf16[8,4,32,128]{3,2,1,0:T(8,128)(2,1)S(1)}, bf16[8,4,32,128]{3,2,1,0:T(8,128)(2,1)S(1)}, u32[]{:S(2)}, u32[]{:S(2)}) %collective-permute-start.6) | collective-permute-done | bytes 262176 | tf_op jit(solution)/shard_map/ppermute | solution.py:39
  189.5 6.2 %collective-permute-done.7 = bf16[8,4,32,128]{3,2,1,0:T(8,128)(2,1)S(1)} collective-permute-done((bf16[8,4,32,128]{3,2,1,0:T(8,128)(2,1)S(1)}, bf16[8,4,32,128]{3,2,1,0:T(8,128)(2,1)S(1)}, u32[]{:S(2)}, u32[]{:S(2)}) %collective-permute-start.7) | collective-permute-done | bytes 262176 | tf_op jit(solution)/shard_map/ppermute | solution.py:40
  (33 shorter events, 8.9 us)
Async XLA Ops:
  0.6 9.5 %copy-start.3 = (s32[3,64]{1,0:T(4,128)S(1)}, s32[3,64]{1,0:T(4,128)}, u32[]{:S(2)}) copy-start(s32[3,64]{1,0:T(4,128)} %param.7) | copy-start | bytes 2308
  0.6 9.6 %copy-start = (s32[2048,16]{0,1:T(8,128)S(1)}, s32[2048,16]{0,1:T(8,128)}, u32[]{:S(2)}) copy-start(s32[2048,16]{0,1:T(8,128)} %param.8) | copy-start | bytes 393220
  2.1 14.0 %collective-permute-start.1 = (bf16[8,4,32,128]{3,2,1,0:T(8,128)(2,1)S(1)}, bf16[8,4,32,128]{3,2,1,0:T(8,128)(2,1)S(1)}, u32[]{:S(2)}, u32[]{:S(2)}) collective-permute-start(bf16[8,4,32,128]{3,2,1,0:T(8,128)(2,1)S(1)} %get-tuple-element.46), channel_id=1, source_target_pairs={{1,0},{2,1},{3,2},{4,3},{5,4},{6,5},{7,6},{8,7},{9,8},{10,9},{11,1... | collective-permute-start | bytes 786440 | tf_op jit(solution)/shard_map/ppermute | solution.py:40
  4.4 11.7 %collective-permute-start = (bf16[8,4,32,128]{3,2,1,0:T(8,128)(2,1)S(1)}, bf16[8,4,32,128]{3,2,1,0:T(8,128)(2,1)S(1)}, u32[]{:S(2)}, u32[]{:S(2)}) collective-permute-start(bf16[8,4,32,128]{3,2,1,0:T(8,128)(2,1)S(1)} %get-tuple-element.47), channel_id=1, source_target_pairs={{0,1},{1,2},{2,3},{3,4},{4,5},{5,6},{6,7},{7,8},{8,9},{9,10},{10,1... | collective-permute-start | bytes 786440 | tf_op jit(solution)/shard_map/ppermute | solution.py:39
  16.2 10.5 %collective-permute-start.2 = (bf16[4,16,32,128]{3,2,1,0:T(8,128)(2,1)S(1)}, bf16[4,16,32,128]{3,2,1,0:T(8,128)(2,1)S(1)}, u32[]{:S(2)}, u32[]{:S(2)}) collective-permute-start(bf16[4,16,32,128]{3,2,1,0:T(8,128)(2,1)S(1)} %pad_maximum_fusion.1), channel_id=1, source_target_pairs={{0,16},{16,32},{32,48},{48,64},{64,80},{80,96},{96,112},{1,17},{17... | collective-permute-start | bytes 1572872 | tf_op jit(solution)/shard_map/ppermute | solution.py:39
  18.2 10.3 %collective-permute-start.3 = (bf16[4,16,32,128]{3,2,1,0:T(8,128)(2,1)S(1)}, bf16[4,16,32,128]{3,2,1,0:T(8,128)(2,1)S(1)}, u32[]{:S(2)}, u32[]{:S(2)}) collective-permute-start(bf16[4,16,32,128]{3,2,1,0:T(8,128)(2,1)S(1)} %pad_maximum_fusion.2), channel_id=1, source_target_pairs={{16,0},{32,16},{48,32},{64,48},{80,64},{96,80},{112,96},{17,1},{33... | collective-permute-start | bytes 1572872 | tf_op jit(solution)/shard_map/ppermute | solution.py:40
  166.0 10.5 %collective-permute-start.4 = (bf16[4,16,32,128]{3,2,1,0:T(8,128)(2,1)S(1)}, bf16[4,16,32,128]{3,2,1,0:T(8,128)(2,1)S(1)}, u32[]{:S(2)}, u32[]{:S(2)}) collective-permute-start(bf16[4,16,32,128]{3,2,1,0:T(8,128)(2,1)S(1)} %bitcast.35), channel_id=1, source_target_pairs={{0,16},{16,32},{32,48},{48,64},{64,80},{80,96},{96,112},{1,17},{17... | collective-permute-start | bytes 1572872 | tf_op jit(solution)/shard_map/ppermute | solution.py:39
  168.0 10.3 %collective-permute-start.5 = (bf16[4,16,32,128]{3,2,1,0:T(8,128)(2,1)S(1)}, bf16[4,16,32,128]{3,2,1,0:T(8,128)(2,1)S(1)}, u32[]{:S(2)}, u32[]{:S(2)}) collective-permute-start(bf16[4,16,32,128]{3,2,1,0:T(8,128)(2,1)S(1)} %bitcast.34), channel_id=1, source_target_pairs={{16,0},{32,16},{48,32},{64,48},{80,64},{96,80},{112,96},{17,1},{33... | collective-permute-start | bytes 1572872 | tf_op jit(solution)/shard_map/ppermute | solution.py:40
  178.7 10.8 %collective-permute-start.6 = (bf16[8,4,32,128]{3,2,1,0:T(8,128)(2,1)S(1)}, bf16[8,4,32,128]{3,2,1,0:T(8,128)(2,1)S(1)}, u32[]{:S(2)}, u32[]{:S(2)}) collective-permute-start(bf16[8,4,32,128]{3,2,1,0:T(8,128)(2,1)S(1)} %get-tuple-element.42), channel_id=1, source_target_pairs={{0,1},{1,2},{2,3},{3,4},{4,5},{5,6},{6,7},{7,8},{8,9},{9,10},{10,1... | collective-permute-start | bytes 786440 | tf_op jit(solution)/shard_map/ppermute | solution.py:39
  183.3 12.4 %collective-permute-start.7 = (bf16[8,4,32,128]{3,2,1,0:T(8,128)(2,1)S(1)}, bf16[8,4,32,128]{3,2,1,0:T(8,128)(2,1)S(1)}, u32[]{:S(2)}, u32[]{:S(2)}) collective-permute-start(bf16[8,4,32,128]{3,2,1,0:T(8,128)(2,1)S(1)} %get-tuple-element.43), channel_id=1, source_target_pairs={{1,0},{2,1},{3,2},{4,3},{5,4},{6,5},{7,6},{8,7},{9,8},{10,9},{11,1... | collective-permute-start | bytes 786440 | tf_op jit(solution)/shard_map/ppermute | solution.py:40
  186.8 9.1 %copy-start.1 = (bf16[8,8,32,128]{3,2,1,0:T(8,128)(2,1)S(1)}, bf16[8,8,32,128]{3,2,1,0:T(8,128)(2,1)}, u32[]{:S(2)}) copy-start(bf16[8,8,32,128]{3,2,1,0:T(8,128)(2,1)} %param.6) | copy-start | bytes 1572868
  186.8 9.1 %copy-start.2 = (bf16[8,8,32,128]{3,2,1,0:T(8,128)(2,1)S(1)}, bf16[8,8,32,128]{3,2,1,0:T(8,128)(2,1)}, u32[]{:S(2)}) copy-start(bf16[8,8,32,128]{3,2,1,0:T(8,128)(2,1)} %param.5) | copy-start | bytes 1572868

commit v8 on v7

--- a/solution.py
+++ b/solution.py
@@ -291,6 +291,7 @@
                 moved = pltpu.roll(panels[h * 8 + k], lax.rem(128 + k * NB - start, 128), axis=1)
                 joined = jnp.where((lane16 >> 4) == k, moved, joined)
             pivots.append(joined)
+        originals = pivots
         pivots = invert_blocks(jnp.concatenate(pivots, 0))
         in_block = (lane16 >= start) & (lane16 < start + NB)
         identity = jnp.where(lane16 - start == sub16, 1.0, 0.0)
@@ -302,6 +303,8 @@
                 [jnp.where(in_block, identity, panels[h * 8 + k]) for k in range(8)], 0
             )
             product = wide_product(left, right)
+            own = jnp.where(same, jnp.concatenate([originals[h]] * 8, 0), 0.0)
+            product = product + wide_product(left, right - wide_product(own, product))
             scaled += [product[k * NB : (k + 1) * NB] for k in range(8)]
         pick = start + (lane_id & (NB - 1))
         for g in range(per):

time: 198 us -> 205 us (1.035)
  Pallas kernels: 46.5 us -> 53.4 us
    pallas_call x9, Pallas kernels: 46.5 us -> 53.4 us  [call(): pl.pallas_call(body, out_shape=out_shape, in_specs=specs or [VMEM] * len(...]
where the time goes in v8:
time: 205 us; the launch traced here: 204 us
  blocking collectives  104 us (51%)
  Pallas kernels  53.4 us (26%)
  starting transfers between devices  25.6 us (12%)
  waiting for transfers between devices  15 us (7%)
  other arithmetic  3.96 us (2%)
    all_to_all x4, blocking collectives, exchange(): rows = lax.all_to_all(rows, BOTH, split_axis=0, concat_axis=0, tiled=True)  104 us
    pallas_call x9, Pallas kernels, call(): pl.pallas_call(body, out_shape=out_shape, in_specs=specs or [VMEM] * len(...  53.4 us
    ppermute x4, starting transfers between devices, neighbors(): before = lax.ppermute(last, axis, up)  14.1 us
    ppermute x4, starting transfers between devices, neighbors(): after = lax.ppermute(first, axis, down)  11.5 us
    ppermute x4, waiting for transfers between devices, neighbors(): after = lax.ppermute(first, axis, down)  9.64 us
    ppermute x4, waiting for transfers between devices, neighbors(): before = lax.ppermute(last, axis, up)  5.33 us
  transfers between devices with their start and end apart: 8, of which 6 were waited for; matrix products, arithmetic and copies ran while one was open for 1% of the time, Pallas kernels for 7%

profile of v8, /device:TPU:104, one launch (start us, length us, event | category | flops | bytes accessed | tf_op | source)
XLA Modules:
  0.0 204.5 jit_solution(17112613035544162562)
XLA Ops:
  2.1 2.3 %collective-permute-start.1 = (bf16[8,4,32,128]{3,2,1,0:T(8,128)(2,1)S(1)}, bf16[8,4,32,128]{3,2,1,0:T(8,128)(2,1)S(1)}, u32[]{:S(2)}, u32[]{:S(2)}) collective-permute-start(bf16[8,4,32,128]{3,2,1,0:T(8,128)(2,1)S(1)} %get-tuple-element.46), channel_id=1, source_target_pairs={{1,0},{2,1},{3,2},{4,3},{5,4},{6,5},{7,6},{8,7},{9,8},{10,9},{11,1... | collective-permute-start | bytes 786440 | tf_op jit(solution)/shard_map/ppermute | solution.py:40
  4.4 5.6 %collective-permute-start = (bf16[8,4,32,128]{3,2,1,0:T(8,128)(2,1)S(1)}, bf16[8,4,32,128]{3,2,1,0:T(8,128)(2,1)S(1)}, u32[]{:S(2)}, u32[]{:S(2)}) collective-permute-start(bf16[8,4,32,128]{3,2,1,0:T(8,128)(2,1)S(1)} %get-tuple-element.47), channel_id=1, source_target_pairs={{0,1},{1,2},{2,3},{3,4},{4,5},{5,6},{6,7},{7,8},{8,9},{9,10},{10,1... | collective-permute-start | bytes 786440 | tf_op jit(solution)/shard_map/ppermute | solution.py:39
  10.3 5.0 %shard_map.69.group_ref = s32[32,128]{1,0:T(8,128)S(1)} custom-call(s32[1]{0:T(128)} %bitcast.4.side_ref, s32[16,2048]{1,0:T(8,128)S(1)} %bitcast.36), custom_call_target="tpu_custom_call" | custom-call | flops 536870912 | bytes 131072 | tf_op jit(solution)/shard_map/pallas_call | solution.py:24
  16.2 1.9 collective-permute-start.2
  18.2 3.6 %collective-permute-start.3 = (bf16[4,16,32,128]{3,2,1,0:T(8,128)(2,1)S(1)}, bf16[4,16,32,128]{3,2,1,0:T(8,128)(2,1)S(1)}, u32[]{:S(2)}, u32[]{:S(2)}) collective-permute-start(bf16[4,16,32,128]{3,2,1,0:T(8,128)(2,1)S(1)} %pad_maximum_fusion.2), channel_id=1, source_target_pairs={{16,0},{32,16},{48,32},{64,48},{80,64},{96,80},{112,96},{17,1},{33... | collective-permute-start | bytes 1572872 | tf_op jit(solution)/shard_map/ppermute | solution.py:40
  21.9 2.7 %shard_map.68 = (f32[4096,128]{1,0:T(8,128)S(1)}, f32[64,128,128]{2,1,0:T(8,128)S(1)}) custom-call(s32[64]{0:T(128)S(1)} %get-tuple-element.36.first_ref, bf16[8,8,32,128]{3,2,1,0:T(8,128)(2,1)S(1)} %fusion.3.own_ref, bf16[8,4,32,128]{3,2,1,0:T(8,128)(2,1)S(1)} %collective-permute-done.yb_ref, bf16[8,4,32,128]{3,2,1,0:T(8,128)(2,1)S(1)} %collective-permute-done.1.ya_ref), custom_call_target="tpu_custom_call" | custom-call | flops 536870912 | bytes 8388608 | tf_op jit(solution)/shard_map/pallas_call | solution.py:24
  24.6 2.2 %collective-permute-done.2.xb_ref = bf16[4,16,32,128]{3,2,1,0:T(8,128)(2,1)S(1)} collective-permute-done((bf16[4,16,32,128]{3,2,1,0:T(8,128)(2,1)S(1)}, bf16[4,16,32,128]{3,2,1,0:T(8,128)(2,1)S(1)}, u32[]{:S(2)}, u32[]{:S(2)}) %collective-permute-start.2) | collective-permute-done | bytes 524320 | tf_op jit(solution)/shard_map/ppermute | solution.py:39
  26.7 1.8 collective-permute-done.3.xa_ref
  28.6 3.3 %shard_map.70 = (f32[8192,128]{1,0:T(8,128)S(1)}, f32[4224,128]{1,0:T(8,128)S(1)}) custom-call(s32[64]{0:T(128)S(1)} %get-tuple-element.52.first_ref, f32[1,128]{1,0:T(1,128)S(1)} %pad_bitcast_fusion.code_ref, f32[4096,128]{1,0:T(8,128)S(1)} %get-tuple-element.18.inner_ref.cells_ref, bf16[4,16,32,128]{3,2,1,0:T(8,128)(2,1)S(1)} %collective-permute-done.2.xb_ref, ...), custom_call_target="tpu_custom_call" | custom-call | flops 536870912 | bytes 10485760 | tf_op jit(solution)/shard_map/pallas_call | solution.py:24
  31.8 38.5 %all_to_all.20 = f32[128,33,1,128]{3,2,1,0:T(1,128)S(1)} all-to-all(f32[128,33,1,128]{3,2,1,0:T(1,128)S(1)} %bitcast.26), channel_id=1, replica_groups=mesh['gx'=8,'gy'=16] {'gx','gy'}, dimensions={0} | all-to-all | bytes 4325376 | tf_op jit(solution)/shard_map/all_to_all | solution.py:531
  70.4 6.4 %shard_map.71 = (f32[2176,128]{1,0:T(8,128)S(1)}, f32[8,128]{1,0:T(8,128)S(1)}) custom-call(s32[9]{0:T(128)S(1)} %and_select_fusion.near_id_ref, s32[32,128]{1,0:T(8,128)S(1)} %shard_map.69.group_ref, f32[4224,128]{1,0:T(8,128)S(1)} %bitcast.27), custom_call_target="tpu_custom_call" | custom-call | flops 4294967296 | bytes 5242880 | tf_op jit(solution)/shard_map/pallas_call | solution.py:24
  76.8 23.7 %all_to_all.21 = f32[128,17,1,128]{3,2,1,0:T(1,128)S(1)} all-to-all(f32[128,17,1,128]{3,2,1,0:T(1,128)S(1)} %bitcast.28), channel_id=1, replica_groups=mesh['gx'=8,'gy'=16] {'gx','gy'}, dimensions={0} | all-to-all | bytes 2228224 | tf_op jit(solution)/shard_map/all_to_all | solution.py:531
  100.5 19.8 %shard_map.72 = bf16[2304,128]{1,0:T(8,128)(2,1)S(1)} custom-call(f32[16]{0:T(128)S(1)} %dynamic_slice.3.tau_ref, f32[2176,128]{1,0:T(8,128)S(1)} %bitcast.29), custom_call_target="tpu_custom_call" | custom-call | flops 3221225472 | bytes 2097152 | tf_op jit(solution)/shard_map/pallas_call | solution.py:24
  120.4 18.2 %all_to_all.22 = bf16[128,9,2,128]{3,2,1,0:T(2,128)(2,1)S(1)} all-to-all(bf16[128,9,2,128]{3,2,1,0:T(2,128)(2,1)S(1)} %bitcast.32), channel_id=1, replica_groups=mesh['gx'=8,'gy'=16] {'gx','gy'}, dimensions={0} | all-to-all | bytes 1179648 | tf_op jit(solution)/shard_map/all_to_all | solution.py:531
  138.6 3.6 %shard_map.73 = bf16[4352,128]{1,0:T(8,128)(2,1)S(1)} custom-call(s32[32,128]{1,0:T(8,128)S(1)} %shard_map.69.group_ref, bf16[2304,128]{1,0:T(8,128)(2,1)S(1)} %bitcast.33), custom_call_target="tpu_custom_call" | custom-call | flops 4294967296 | bytes 3145728 | tf_op jit(solution)/shard_map/pallas_call | solution.py:24
  142.1 24.0 %all_to_all.23 = bf16[128,17,2,128]{3,2,1,0:T(2,128)(2,1)S(1)} all-to-all(bf16[128,17,2,128]{3,2,1,0:T(2,128)(2,1)S(1)} %bitcast.30), channel_id=1, replica_groups=mesh['gx'=8,'gy'=16] {'gx','gy'}, dimensions={0} | all-to-all | bytes 2228224 | tf_op jit(solution)/shard_map/all_to_all | solution.py:531
  166.1 6.8 %shard_map.74 = (f32[4096,128]{1,0:T(8,128)S(1)}, bf16[2048,128]{1,0:T(8,128)(2,1)S(1)}, bf16[2048,128]{1,0:T(8,128)(2,1)S(1)}, bf16[64,128,128]{2,1,0:T(8,128)(2,1)S(1)}) custom-call(s32[64]{0:T(128)S(1)} %get-tuple-element.52.first_ref, f32[8192,128]{1,0:T(8,128)S(1)} %get-tuple-element.22.cells_ref, bf16[4352,128]{1,0:T(8,128)(2,1)S(1)} %bitcast.25), custom_call_target="tpu_custom_call" | custom-call | flops 536870912 | bytes 10485760 | tf_op jit(solution)/shard_map/pallas_call | solution.py:24
  172.9 1.9 collective-permute-start.4
  174.9 3.6 %collective-permute-start.5 = (bf16[4,16,32,128]{3,2,1,0:T(8,128)(2,1)S(1)}, bf16[4,16,32,128]{3,2,1,0:T(8,128)(2,1)S(1)}, u32[]{:S(2)}, u32[]{:S(2)}) collective-permute-start(bf16[4,16,32,128]{3,2,1,0:T(8,128)(2,1)S(1)} %bitcast.34), channel_id=1, source_target_pairs={{16,0},{32,16},{48,32},{64,48},{80,64},{96,80},{112,96},{17,1},{33... | collective-permute-start | bytes 1572872 | tf_op jit(solution)/shard_map/ppermute | solution.py:40
  178.5 4.2 %shard_map.75 = f32[4096,128]{1,0:T(8,128)S(1)} custom-call(s32[64]{0:T(128)S(1)} %get-tuple-element.36.first_ref, f32[4096,128]{1,0:T(8,128)S(1)} %get-tuple-element.18.inner_ref.cells_ref, bf16[64,128,128]{2,1,0:T(8,128)(2,1)S(1)} %get-tuple-element.28.factor_ref, f32[4096,128]{1,0:T(8,128)S(1)} %get-tuple-element.29.start_ref), custom_call_target="tpu_custom_call" | custom-call | flops 536870912 | bytes 8388608 | tf_op jit(solution)/shard_map/pallas_call | solution.py:24
  185.5 4.6 %collective-permute-start.6 = (bf16[8,4,32,128]{3,2,1,0:T(8,128)(2,1)S(1)}, bf16[8,4,32,128]{3,2,1,0:T(8,128)(2,1)S(1)}, u32[]{:S(2)}, u32[]{:S(2)}) collective-permute-start(bf16[8,4,32,128]{3,2,1,0:T(8,128)(2,1)S(1)} %get-tuple-element.42), channel_id=1, source_target_pairs={{0,1},{1,2},{2,3},{3,4},{4,5},{5,6},{6,7},{7,8},{8,9},{9,10},{10,1... | collective-permute-start | bytes 786440 | tf_op jit(solution)/shard_map/ppermute | solution.py:39
  190.2 1.9 collective-permute-start.7
  193.8 2.6 %collective-permute-done.6 = bf16[8,4,32,128]{3,2,1,0:T(8,128)(2,1)S(1)} collective-permute-done((bf16[8,4,32,128]{3,2,1,0:T(8,128)(2,1)S(1)}, bf16[8,4,32,128]{3,2,1,0:T(8,128)(2,1)S(1)}, u32[]{:S(2)}, u32[]{:S(2)}) %collective-permute-start.6) | collective-permute-done | bytes 262176 | tf_op jit(solution)/shard_map/ppermute | solution.py:39
  196.4 6.2 %collective-permute-done.7 = bf16[8,4,32,128]{3,2,1,0:T(8,128)(2,1)S(1)} collective-permute-done((bf16[8,4,32,128]{3,2,1,0:T(8,128)(2,1)S(1)}, bf16[8,4,32,128]{3,2,1,0:T(8,128)(2,1)S(1)}, u32[]{:S(2)}, u32[]{:S(2)}) %collective-permute-start.7) | collective-permute-done | bytes 262176 | tf_op jit(solution)/shard_map/ppermute | solution.py:40
  (33 shorter events, 8.9 us)
Async XLA Ops:
  0.6 9.5 %copy-start.3 = (s32[3,64]{1,0:T(4,128)S(1)}, s32[3,64]{1,0:T(4,128)}, u32[]{:S(2)}) copy-start(s32[3,64]{1,0:T(4,128)} %param.7) | copy-start | bytes 2308
  0.6 9.6 %copy-start = (s32[2048,16]{0,1:T(8,128)S(1)}, s32[2048,16]{0,1:T(8,128)}, u32[]{:S(2)}) copy-start(s32[2048,16]{0,1:T(8,128)} %param.8) | copy-start | bytes 393220
  2.1 14.0 %collective-permute-start.1 = (bf16[8,4,32,128]{3,2,1,0:T(8,128)(2,1)S(1)}, bf16[8,4,32,128]{3,2,1,0:T(8,128)(2,1)S(1)}, u32[]{:S(2)}, u32[]{:S(2)}) collective-permute-start(bf16[8,4,32,128]{3,2,1,0:T(8,128)(2,1)S(1)} %get-tuple-element.46), channel_id=1, source_target_pairs={{1,0},{2,1},{3,2},{4,3},{5,4},{6,5},{7,6},{8,7},{9,8},{10,9},{11,1... | collective-permute-start | bytes 786440 | tf_op jit(solution)/shard_map/ppermute | solution.py:40
  4.4 11.7 %collective-permute-start = (bf16[8,4,32,128]{3,2,1,0:T(8,128)(2,1)S(1)}, bf16[8,4,32,128]{3,2,1,0:T(8,128)(2,1)S(1)}, u32[]{:S(2)}, u32[]{:S(2)}) collective-permute-start(bf16[8,4,32,128]{3,2,1,0:T(8,128)(2,1)S(1)} %get-tuple-element.47), channel_id=1, source_target_pairs={{0,1},{1,2},{2,3},{3,4},{4,5},{5,6},{6,7},{7,8},{8,9},{9,10},{10,1... | collective-permute-start | bytes 786440 | tf_op jit(solution)/shard_map/ppermute | solution.py:39
  16.2 10.5 %collective-permute-start.2 = (bf16[4,16,32,128]{3,2,1,0:T(8,128)(2,1)S(1)}, bf16[4,16,32,128]{3,2,1,0:T(8,128)(2,1)S(1)}, u32[]{:S(2)}, u32[]{:S(2)}) collective-permute-start(bf16[4,16,32,128]{3,2,1,0:T(8,128)(2,1)S(1)} %pad_maximum_fusion.1), channel_id=1, source_target_pairs={{0,16},{16,32},{32,48},{48,64},{64,80},{80,96},{96,112},{1,17},{17... | collective-permute-start | bytes 1572872 | tf_op jit(solution)/shard_map/ppermute | solution.py:39
  18.2 10.3 %collective-permute-start.3 = (bf16[4,16,32,128]{3,2,1,0:T(8,128)(2,1)S(1)}, bf16[4,16,32,128]{3,2,1,0:T(8,128)(2,1)S(1)}, u32[]{:S(2)}, u32[]{:S(2)}) collective-permute-start(bf16[4,16,32,128]{3,2,1,0:T(8,128)(2,1)S(1)} %pad_maximum_fusion.2), channel_id=1, source_target_pairs={{16,0},{32,16},{48,32},{64,48},{80,64},{96,80},{112,96},{17,1},{33... | collective-permute-start | bytes 1572872 | tf_op jit(solution)/shard_map/ppermute | solution.py:40
  172.9 10.5 %collective-permute-start.4 = (bf16[4,16,32,128]{3,2,1,0:T(8,128)(2,1)S(1)}, bf16[4,16,32,128]{3,2,1,0:T(8,128)(2,1)S(1)}, u32[]{:S(2)}, u32[]{:S(2)}) collective-permute-start(bf16[4,16,32,128]{3,2,1,0:T(8,128)(2,1)S(1)} %bitcast.35), channel_id=1, source_target_pairs={{0,16},{16,32},{32,48},{48,64},{64,80},{80,96},{96,112},{1,17},{17... | collective-permute-start | bytes 1572872 | tf_op jit(solution)/shard_map/ppermute | solution.py:39
  174.9 10.3 %collective-permute-start.5 = (bf16[4,16,32,128]{3,2,1,0:T(8,128)(2,1)S(1)}, bf16[4,16,32,128]{3,2,1,0:T(8,128)(2,1)S(1)}, u32[]{:S(2)}, u32[]{:S(2)}) collective-permute-start(bf16[4,16,32,128]{3,2,1,0:T(8,128)(2,1)S(1)} %bitcast.34), channel_id=1, source_target_pairs={{16,0},{32,16},{48,32},{64,48},{80,64},{96,80},{112,96},{17,1},{33... | collective-permute-start | bytes 1572872 | tf_op jit(solution)/shard_map/ppermute | solution.py:40
  185.5 10.8 %collective-permute-start.6 = (bf16[8,4,32,128]{3,2,1,0:T(8,128)(2,1)S(1)}, bf16[8,4,32,128]{3,2,1,0:T(8,128)(2,1)S(1)}, u32[]{:S(2)}, u32[]{:S(2)}) collective-permute-start(bf16[8,4,32,128]{3,2,1,0:T(8,128)(2,1)S(1)} %get-tuple-element.42), channel_id=1, source_target_pairs={{0,1},{1,2},{2,3},{3,4},{4,5},{5,6},{6,7},{7,8},{8,9},{9,10},{10,1... | collective-permute-start | bytes 786440 | tf_op jit(solution)/shard_map/ppermute | solution.py:39
  190.2 12.4 %collective-permute-start.7 = (bf16[8,4,32,128]{3,2,1,0:T(8,128)(2,1)S(1)}, bf16[8,4,32,128]{3,2,1,0:T(8,128)(2,1)S(1)}, u32[]{:S(2)}, u32[]{:S(2)}) collective-permute-start(bf16[8,4,32,128]{3,2,1,0:T(8,128)(2,1)S(1)} %get-tuple-element.43), channel_id=1, source_target_pairs={{1,0},{2,1},{3,2},{4,3},{5,4},{6,5},{7,6},{8,7},{9,8},{10,9},{11,1... | collective-permute-start | bytes 786440 | tf_op jit(solution)/shard_map/ppermute | solution.py:40
  193.7 9.0 %copy-start.1 = (bf16[8,8,32,128]{3,2,1,0:T(8,128)(2,1)S(1)}, bf16[8,8,32,128]{3,2,1,0:T(8,128)(2,1)}, u32[]{:S(2)}) copy-start(bf16[8,8,32,128]{3,2,1,0:T(8,128)(2,1)} %param.6) | copy-start | bytes 1572868
  193.7 9.0 %copy-start.2 = (bf16[8,8,32,128]{3,2,1,0:T(8,128)(2,1)S(1)}, bf16[8,8,32,128]{3,2,1,0:T(8,128)(2,1)}, u32[]{:S(2)}) copy-start(bf16[8,8,32,128]{3,2,1,0:T(8,128)(2,1)} %param.5) | copy-start | bytes 1572868

commit v9 on v7

--- a/solution.py
+++ b/solution.py
@@ -291,17 +291,26 @@
                 moved = pltpu.roll(panels[h * 8 + k], lax.rem(128 + k * NB - start, 128), axis=1)
                 joined = jnp.where((lane16 >> 4) == k, moved, joined)
             pivots.append(joined)
+        originals = pivots
         pivots = invert_blocks(jnp.concatenate(pivots, 0))
         in_block = (lane16 >= start) & (lane16 < start + NB)
         identity = jnp.where(lane16 - start == sub16, 1.0, 0.0)
         in_lanes = (lane_id >= start) & (lane_id < start + NB)
         scaled = []
+        lefts, owns, rights = [], [], []
         for h in range(2):
-            left = jnp.where(same, jnp.concatenate([pivots[h * NB : (h + 1) * NB]] * 8, 0), 0.0)
-            right = jnp.concatenate(
-                [jnp.where(in_block, identity, panels[h * 8 + k]) for k in range(8)], 0
+            pivot = pivots[h * NB : (h + 1) * NB]
+            lefts.append(jnp.where(same, jnp.concatenate([pivot] * 8, 0), 0.0))
+            owns.append(jnp.where(same, jnp.concatenate([originals[h]] * 8, 0), 0.0))
+            rights.append(
+                jnp.concatenate(
+                    [jnp.where(in_block, identity, panels[h * 8 + k]) for k in range(8)], 0
+                )
             )
-            product = wide_product(left, right)
+        products = [wide_product(lefts[h], rights[h]) for h in range(2)]
+        rests = [rights[h] - wide_product(owns[h], products[h]) for h in range(2)]
+        products = [products[h] + wide_product(lefts[h], rests[h]) for h in range(2)]
+        for product in products:
             scaled += [product[k * NB : (k + 1) * NB] for k in range(8)]
         pick = start + (lane_id & (NB - 1))
         for g in range(per):

time: 198 us -> 201 us (1.015)
  Pallas kernels: 46.5 us -> 49.1 us
    pallas_call x9, Pallas kernels: 46.5 us -> 49.1 us  [call(): pl.pallas_call(body, out_shape=out_shape, in_specs=specs or [VMEM] * len(...]
where the time goes in v9:
time: 201 us; the launch traced here: 200 us
  blocking collectives  104 us (52%)
  Pallas kernels  49.1 us (24%)
  starting transfers between devices  25.6 us (13%)
  waiting for transfers between devices  15 us (7%)
  other arithmetic  3.96 us (2%)
    all_to_all x4, blocking collectives, exchange(): rows = lax.all_to_all(rows, BOTH, split_axis=0, concat_axis=0, tiled=True)  104 us
    pallas_call x9, Pallas kernels, call(): pl.pallas_call(body, out_shape=out_shape, in_specs=specs or [VMEM] * len(...  49.1 us
    ppermute x4, starting transfers between devices, neighbors(): before = lax.ppermute(last, axis, up)  14.1 us
    ppermute x4, starting transfers between devices, neighbors(): after = lax.ppermute(first, axis, down)  11.5 us
    ppermute x4, waiting for transfers between devices, neighbors(): after = lax.ppermute(first, axis, down)  9.64 us
    ppermute x4, waiting for transfers between devices, neighbors(): before = lax.ppermute(last, axis, up)  5.33 us
  transfers between devices with their start and end apart: 8, of which 6 were waited for; matrix products, arithmetic and copies ran while one was open for 1% of the time, Pallas kernels for 7%

profile of v9, /device:TPU:104, one launch (start us, length us, event | category | flops | bytes accessed | tf_op | source)
XLA Modules:
  0.0 200.1 jit_solution(3067988458964032507)
XLA Ops:
  2.1 2.3 %collective-permute-start.1 = (bf16[8,4,32,128]{3,2,1,0:T(8,128)(2,1)S(1)}, bf16[8,4,32,128]{3,2,1,0:T(8,128)(2,1)S(1)}, u32[]{:S(2)}, u32[]{:S(2)}) collective-permute-start(bf16[8,4,32,128]{3,2,1,0:T(8,128)(2,1)S(1)} %get-tuple-element.46), channel_id=1, source_target_pairs={{1,0},{2,1},{3,2},{4,3},{5,4},{6,5},{7,6},{8,7},{9,8},{10,9},{11,1... | collective-permute-start | bytes 786440 | tf_op jit(solution)/shard_map/ppermute | solution.py:40
  4.4 5.6 %collective-permute-start = (bf16[8,4,32,128]{3,2,1,0:T(8,128)(2,1)S(1)}, bf16[8,4,32,128]{3,2,1,0:T(8,128)(2,1)S(1)}, u32[]{:S(2)}, u32[]{:S(2)}) collective-permute-start(bf16[8,4,32,128]{3,2,1,0:T(8,128)(2,1)S(1)} %get-tuple-element.47), channel_id=1, source_target_pairs={{0,1},{1,2},{2,3},{3,4},{4,5},{5,6},{6,7},{7,8},{8,9},{9,10},{10,1... | collective-permute-start | bytes 786440 | tf_op jit(solution)/shard_map/ppermute | solution.py:39
  10.3 5.0 %shard_map.69.group_ref = s32[32,128]{1,0:T(8,128)S(1)} custom-call(s32[1]{0:T(128)} %bitcast.4.side_ref, s32[16,2048]{1,0:T(8,128)S(1)} %bitcast.36), custom_call_target="tpu_custom_call" | custom-call | flops 536870912 | bytes 131072 | tf_op jit(solution)/shard_map/pallas_call | solution.py:24
  16.2 1.9 collective-permute-start.2
  18.2 3.6 %collective-permute-start.3 = (bf16[4,16,32,128]{3,2,1,0:T(8,128)(2,1)S(1)}, bf16[4,16,32,128]{3,2,1,0:T(8,128)(2,1)S(1)}, u32[]{:S(2)}, u32[]{:S(2)}) collective-permute-start(bf16[4,16,32,128]{3,2,1,0:T(8,128)(2,1)S(1)} %pad_maximum_fusion.2), channel_id=1, source_target_pairs={{16,0},{32,16},{48,32},{64,48},{80,64},{96,80},{112,96},{17,1},{33... | collective-permute-start | bytes 1572872 | tf_op jit(solution)/shard_map/ppermute | solution.py:40
  21.9 2.7 %shard_map.68 = (f32[4096,128]{1,0:T(8,128)S(1)}, f32[64,128,128]{2,1,0:T(8,128)S(1)}) custom-call(s32[64]{0:T(128)S(1)} %get-tuple-element.36.first_ref, bf16[8,8,32,128]{3,2,1,0:T(8,128)(2,1)S(1)} %fusion.3.own_ref, bf16[8,4,32,128]{3,2,1,0:T(8,128)(2,1)S(1)} %collective-permute-done.yb_ref, bf16[8,4,32,128]{3,2,1,0:T(8,128)(2,1)S(1)} %collective-permute-done.1.ya_ref), custom_call_target="tpu_custom_call" | custom-call | flops 536870912 | bytes 8388608 | tf_op jit(solution)/shard_map/pallas_call | solution.py:24
  24.6 2.2 %collective-permute-done.2.xb_ref = bf16[4,16,32,128]{3,2,1,0:T(8,128)(2,1)S(1)} collective-permute-done((bf16[4,16,32,128]{3,2,1,0:T(8,128)(2,1)S(1)}, bf16[4,16,32,128]{3,2,1,0:T(8,128)(2,1)S(1)}, u32[]{:S(2)}, u32[]{:S(2)}) %collective-permute-start.2) | collective-permute-done | bytes 524320 | tf_op jit(solution)/shard_map/ppermute | solution.py:39
  26.7 1.8 collective-permute-done.3.xa_ref
  28.6 3.3 %shard_map.70 = (f32[8192,128]{1,0:T(8,128)S(1)}, f32[4224,128]{1,0:T(8,128)S(1)}) custom-call(s32[64]{0:T(128)S(1)} %get-tuple-element.52.first_ref, f32[1,128]{1,0:T(1,128)S(1)} %pad_bitcast_fusion.code_ref, f32[4096,128]{1,0:T(8,128)S(1)} %get-tuple-element.18.inner_ref.cells_ref, bf16[4,16,32,128]{3,2,1,0:T(8,128)(2,1)S(1)} %collective-permute-done.2.xb_ref, ...), custom_call_target="tpu_custom_call" | custom-call | flops 536870912 | bytes 10485760 | tf_op jit(solution)/shard_map/pallas_call | solution.py:24
  31.9 38.5 %all_to_all.20 = f32[128,33,1,128]{3,2,1,0:T(1,128)S(1)} all-to-all(f32[128,33,1,128]{3,2,1,0:T(1,128)S(1)} %bitcast.26), channel_id=1, replica_groups=mesh['gx'=8,'gy'=16] {'gx','gy'}, dimensions={0} | all-to-all | bytes 4325376 | tf_op jit(solution)/shard_map/all_to_all | solution.py:537
  70.4 6.4 %shard_map.71 = (f32[2176,128]{1,0:T(8,128)S(1)}, f32[8,128]{1,0:T(8,128)S(1)}) custom-call(s32[9]{0:T(128)S(1)} %and_select_fusion.near_id_ref, s32[32,128]{1,0:T(8,128)S(1)} %shard_map.69.group_ref, f32[4224,128]{1,0:T(8,128)S(1)} %bitcast.27), custom_call_target="tpu_custom_call" | custom-call | flops 4294967296 | bytes 5242880 | tf_op jit(solution)/shard_map/pallas_call | solution.py:24
  76.8 23.7 %all_to_all.21 = f32[128,17,1,128]{3,2,1,0:T(1,128)S(1)} all-to-all(f32[128,17,1,128]{3,2,1,0:T(1,128)S(1)} %bitcast.28), channel_id=1, replica_groups=mesh['gx'=8,'gy'=16] {'gx','gy'}, dimensions={0} | all-to-all | bytes 2228224 | tf_op jit(solution)/shard_map/all_to_all | solution.py:537
  100.5 15.5 %shard_map.72 = bf16[2304,128]{1,0:T(8,128)(2,1)S(1)} custom-call(f32[16]{0:T(128)S(1)} %dynamic_slice.3.tau_ref, f32[2176,128]{1,0:T(8,128)S(1)} %bitcast.29), custom_call_target="tpu_custom_call" | custom-call | flops 3221225472 | bytes 2097152 | tf_op jit(solution)/shard_map/pallas_call | solution.py:24
  116.1 18.1 %all_to_all.22 = bf16[128,9,2,128]{3,2,1,0:T(2,128)(2,1)S(1)} all-to-all(bf16[128,9,2,128]{3,2,1,0:T(2,128)(2,1)S(1)} %bitcast.32), channel_id=1, replica_groups=mesh['gx'=8,'gy'=16] {'gx','gy'}, dimensions={0} | all-to-all | bytes 1179648 | tf_op jit(solution)/shard_map/all_to_all | solution.py:537
  134.2 3.6 %shard_map.73 = bf16[4352,128]{1,0:T(8,128)(2,1)S(1)} custom-call(s32[32,128]{1,0:T(8,128)S(1)} %shard_map.69.group_ref, bf16[2304,128]{1,0:T(8,128)(2,1)S(1)} %bitcast.33), custom_call_target="tpu_custom_call" | custom-call | flops 4294967296 | bytes 3145728 | tf_op jit(solution)/shard_map/pallas_call | solution.py:24
  137.8 24.0 %all_to_all.23 = bf16[128,17,2,128]{3,2,1,0:T(2,128)(2,1)S(1)} all-to-all(bf16[128,17,2,128]{3,2,1,0:T(2,128)(2,1)S(1)} %bitcast.30), channel_id=1, replica_groups=mesh['gx'=8,'gy'=16] {'gx','gy'}, dimensions={0} | all-to-all | bytes 2228224 | tf_op jit(solution)/shard_map/all_to_all | solution.py:537
  161.7 6.9 %shard_map.74 = (f32[4096,128]{1,0:T(8,128)S(1)}, bf16[2048,128]{1,0:T(8,128)(2,1)S(1)}, bf16[2048,128]{1,0:T(8,128)(2,1)S(1)}, bf16[64,128,128]{2,1,0:T(8,128)(2,1)S(1)}) custom-call(s32[64]{0:T(128)S(1)} %get-tuple-element.52.first_ref, f32[8192,128]{1,0:T(8,128)S(1)} %get-tuple-element.22.cells_ref, bf16[4352,128]{1,0:T(8,128)(2,1)S(1)} %bitcast.25), custom_call_target="tpu_custom_call" | custom-call | flops 536870912 | bytes 10485760 | tf_op jit(solution)/shard_map/pallas_call | solution.py:24
  168.6 1.9 collective-permute-start.4
  170.5 3.6 %collective-permute-start.5 = (bf16[4,16,32,128]{3,2,1,0:T(8,128)(2,1)S(1)}, bf16[4,16,32,128]{3,2,1,0:T(8,128)(2,1)S(1)}, u32[]{:S(2)}, u32[]{:S(2)}) collective-permute-start(bf16[4,16,32,128]{3,2,1,0:T(8,128)(2,1)S(1)} %bitcast.34), channel_id=1, source_target_pairs={{16,0},{32,16},{48,32},{64,48},{80,64},{96,80},{112,96},{17,1},{33... | collective-permute-start | bytes 1572872 | tf_op jit(solution)/shard_map/ppermute | solution.py:40
  174.2 4.2 %shard_map.75 = f32[4096,128]{1,0:T(8,128)S(1)} custom-call(s32[64]{0:T(128)S(1)} %get-tuple-element.36.first_ref, f32[4096,128]{1,0:T(8,128)S(1)} %get-tuple-element.18.inner_ref.cells_ref, bf16[64,128,128]{2,1,0:T(8,128)(2,1)S(1)} %get-tuple-element.28.factor_ref, f32[4096,128]{1,0:T(8,128)S(1)} %get-tuple-element.29.start_ref), custom_call_target="tpu_custom_call" | custom-call | flops 536870912 | bytes 8388608 | tf_op jit(solution)/shard_map/pallas_call | solution.py:24
  181.2 4.6 %collective-permute-start.6 = (bf16[8,4,32,128]{3,2,1,0:T(8,128)(2,1)S(1)}, bf16[8,4,32,128]{3,2,1,0:T(8,128)(2,1)S(1)}, u32[]{:S(2)}, u32[]{:S(2)}) collective-permute-start(bf16[8,4,32,128]{3,2,1,0:T(8,128)(2,1)S(1)} %get-tuple-element.42), channel_id=1, source_target_pairs={{0,1},{1,2},{2,3},{3,4},{4,5},{5,6},{6,7},{7,8},{8,9},{9,10},{10,1... | collective-permute-start | bytes 786440 | tf_op jit(solution)/shard_map/ppermute | solution.py:39
  185.9 1.9 collective-permute-start.7
  189.4 2.6 %collective-permute-done.6 = bf16[8,4,32,128]{3,2,1,0:T(8,128)(2,1)S(1)} collective-permute-done((bf16[8,4,32,128]{3,2,1,0:T(8,128)(2,1)S(1)}, bf16[8,4,32,128]{3,2,1,0:T(8,128)(2,1)S(1)}, u32[]{:S(2)}, u32[]{:S(2)}) %collective-permute-start.6) | collective-permute-done | bytes 262176 | tf_op jit(solution)/shard_map/ppermute | solution.py:39
  192.0 6.2 %collective-permute-done.7 = bf16[8,4,32,128]{3,2,1,0:T(8,128)(2,1)S(1)} collective-permute-done((bf16[8,4,32,128]{3,2,1,0:T(8,128)(2,1)S(1)}, bf16[8,4,32,128]{3,2,1,0:T(8,128)(2,1)S(1)}, u32[]{:S(2)}, u32[]{:S(2)}) %collective-permute-start.7) | collective-permute-done | bytes 262176 | tf_op jit(solution)/shard_map/ppermute | solution.py:40
  (33 shorter events, 8.9 us)
Async XLA Ops:
  0.6 9.5 %copy-start.3 = (s32[3,64]{1,0:T(4,128)S(1)}, s32[3,64]{1,0:T(4,128)}, u32[]{:S(2)}) copy-start(s32[3,64]{1,0:T(4,128)} %param.7) | copy-start | bytes 2308
  0.6 9.6 %copy-start = (s32[2048,16]{0,1:T(8,128)S(1)}, s32[2048,16]{0,1:T(8,128)}, u32[]{:S(2)}) copy-start(s32[2048,16]{0,1:T(8,128)} %param.8) | copy-start | bytes 393220
  2.1 14.0 %collective-permute-start.1 = (bf16[8,4,32,128]{3,2,1,0:T(8,128)(2,1)S(1)}, bf16[8,4,32,128]{3,2,1,0:T(8,128)(2,1)S(1)}, u32[]{:S(2)}, u32[]{:S(2)}) collective-permute-start(bf16[8,4,32,128]{3,2,1,0:T(8,128)(2,1)S(1)} %get-tuple-element.46), channel_id=1, source_target_pairs={{1,0},{2,1},{3,2},{4,3},{5,4},{6,5},{7,6},{8,7},{9,8},{10,9},{11,1... | collective-permute-start | bytes 786440 | tf_op jit(solution)/shard_map/ppermute | solution.py:40
  4.4 11.7 %collective-permute-start = (bf16[8,4,32,128]{3,2,1,0:T(8,128)(2,1)S(1)}, bf16[8,4,32,128]{3,2,1,0:T(8,128)(2,1)S(1)}, u32[]{:S(2)}, u32[]{:S(2)}) collective-permute-start(bf16[8,4,32,128]{3,2,1,0:T(8,128)(2,1)S(1)} %get-tuple-element.47), channel_id=1, source_target_pairs={{0,1},{1,2},{2,3},{3,4},{4,5},{5,6},{6,7},{7,8},{8,9},{9,10},{10,1... | collective-permute-start | bytes 786440 | tf_op jit(solution)/shard_map/ppermute | solution.py:39
  16.2 10.5 %collective-permute-start.2 = (bf16[4,16,32,128]{3,2,1,0:T(8,128)(2,1)S(1)}, bf16[4,16,32,128]{3,2,1,0:T(8,128)(2,1)S(1)}, u32[]{:S(2)}, u32[]{:S(2)}) collective-permute-start(bf16[4,16,32,128]{3,2,1,0:T(8,128)(2,1)S(1)} %pad_maximum_fusion.1), channel_id=1, source_target_pairs={{0,16},{16,32},{32,48},{48,64},{64,80},{80,96},{96,112},{1,17},{17... | collective-permute-start | bytes 1572872 | tf_op jit(solution)/shard_map/ppermute | solution.py:39
  18.2 10.3 %collective-permute-start.3 = (bf16[4,16,32,128]{3,2,1,0:T(8,128)(2,1)S(1)}, bf16[4,16,32,128]{3,2,1,0:T(8,128)(2,1)S(1)}, u32[]{:S(2)}, u32[]{:S(2)}) collective-permute-start(bf16[4,16,32,128]{3,2,1,0:T(8,128)(2,1)S(1)} %pad_maximum_fusion.2), channel_id=1, source_target_pairs={{16,0},{32,16},{48,32},{64,48},{80,64},{96,80},{112,96},{17,1},{33... | collective-permute-start | bytes 1572872 | tf_op jit(solution)/shard_map/ppermute | solution.py:40
  168.6 10.5 %collective-permute-start.4 = (bf16[4,16,32,128]{3,2,1,0:T(8,128)(2,1)S(1)}, bf16[4,16,32,128]{3,2,1,0:T(8,128)(2,1)S(1)}, u32[]{:S(2)}, u32[]{:S(2)}) collective-permute-start(bf16[4,16,32,128]{3,2,1,0:T(8,128)(2,1)S(1)} %bitcast.35), channel_id=1, source_target_pairs={{0,16},{16,32},{32,48},{48,64},{64,80},{80,96},{96,112},{1,17},{17... | collective-permute-start | bytes 1572872 | tf_op jit(solution)/shard_map/ppermute | solution.py:39
  170.5 10.3 %collective-permute-start.5 = (bf16[4,16,32,128]{3,2,1,0:T(8,128)(2,1)S(1)}, bf16[4,16,32,128]{3,2,1,0:T(8,128)(2,1)S(1)}, u32[]{:S(2)}, u32[]{:S(2)}) collective-permute-start(bf16[4,16,32,128]{3,2,1,0:T(8,128)(2,1)S(1)} %bitcast.34), channel_id=1, source_target_pairs={{16,0},{32,16},{48,32},{64,48},{80,64},{96,80},{112,96},{17,1},{33... | collective-permute-start | bytes 1572872 | tf_op jit(solution)/shard_map/ppermute | solution.py:40
  181.2 10.8 %collective-permute-start.6 = (bf16[8,4,32,128]{3,2,1,0:T(8,128)(2,1)S(1)}, bf16[8,4,32,128]{3,2,1,0:T(8,128)(2,1)S(1)}, u32[]{:S(2)}, u32[]{:S(2)}) collective-permute-start(bf16[8,4,32,128]{3,2,1,0:T(8,128)(2,1)S(1)} %get-tuple-element.42), channel_id=1, source_target_pairs={{0,1},{1,2},{2,3},{3,4},{4,5},{5,6},{6,7},{7,8},{8,9},{9,10},{10,1... | collective-permute-start | bytes 786440 | tf_op jit(solution)/shard_map/ppermute | solution.py:39
  185.9 12.4 %collective-permute-start.7 = (bf16[8,4,32,128]{3,2,1,0:T(8,128)(2,1)S(1)}, bf16[8,4,32,128]{3,2,1,0:T(8,128)(2,1)S(1)}, u32[]{:S(2)}, u32[]{:S(2)}) collective-permute-start(bf16[8,4,32,128]{3,2,1,0:T(8,128)(2,1)S(1)} %get-tuple-element.43), channel_id=1, source_target_pairs={{1,0},{2,1},{3,2},{4,3},{5,4},{6,5},{7,6},{8,7},{9,8},{10,9},{11,1... | collective-permute-start | bytes 786440 | tf_op jit(solution)/shard_map/ppermute | solution.py:40
  189.4 9.0 %copy-start.1 = (bf16[8,8,32,128]{3,2,1,0:T(8,128)(2,1)S(1)}, bf16[8,8,32,128]{3,2,1,0:T(8,128)(2,1)}, u32[]{:S(2)}) copy-start(bf16[8,8,32,128]{3,2,1,0:T(8,128)(2,1)} %param.6) | copy-start | bytes 1572868
  189.4 9.0 %copy-start.2 = (bf16[8,8,32,128]{3,2,1,0:T(8,128)(2,1)S(1)}, bf16[8,8,32,128]{3,2,1,0:T(8,128)(2,1)}, u32[]{:S(2)}) copy-start(bf16[8,8,32,128]{3,2,1,0:T(8,128)(2,1)} %param.5) | copy-start | bytes 1572868
